TPU v7x, 32 devices: a whole 2x2x4 slice. The times are simulated.
32 devices in a mesh: dp: 16 (over z, y, core), rep: 2 (over x).
Axes of the slice: x: 2, y: 2, z: 4, core: 2. Of those that a mesh axis runs over, the one named last changes fastest.
Arguments:
- tokens: bfloat16 [512, 2048], P(('dp', 'rep')), may hold values from -6 to 6
- norm_gain: float32 [2048], replicated, may hold values from 0.1 to 1.9
- expert_weights: bfloat16 [8, 2048, 2304], P(None, ('dp', 'rep')), may hold values from -0.125 to 0.125
- slot_expert: int32 [16], replicated, may hold values from 0 to 7, as said below
- pair_slots: int32 [512, 8], P(('dp', 'rep')), may hold values from 0 to 15, all different within a row; in each aligned block of 16 rows (0 to 15, 16 to 31, ...) at most 16 rows name the same one
- combine_weights: float32 [512, 8], P(('dp', 'rep')), may hold values from 0.25 to 2
Outputs:
- layer_out: bfloat16 [512, 2048], P(('dp', 'rep'))
Inputs may be any that keep to these rules, and one draw needn't show every extreme that they name: `slot_expert`: every one of the 8 experts is held by at least one slot. `pair_slots`: each row names 8 different slots; among the 16 rows of one device no slot is named by more than 16 rows.
All inputs are finite; a program needn't handle non-finite values.
Results may differ from a plain program's by a relative error of at most 0.0071.
Values may be sent and summed in bfloat16 or wider, within the bound.
No kernel may reach another device: no remote copies, remote signals or barrier semaphores. Data moves between devices by JAX's collectives and lax.ppermute only.
A program may use at most 64 MiB of HBM per device.

v0:
```python
import jax
import jax.numpy as jnp
from jax import lax
from jax.sharding import PartitionSpec as P


def per_device(tokens, norm_gain, expert_weights, slot_expert, pair_slots, combine_weights):
    slot_count = lax.axis_size("dp")
    model_width = tokens.shape[1]
    packed_width = expert_weights.shape[2]
    hidden_units = packed_width // 3
    token_count = tokens.shape[0]
    choice_count = pair_slots.shape[1]
    pair_count = token_count * choice_count
    capacity = max(2, 2 * pair_count // slot_count)
    outgoing = jnp.take(expert_weights, slot_expert, axis=0)
    arrived = lax.all_to_all(outgoing, "dp", split_axis=0, concat_axis=0, tiled=True)
    assembled = lax.all_gather(arrived[:, None], "rep", axis=1, tiled=True)
    weight = assembled.reshape(model_width, packed_width)
    values = tokens.astype(jnp.float32)
    mean_square = jnp.mean(values * values, axis=1, keepdims=True)
    normed = (values * lax.rsqrt(mean_square + 1e-06) * norm_gain[None, :]).astype(jnp.bfloat16)
    targets = pair_slots.reshape(pair_count)
    onehot = (targets[:, None] == jnp.arange(slot_count, dtype=jnp.int32)[None, :]).astype(
        jnp.int32
    )
    before = jnp.cumsum(onehot, axis=0) - onehot
    position = jnp.sum(before * onehot, axis=1)
    target_row = targets * capacity + position
    selector = (
        jnp.arange(slot_count * capacity, dtype=jnp.int32)[:, None] == target_row[None, :]
    ).astype(jnp.bfloat16)
    pair_rows = jnp.repeat(normed, choice_count, axis=0)
    outbound = jnp.dot(selector, pair_rows, preferred_element_type=jnp.float32).astype(jnp.bfloat16)
    outbound = outbound.reshape(slot_count, capacity, model_width)
    rows = lax.all_to_all(outbound, "dp", split_axis=0, concat_axis=0, tiled=True).reshape(
        -1, model_width
    )
    gate_up = jnp.dot(rows, weight[:, : 2 * hidden_units], preferred_element_type=jnp.float32)
    hidden = (jax.nn.silu(gate_up[:, :hidden_units]) * gate_up[:, hidden_units:]).astype(
        jnp.bfloat16
    )
    result = lax.dot_general(
        hidden,
        weight[:, 2 * hidden_units :],
        (((1,), (1,)), ((), ())),
        preferred_element_type=jnp.float32,
    )
    result = result.astype(jnp.bfloat16).reshape(slot_count, -1, model_width)
    returned = lax.all_to_all(result, "dp", split_axis=0, concat_axis=0, tiled=True)
    expert_out = jnp.dot(
        selector.T,
        returned.reshape(slot_count * capacity, model_width),
        preferred_element_type=jnp.float32,
    )
    expert_out = expert_out.reshape(token_count, choice_count, model_width)
    mixed = jnp.sum(expert_out * combine_weights[:, :, None], axis=1)
    return mixed.astype(jnp.bfloat16)


def solution(mesh):
    placed = (
        P(("dp", "rep"), None),
        P(),
        P(None, ("dp", "rep"), None),
        P(),
        P(("dp", "rep"), None),
        P(("dp", "rep"), None),
    )
    return jax.shard_map(
        per_device, mesh=mesh, in_specs=placed, out_specs=P(("dp", "rep"), None), check_vma=False
    )
```

profile of v0, /device:TPU:0, one launch (start us, length us, event | category | flops | bytes accessed | tf_op | source)
XLA Modules:
  0.0 288.5 jit_solution(6897583741387915493)
XLA Ops:
  6.5 0.0 copy-start
  6.5 0.0 all-gather.3.cloned.1.call-start
  6.5 0.8 compare_select_fusion
  7.3 0.7 compare_and_fusion
  8.0 0.2 copy-done
  8.2 3.0 %gather_fusion = bf16[16,64,2304]{2,1,0:T(8,128)(2,1)} fusion(bf16[8,64,2304]{2,1,0:T(8,128)(2,1)S(1)} %copy-done, s32[1024]{0:T(1024)S(1)} %pad_clamp_fusion), kind=kCustom, calls=%fused_computation | custom fusion | bytes 9437248 | tf_op jit(solution)/shard_map/jit(_take)/gather | solution.py:16
  11.2 2.9 broadcast_select_fusion
  14.0 110.7 %all_to_all.15 = bf16[16,64,2304]{2,1,0:T(8,128)(2,1)} all-to-all(bf16[16,64,2304]{2,1,0:T(8,128)(2,1)S(1)} %broadcast_select_fusion), channel_id=1, replica_groups=mesh['dp'=16,'rep'=2] {'dp'}, dimensions={0} | all-to-all | bytes 9437184 | tf_op jit(solution)/shard_map/all_to_all | solution.py:17
  124.7 0.0 copy-start.3
  124.7 0.0 copy-start.1
  124.7 0.0 all-gather.3.cloned.1.call-update
  124.7 0.7 copy-done.3
  125.4 0.1 copy.9
  125.5 0.1 reshape.71
  125.5 0.1 fusion.20
  125.6 0.2 reduce_window_sum.11
  125.8 0.0 copy-done.1
  125.8 0.1 fusion.13
  125.9 0.2 select_reduce_fusion
  126.2 0.0 copy-done.2
  126.2 0.1 fusion.15
  126.2 0.4 convolution_convert_fusion
  126.7 29.9 %all_to_all.16 = bf16[16,16,2048]{2,1,0:T(8,128)(2,1)S(1)} all-to-all(bf16[16,16,2048]{2,1,0:T(8,128)(2,1)S(1)} %bitcast.15), channel_id=1, replica_groups=mesh['dp'=16,'rep'=2] {'dp'}, dimensions={0} | all-to-all | bytes 2097152 | tf_op jit(solution)/shard_map/all_to_all | solution.py:36
  156.5 87.0 %all-gather.3.cloned.1.call-done = bf16[16,128,2304]{2,1,0:T(8,128)(2,1)} async-done(((bf16[16,64,2304]{2,1,0:T(8,128)(2,1)}), bf16[16,128,2304]{2,1,0:T(8,128)(2,1)}) %all-gather.3.cloned.1.call-update) | async-done | bytes 9437200 | tf_op jit(solution)/shard_map/all_gather | solution.py:18
  243.5 4.6 %fusion = f32[256,1536]{1,0:T(8,128)S(1)} fusion(bf16[256,2048]{1,0:T(8,128)(2,1)S(1)} %bitcast.18, bf16[2048,2304]{1,0:T(8,128)(2,1)} %bitcast.19), kind=kOutput, calls=%fused_computation.1 | convolution fusion | flops 1610612736 | bytes 8912896 | tf_op jit(solution)/shard_map/dot_general | solution.py:39
  248.1 0.0 copy-start.4
  248.1 3.9 %fusion.4 = bf16[256,2048]{1,0:T(8,128)(2,1)} fusion(bf16[2048,2304]{1,0:T(8,128)(2,1)} %bitcast.20, f32[256,1536]{1,0:T(8,128)S(1)} %fusion), kind=kOutput, calls=%fused_computation.7 | convolution fusion | flops 807010304 | bytes 5767168 | tf_op jit(solution)/shard_map/dot_general | solution.py:43
  252.0 5.6 %all-to-all-start.2 = ((bf16[16,16,2048]{2,1,0:T(8,128)(2,1)}), bf16[16,16,2048]{2,1,0:T(8,128)(2,1)S(1)}, u32[]{:S(2)}, u32[]{:S(2)}) async-start(bf16[16,16,2048]{2,1,0:T(8,128)(2,1)} %bitcast.17), calls=%async_computation.2 | async-start | bytes 2097152 | tf_op jit(solution)/shard_map/all_to_all | solution.py:50
  257.6 0.0 copy-done.4
  257.7 0.1 copy.10
  257.7 22.8 %all-to-all-done.2 = bf16[16,16,2048]{2,1,0:T(8,128)(2,1)S(1)} async-done(((bf16[16,16,2048]{2,1,0:T(8,128)(2,1)}), bf16[16,16,2048]{2,1,0:T(8,128)(2,1)S(1)}, u32[]{:S(2)}, u32[]{:S(2)}) %all-to-all-start.2) | async-done | bytes 1048608 | tf_op jit(solution)/shard_map/all_to_all | solution.py:50
  280.5 1.1 fusion.7
  (4 shorter events, 0.0 us)
Async XLA Ops:
  6.5 1.7 copy-start
  6.5 237.0 %all-gather.3.cloned.1.call-start = ((), (), s32[]{:S(2)}) async-start(), calls=%async_computation.3 | async-start | bytes 14155776 | tf_op jit(solution)/shard_map/all_gather | solution.py:18
  124.7 0.7 copy-start.3
  124.7 1.1 copy-start.1
  124.7 1.5 copy-start.2
  248.1 9.6 %copy-start.4 = (f32[16,8]{0,1:T(8,128)S(1)}, f32[16,8]{0,1:T(8,128)}, u32[]{:S(2)}) copy-start(f32[16,8]{0,1:T(8,128)} %param.11) | copy-start | bytes 1540
  252.0 28.5 %all-to-all-start.2 = ((bf16[16,16,2048]{2,1,0:T(8,128)(2,1)}), bf16[16,16,2048]{2,1,0:T(8,128)(2,1)S(1)}, u32[]{:S(2)}, u32[]{:S(2)}) async-start(bf16[16,16,2048]{2,1,0:T(8,128)(2,1)} %bitcast.17), calls=%async_computation.2 | async-start | bytes 2097152 | tf_op jit(solution)/shard_map/all_to_all | solution.py:50
Sparse Core Ops, SparseCore 0:
  124.8 118.6 all-gather.2
where the time goes:
time: 290 us; the launch traced here: 289 us
  blocking collectives  141 us (49%)
  waiting for transfers between devices  110 us (38%)
  between operations  13.5 us (5%)
  matrix products  10.1 us (3%)
  starting transfers between devices  5.62 us (2%)
  other arithmetic  4.98 us (2%)
  local copies, waits for them, and re-layouts  4.07 us (1%)
    all_to_all x1, blocking collectives, per_device(): lax.all_to_all(outgoing, 'dp', split_axis=0, concat_axis=0, tiled=True)  111 us
    all_gather x1, waiting for transfers between devices, per_device(): assembled = lax.all_gather(arrived[:, None], 'rep', axis=1, tiled=True)  87 us
    all_to_all x1, blocking collectives, per_device(): lax.all_to_all(outbound, 'dp', split_axis=0, concat_axis=0, tiled=True)  29.9 us
    all_to_all x1, waiting for transfers between devices, per_device(): lax.all_to_all(result, 'dp', split_axis=0, concat_axis=0, tiled=True)  22.8 us
  transfers between devices with their start and end apart: 2, of which 2 were waited for; matrix products, arithmetic and copies ran while one was open for 0% of the time, Pallas kernels for 0%

commit v1 on v0

--- a/solution.py
+++ b/solution.py
@@ -1,7 +1,77 @@
+import functools
 import jax
 import jax.numpy as jnp
 from jax import lax
-from jax.sharding import PartitionSpec as P
+from jax.sharding import Mesh, PartitionSpec as P
+
+SWAP = [(0, 1), (1, 0)]
+
+
+def normalize(tokens, norm_gain):
+    values = tokens.astype(jnp.float32)
+    mean_square = jnp.mean(values * values, axis=1, keepdims=True)
+    return (values * lax.rsqrt(mean_square + 1e-06) * norm_gain[None, :]).astype(jnp.bfloat16)
+
+
+def dense_layer(tokens, norm_gain, expert_weights, slot_expert, pair_slots, combine_weights):
+    experts, own_rows, packed = expert_weights.shape
+    token_count, width = tokens.shape
+    hidden_units = packed // 3
+    part = hidden_units // 2
+    half_axes = ("z", "y", "c", "x")
+    chip_axes = ("z", "y", "x")
+    everywhere = ("h",) + half_axes
+    nz, ny, nx = (lax.axis_size(a) for a in chip_axes)
+    chips = nz * ny * nx
+    peers = 2 * chips
+    blocks = expert_weights.reshape(nz, ny, nx, own_rows, 3, 2, part)
+    blocks = blocks.transpose(0, 1, 5, 2, 3, 4, 6)
+    gate_up = blocks[:, :, :, :, :, :2].reshape(peers, own_rows, 2 * part)
+    down = blocks[:, :, :, :, :, 2].reshape(1, peers, own_rows, part)
+    down = jnp.broadcast_to(down, (2, peers, own_rows, part)).reshape(2 * peers, own_rows, part)
+    gate_up = lax.all_to_all(gate_up, half_axes, 0, 0, tiled=True).reshape(peers * own_rows, 2 * part)
+    normed = normalize(tokens, norm_gain)
+    h = lax.axis_index("h")
+    halves = normed.reshape(token_count, 2, width // 2)
+    mine = lax.dynamic_index_in_dim(halves, h, 1, keepdims=False)
+    other = lax.dynamic_index_in_dim(halves, 1 - h, 1, keepdims=False)
+    near = jnp.stack([mine, lax.ppermute(other, "h", SWAP)])
+    spread = jnp.broadcast_to(near[None], (chips,) + near.shape)
+    spread = lax.all_to_all(spread, chip_axes, 0, 0, tiled=True)
+    spread = spread.transpose(1, 0, 2, 3).reshape(2, chips * token_count, width // 2)
+    crossed = lax.ppermute(spread, "c", SWAP)
+    rows = jnp.concatenate([spread[:, None], crossed[:, None]], axis=1)
+    rows = rows.reshape(4 * chips * token_count, width // 2)
+    down = lax.all_to_all(down, everywhere, 0, 0, tiled=True).reshape(width, part)
+    partial = jnp.dot(rows, gate_up, preferred_element_type=jnp.float32)
+    mid = partial.shape[0] // 2
+    arrived = lax.ppermute(partial[mid:].astype(jnp.bfloat16), "h", SWAP)
+    pre = partial[:mid] + arrived.astype(jnp.float32)
+    hidden = (jax.nn.silu(pre[:, :part]) * pre[:, part:]).astype(jnp.bfloat16)
+    result = lax.dot_general(hidden, down, (((1,), (1,)), ((), ())), preferred_element_type=jnp.float32)
+    quarter = mid // 2
+    arrived = lax.ppermute(result[quarter:].astype(jnp.bfloat16), "c", SWAP)
+    result = (result[:quarter] + arrived.astype(jnp.float32)).astype(jnp.bfloat16)
+    result = result.reshape(chips, token_count, width)
+    returned = lax.all_to_all(result, chip_axes, 0, 0, tiled=True).astype(jnp.float32)
+    chosen = jnp.sum(
+        jnp.where(
+            pair_slots[:, :, None] == jnp.arange(slot_expert.shape[0], dtype=jnp.int32)[None, None, :],
+            slot_expert[None, None, :],
+            0,
+        ),
+        axis=2,
+    )
+    coefficient = jnp.sum(
+        jnp.where(
+            chosen[:, :, None] == jnp.arange(experts, dtype=jnp.int32)[None, None, :],
+            combine_weights[:, :, None],
+            0.0,
+        ),
+        axis=1,
+    )
+    mixed = jnp.sum(returned * coefficient.T[:, :, None], axis=0)
+    return mixed.astype(jnp.bfloat16)
 
 
 def per_device(tokens, norm_gain, expert_weights, slot_expert, pair_slots, combine_weights):
@@ -59,14 +129,23 @@
 
 
 def solution(mesh):
-    placed = (
-        P(("dp", "rep"), None),
-        P(),
-        P(None, ("dp", "rep"), None),
-        P(),
-        P(("dp", "rep"), None),
-        P(("dp", "rep"), None),
-    )
-    return jax.shard_map(
-        per_device, mesh=mesh, in_specs=placed, out_specs=P(("dp", "rep"), None), check_vma=False
-    )
+    slots, engines = mesh.shape["dp"], mesh.shape["rep"]
+
+    def layer(tokens, norm_gain, expert_weights, slot_expert, pair_slots, combine_weights):
+        experts, _, packed = expert_weights.shape
+        dense = slots % 8 == 0 and slots * engines == 4 * experts and packed % 6 == 0
+        if dense:
+            devices = mesh.devices.reshape(2, slots // 8, 2, 2, engines)
+            inner, split = Mesh(devices, ("h", "z", "y", "c", "x")), ("h", "z", "y", "c", "x")
+        else:
+            inner, split = mesh, ("dp", "rep")
+        placed = (P(split, None), P(), P(None, split, None), P(), P(split, None), P(split, None))
+        return jax.shard_map(
+            dense_layer if dense else per_device,
+            mesh=inner,
+            in_specs=placed,
+            out_specs=P(split, None),
+            check_vma=False,
+        )(tokens, norm_gain, expert_weights, slot_expert, pair_slots, combine_weights)
+
+    return layer

time: 290 us -> 133 us (0.46)
  blocking collectives: 141 us -> 0 us
  waiting for transfers between devices: 110 us -> 81.8 us
  starting transfers between devices: 5.62 us -> 26.5 us
  between operations: 13.5 us -> 0.2 us
  local copies, waits for them, and re-layouts: 4.07 us -> 16.6 us
  matrix products: 10.1 us -> 3.13 us
    all_to_all x2 -> x0, blocking collectives: 141 us -> none  [the longest x1 111 us: per_device(): lax.all_to_all(outgoing, 'dp', split_axis=0, concat_axis=0, tiled=True)]
    all_gather x1 -> x0, waiting for transfers between devices: 87 us -> none  [per_device(): assembled = lax.all_gather(arrived[:, None], 'rep', axis=1, tiled=True)]
    ppermute x0 -> x4, waiting for transfers between devices: none -> 52.7 us  [the longest x1 46.9 us: dense_layer(): arrived = lax.ppermute(partial[mid:].astype(jnp.bfloat16), 'h', SWAP)]
    all_to_all x1 -> x4, starting transfers between devices: 5.62 us -> 19.3 us  [the longest x1 5.62 us: dense_layer(): lax.all_to_all(down, everywhere, 0, 0, tiled=True).reshape(width, part)]
    reshape x1 -> x3, local copies, waits for them, and re-layouts: 0.09 us -> 9.54 us  [the longest x1 4.9 us: dense_layer(): gate_up = blocks[:, :, :, :, :, :2].reshape(peers, own_rows, 2 * part)]
    ppermute x0 -> x4, starting transfers between devices: none -> 7.26 us  [the longest x1 4.13 us: dense_layer(): near = jnp.stack([mine, lax.ppermute(other, 'h', SWAP)])]
    dot_general x4 -> x2, matrix products: 10.1 us -> 3.13 us  [the longest x1 2.38 us: dense_layer(): partial = jnp.dot(rows, gate_up, preferred_element_type=jnp.float32)]
    all_to_all x1 -> x4, waiting for transfers between devices: 22.8 us -> 29.1 us  [the longest x1 20.3 us: dense_layer(): lax.all_to_all(gate_up, half_axes, 0, 0, tiled=True)]
  transfers between devices with their start and end apart: 2 -> 8, of which waited for: 2 -> 6; matrix products, arithmetic and copies ran while one was open for 0% -> 13% of each run, Pallas kernels for 0% -> 0%
where the time goes in v1:
time: 133 us; the launch traced here: 132 us
  waiting for transfers between devices  81.8 us (62%)
  starting transfers between devices  26.5 us (20%)
  local copies, waits for them, and re-layouts  16.6 us (12%)
  other arithmetic  4.23 us (3%)
  matrix products  3.13 us (2%)
    ppermute x1, waiting for transfers between devices, dense_layer(): arrived = lax.ppermute(partial[mid:].astype(jnp.bfloat16), 'h', SWAP)  46.9 us
    all_to_all x1, waiting for transfers between devices, dense_layer(): lax.all_to_all(gate_up, half_axes, 0, 0, tiled=True)  20.3 us
    all_to_all x1, waiting for transfers between devices, dense_layer(): lax.all_to_all(result, chip_axes, 0, 0, tiled=True).astype(jnp.float32)  8.82 us
    all_to_all x1, starting transfers between devices, dense_layer(): lax.all_to_all(down, everywhere, 0, 0, tiled=True).reshape(width, part)  5.62 us
    all_to_all x1, starting transfers between devices, dense_layer(): lax.all_to_all(gate_up, half_axes, 0, 0, tiled=True)  5.25 us
    reshape x1, local copies, waits for them, and re-layouts, dense_layer(): gate_up = blocks[:, :, :, :, :, :2].reshape(peers, own_rows, 2 * part)  4.9 us
    all_to_all x1, starting transfers between devices, dense_layer(): spread = lax.all_to_all(spread, chip_axes, 0, 0, tiled=True)  4.71 us
    reshape x1, local copies, waits for them, and re-layouts, dense_layer(): blocks = expert_weights.reshape(nz, ny, nx, own_rows, 3, 2, part)  4.6 us
  transfers between devices with their start and end apart: 8, of which 6 were waited for; matrix products, arithmetic and copies ran while one was open for 13% of the time, Pallas kernels for 0%

profile of v1, /device:TPU:0, one launch (start us, length us, event | category | flops | bytes accessed | tf_op | source)
XLA Modules:
  0.0 132.4 jit_solution(6840596682809802799)
XLA Ops:
  0.0 1.0 fusion.5
  1.0 0.9 fusion.7
  2.0 0.1 constant_dynamic-slice_fusion.1
  2.1 4.1 %collective-permute-start = (bf16[16,1024]{1,0:T(8,128)(2,1)S(1)}, bf16[16,1024]{1,0:T(8,128)(2,1)S(1)}, u32[]{:S(2)}, u32[]{:S(2)}) collective-permute-start(bf16[16,1024]{1,0:T(8,128)(2,1)S(1)} %bitcast.33), channel_id=1, source_target_pairs={{0,16},{16,0},{1,17},{17,1},{2,18},{18,2},{3,19},{19,3},{4,20},{20... | collective-permute-start | bytes 98312 | tf_op jit(solution)/shard_map/ppermute | solution.py:38
  6.3 2.2 %collective-permute-done = bf16[16,1024]{1,0:T(8,128)(2,1)S(1)} collective-permute-done((bf16[16,1024]{1,0:T(8,128)(2,1)S(1)}, bf16[16,1024]{1,0:T(8,128)(2,1)S(1)}, u32[]{:S(2)}, u32[]{:S(2)}) %collective-permute-start) | collective-permute-done | bytes 32800 | tf_op jit(solution)/shard_map/ppermute | solution.py:38
  8.5 0.8 broadcast_in_dim.32
  9.4 4.7 %all-to-all-start = ((bf16[8,2,16,1024]{3,2,1,0:T(8,128)(2,1)}), bf16[8,2,16,1024]{3,2,1,0:T(8,128)(2,1)S(1)}, u32[]{:S(2)}, u32[]{:S(2)}) async-start(bf16[8,2,16,1024]{3,2,1,0:T(8,128)(2,1)} %broadcast_in_dim.32), calls=%async_computation | async-start | bytes 1048576 | tf_op jit(solution)/shard_map/all_to_all | solution.py:40
  14.1 4.6 %reshape.47 = bf16[2,2,2,64,3,2,384]{6,5,4,3,2,1,0:T(2,128)(2,1)S(1)} reshape(bf16[8,64,2304]{2,1,0:T(8,128)(2,1)} %param.8) | data formatting | bytes 4718592 | tf_op jit(solution)/shard_map/reshape | solution.py:27
  18.7 1.1 slice.34
  19.8 2.5 %copy.25 = bf16[2,2,2,2,64,2,384]{6,5,4,3,2,1,0:T(2,128)(2,1)} copy(bf16[2,2,2,2,64,2,384]{6,2,5,4,3,1,0:T(2,128)(2,1)S(1)} %slice.34) | data formatting | bytes 3145728 | tf_op jit(solution)/shard_map/slice | solution.py:29
  22.2 4.9 %reshape.48 = bf16[16,64,768]{2,1,0:T(8,128)(2,1)} reshape(bf16[2,2,2,2,64,2,384]{6,5,4,3,2,1,0:T(2,128)(2,1)} %copy.25) | data formatting | bytes 3145728 | tf_op jit(solution)/shard_map/reshape | solution.py:29
  27.1 5.2 %all-to-all-start.1 = ((bf16[16,64,768]{2,1,0:T(8,128)(2,1)}), bf16[16,64,768]{2,1,0:T(8,128)(2,1)}, u32[]{:S(2)}, u32[]{:S(2)}) async-start(bf16[16,64,768]{2,1,0:T(8,128)(2,1)} %reshape.48), calls=%async_computation.1 | async-start | bytes 3145728 | tf_op jit(solution)/shard_map/all_to_all | solution.py:32
  32.4 0.5 slice.39
  33.0 0.1 copy.26
  33.1 20.3 %all-to-all-done.1 = bf16[16,64,768]{2,1,0:T(8,128)(2,1)} async-done(((bf16[16,64,768]{2,1,0:T(8,128)(2,1)}), bf16[16,64,768]{2,1,0:T(8,128)(2,1)}, u32[]{:S(2)}, u32[]{:S(2)}) %all-to-all-start.1) | async-done | bytes 1572896 | tf_op jit(solution)/shard_map/all_to_all | solution.py:32
  53.4 1.4 %broadcast_in_dim.52 = bf16[2,16,64,384]{3,2,1,0:T(8,128)(2,1)} broadcast(bf16[16,64,384]{2,1,0:T(8,128)(2,1)S(1)} %bitcast.27), dimensions={1,2,3} | broadcast | bytes 2359296 | tf_op jit(solution)/shard_map/broadcast_in_dim | solution.py:31
  54.8 5.6 %all-to-all-start.2 = ((bf16[32,64,384]{2,1,0:T(8,128)(2,1)}), bf16[32,64,384]{2,1,0:T(8,128)(2,1)S(1)}, u32[]{:S(2)}, u32[]{:S(2)}) async-start(bf16[32,64,384]{2,1,0:T(8,128)(2,1)} %bitcast.9), calls=%async_computation.2 | async-start | bytes 3145728 | tf_op jit(solution)/shard_map/all_to_all | solution.py:45
  60.4 0.3 collective-permute-start.1
  60.8 1.7 %collective-permute-done.1 = bf16[2,128,1024]{2,1,0:T(8,128)(2,1)S(1)} collective-permute-done((bf16[2,128,1024]{2,1,0:T(8,128)(2,1)S(1)}, bf16[2,128,1024]{2,1,0:T(8,128)(2,1)S(1)}, u32[]{:S(2)}, u32[]{:S(2)}) %collective-permute-start.1) | collective-permute-done | bytes 524320 | tf_op jit(solution)/shard_map/ppermute | solution.py:42
  62.4 0.1 pad_maximum_fusion
  62.6 2.4 %fusion.9 = f32[512,768]{1,0:T(8,128)S(1)} fusion(bf16[512,1024]{1,0:T(8,128)(2,1)S(1)} %bitcast.30, bf16[1024,768]{1,0:T(8,128)(2,1)} %bitcast.7), kind=kOutput, calls=%fused_computation.27 | convolution fusion | flops 805306368 | bytes 4194304 | tf_op jit(solution)/shard_map/dot_general | solution.py:46
  65.0 2.7 %collective-permute-start.2 = (bf16[256,768]{1,0:T(8,128)(2,1)S(1)}, bf16[256,768]{1,0:T(8,128)(2,1)S(1)}, u32[]{:S(2)}, u32[]{:S(2)}) collective-permute-start(bf16[256,768]{1,0:T(8,128)(2,1)S(1)} %slice.55), channel_id=1, source_target_pairs={{0,16},{16,0},{1,17},{17,1},{2,18},{18,2},{3,19},{19,3},{4,20},{20... | collective-permute-start | bytes 1179656 | tf_op jit(solution)/shard_map/ppermute | solution.py:48
  67.8 46.9 %collective-permute-done.2 = bf16[256,768]{1,0:T(8,128)(2,1)S(1)} collective-permute-done((bf16[256,768]{1,0:T(8,128)(2,1)S(1)}, bf16[256,768]{1,0:T(8,128)(2,1)S(1)}, u32[]{:S(2)}, u32[]{:S(2)}) %collective-permute-start.2) | collective-permute-done | bytes 393248 | tf_op jit(solution)/shard_map/ppermute | solution.py:48
  114.8 0.7 fusion.2
  115.6 0.1 collective-permute-start.3
  115.7 1.9 %collective-permute-done.3 = bf16[128,2048]{1,0:T(8,128)(2,1)S(1)} collective-permute-done((bf16[128,2048]{1,0:T(8,128)(2,1)S(1)}, bf16[128,2048]{1,0:T(8,128)(2,1)S(1)}, u32[]{:S(2)}, u32[]{:S(2)}) %collective-permute-start.3) | collective-permute-done | bytes 524320 | tf_op jit(solution)/shard_map/ppermute | solution.py:53
  117.6 0.9 fusion
  118.5 3.7 %all-to-all-start.3 = ((bf16[8,16,2048]{2,1,0:T(8,128)(2,1)}), bf16[8,16,2048]{2,1,0:T(8,128)(2,1)S(1)}, u32[]{:S(2)}, u32[]{:S(2)}) async-start(bf16[8,16,2048]{2,1,0:T(8,128)(2,1)} %bitcast.11), calls=%async_computation.3 | async-start | bytes 1048576 | tf_op jit(solution)/shard_map/all_to_all | solution.py:56
  122.2 0.1 copy.27
  122.3 0.4 select_reduce_fusion
  122.8 8.8 %all-to-all-done.3 = bf16[8,16,2048]{2,1,0:T(8,128)(2,1)S(1)} async-done(((bf16[8,16,2048]{2,1,0:T(8,128)(2,1)}), bf16[8,16,2048]{2,1,0:T(8,128)(2,1)S(1)}, u32[]{:S(2)}, u32[]{:S(2)}) %all-to-all-start.3) | async-done | bytes 524320 | tf_op jit(solution)/shard_map/all_to_all | solution.py:56
  131.6 0.8 multiply_reduce_fusion
  (20 shorter events, 0.5 us)
Async XLA Ops:
  2.1 6.4 %collective-permute-start = (bf16[16,1024]{1,0:T(8,128)(2,1)S(1)}, bf16[16,1024]{1,0:T(8,128)(2,1)S(1)}, u32[]{:S(2)}, u32[]{:S(2)}) collective-permute-start(bf16[16,1024]{1,0:T(8,128)(2,1)S(1)} %bitcast.33), channel_id=1, source_target_pairs={{0,16},{16,0},{1,17},{17,1},{2,18},{18,2},{3,19},{19,3},{4,20},{20... | collective-permute-start | bytes 98312 | tf_op jit(solution)/shard_map/ppermute | solution.py:38
  9.4 17.8 %all-to-all-start = ((bf16[8,2,16,1024]{3,2,1,0:T(8,128)(2,1)}), bf16[8,2,16,1024]{3,2,1,0:T(8,128)(2,1)S(1)}, u32[]{:S(2)}, u32[]{:S(2)}) async-start(bf16[8,2,16,1024]{3,2,1,0:T(8,128)(2,1)} %broadcast_in_dim.32), calls=%async_computation | async-start | bytes 1048576 | tf_op jit(solution)/shard_map/all_to_all | solution.py:40
  27.1 26.2 %all-to-all-start.1 = ((bf16[16,64,768]{2,1,0:T(8,128)(2,1)}), bf16[16,64,768]{2,1,0:T(8,128)(2,1)}, u32[]{:S(2)}, u32[]{:S(2)}) async-start(bf16[16,64,768]{2,1,0:T(8,128)(2,1)} %reshape.48), calls=%async_computation.1 | async-start | bytes 3145728 | tf_op jit(solution)/shard_map/all_to_all | solution.py:32
  54.8 60.0 %all-to-all-start.2 = ((bf16[32,64,384]{2,1,0:T(8,128)(2,1)}), bf16[32,64,384]{2,1,0:T(8,128)(2,1)S(1)}, u32[]{:S(2)}, u32[]{:S(2)}) async-start(bf16[32,64,384]{2,1,0:T(8,128)(2,1)} %bitcast.9), calls=%async_computation.2 | async-start | bytes 3145728 | tf_op jit(solution)/shard_map/all_to_all | solution.py:45
  60.4 2.0 %collective-permute-start.1 = (bf16[2,128,1024]{2,1,0:T(8,128)(2,1)S(1)}, bf16[2,128,1024]{2,1,0:T(8,128)(2,1)S(1)}, u32[]{:S(2)}, u32[]{:S(2)}) collective-permute-start(bf16[2,128,1024]{2,1,0:T(8,128)(2,1)S(1)} %bitcast.28), channel_id=1, source_target_pairs={{0,2},{2,0},{1,3},{3,1},{4,6},{6,4},{5,7},{7,5},{8,10},{10,8},{9,1... | collective-permute-start | bytes 1572872 | tf_op jit(solution)/shard_map/ppermute | solution.py:42
  65.0 49.6 %collective-permute-start.2 = (bf16[256,768]{1,0:T(8,128)(2,1)S(1)}, bf16[256,768]{1,0:T(8,128)(2,1)S(1)}, u32[]{:S(2)}, u32[]{:S(2)}) collective-permute-start(bf16[256,768]{1,0:T(8,128)(2,1)S(1)} %slice.55), channel_id=1, source_target_pairs={{0,16},{16,0},{1,17},{17,1},{2,18},{18,2},{3,19},{19,3},{4,20},{20... | collective-permute-start | bytes 1179656 | tf_op jit(solution)/shard_map/ppermute | solution.py:48
  115.6 6.6 %copy-start = (s32[16,8]{0,1:T(8,128)S(1)}, s32[16,8]{0,1:T(8,128)}, u32[]{:S(2)}) copy-start(s32[16,8]{0,1:T(8,128)} %param.10) | copy-start | bytes 1540
  115.6 6.7 %copy-start.2 = (s32[16]{0:T(128)S(1)}, s32[16]{0:T(128)}, u32[]{:S(2)}) copy-start(s32[16]{0:T(128)} %param.9) | copy-start | bytes 196
  115.6 7.2 %copy-start.1 = (f32[16,8]{0,1:T(8,128)S(1)}, f32[16,8]{0,1:T(8,128)}, u32[]{:S(2)}) copy-start(f32[16,8]{0,1:T(8,128)} %param.11) | copy-start | bytes 1540
  115.6 2.0 %collective-permute-start.3 = (bf16[128,2048]{1,0:T(8,128)(2,1)S(1)}, bf16[128,2048]{1,0:T(8,128)(2,1)S(1)}, u32[]{:S(2)}, u32[]{:S(2)}) collective-permute-start(bf16[128,2048]{1,0:T(8,128)(2,1)S(1)} %slice.54), channel_id=1, source_target_pairs={{0,2},{2,0},{1,3},{3,1},{4,6},{6,4},{5,7},{7,5},{8,10},{10,8},{9,1... | collective-permute-start | bytes 1572872 | tf_op jit(solution)/shard_map/ppermute | solution.py:53
  118.5 13.1 %all-to-all-start.3 = ((bf16[8,16,2048]{2,1,0:T(8,128)(2,1)}), bf16[8,16,2048]{2,1,0:T(8,128)(2,1)S(1)}, u32[]{:S(2)}, u32[]{:S(2)}) async-start(bf16[8,16,2048]{2,1,0:T(8,128)(2,1)} %bitcast.11), calls=%async_computation.3 | async-start | bytes 1048576 | tf_op jit(solution)/shard_map/all_to_all | solution.py:56

commit v2 on v0

--- a/solution.py
+++ b/solution.py
@@ -1,7 +1,103 @@
 import jax
 import jax.numpy as jnp
 from jax import lax
-from jax.sharding import PartitionSpec as P
+from jax.sharding import Mesh, PartitionSpec as P
+
+SWAP = [(0, 1), (1, 0)]
+CROSS = [(0, 3), (1, 2), (2, 1), (3, 0)]
+
+
+def normalize(tokens, norm_gain):
+    values = tokens.astype(jnp.float32)
+    mean_square = jnp.mean(values * values, axis=1, keepdims=True)
+    return (values * lax.rsqrt(mean_square + 1e-06) * norm_gain[None, :]).astype(jnp.bfloat16)
+
+
+def in_order(bit, near, far, axis):
+    return jnp.where(
+        bit == 0, jnp.concatenate([near, far], axis=axis), jnp.concatenate([far, near], axis=axis)
+    )
+
+
+def slot_coefficients(slot_expert, pair_slots, combine_weights, experts):
+    slots = jnp.arange(slot_expert.shape[0], dtype=jnp.int32)
+    held = slot_expert[None, None, :]
+    chosen = jnp.sum(jnp.where(pair_slots[:, :, None] == slots[None, None, :], held, 0), axis=2)
+    numbers = jnp.arange(experts, dtype=jnp.int32)
+    weights = combine_weights[:, :, None]
+    return jnp.sum(jnp.where(chosen[:, :, None] == numbers[None, None, :], weights, 0.0), axis=1)
+
+
+def dense_layer(tokens, norm_gain, expert_weights, slot_expert, pair_slots, combine_weights):
+    experts, own_rows, packed = expert_weights.shape
+    token_count, width = tokens.shape
+    hidden_units = packed // 3
+    chip_axes = ("z", "y", "x")
+    chips = experts
+    engines = lax.axis_size("x")
+    h, c = lax.axis_index("h"), lax.axis_index("c")
+    group = engines * own_rows
+    groups = width // (4 * group)
+
+    far_down = lax.ppermute(expert_weights[:, :, 2 * hidden_units :], "h", SWAP)
+    weights = lax.all_to_all(expert_weights, chip_axes, 0, 0, tiled=True)
+    far_down = lax.all_to_all(far_down, chip_axes, 0, 0, tiled=True)
+    gate_up = weights[:, :, : 2 * hidden_units].reshape(chips * own_rows, 2 * hidden_units)
+    near_down = weights[:, :, 2 * hidden_units :].reshape(chips * own_rows, hidden_units)
+    far_down = far_down.reshape(chips * own_rows, hidden_units)
+
+    normed = normalize(tokens, norm_gain)
+    pieces = [
+        jnp.concatenate(
+            [normed[:, ((i * groups + g) * 2 + j) * group :][:, :group] for g in range(groups)], axis=1
+        )
+        for i in range(2)
+        for j in range(2)
+    ]
+
+    def piece(i, j):
+        at = 2 * i + j
+        return jnp.where(
+            at < 2, jnp.where(at == 0, pieces[0], pieces[1]), jnp.where(at == 2, pieces[2], pieces[3])
+        )
+
+    rows = jnp.stack(
+        [
+            piece(h, c),
+            lax.ppermute(piece(h, 1 - c), "c", SWAP),
+            lax.ppermute(piece(1 - h, c), "h", SWAP),
+            lax.ppermute(piece(1 - h, 1 - c), ("h", "c"), CROSS),
+        ]
+    )
+    for axis in ("x", "y", "z"):
+        rows = in_order(lax.axis_index(axis), rows, lax.ppermute(rows, axis, SWAP), 1)
+    count = chips * token_count
+
+    def products(first):
+        block = rows[first : first + 2].reshape(2 * count, -1)
+        sums = jnp.dot(block, gate_up, preferred_element_type=jnp.float32)
+        arrived = lax.ppermute(sums[count:].astype(jnp.bfloat16), "c", SWAP)
+        return sums[:count] + arrived.astype(jnp.float32)
+
+    far = lax.ppermute(products(2).astype(jnp.bfloat16), "h", SWAP)
+    pre = products(0) + far.astype(jnp.float32)
+    hidden = (jax.nn.silu(pre[:, :hidden_units]) * pre[:, hidden_units:]).astype(jnp.bfloat16)
+    hidden = in_order(c, hidden, lax.ppermute(hidden, "c", SWAP), 0)
+
+    def result(down):
+        return lax.dot_general(
+            hidden, down, (((1,), (1,)), ((), ())), preferred_element_type=jnp.float32
+        ).astype(jnp.bfloat16)
+
+    outbound = jnp.concatenate([result(near_down), result(far_down)], axis=1)
+    outbound = outbound.reshape(2 * chips, token_count, width // 2)
+    returned = lax.all_to_all(outbound, ("c",) + chip_axes, 0, 0, tiled=True)
+    returned = returned.reshape(2, chips, token_count, width // 2).astype(jnp.float32)
+    coefficient = slot_coefficients(slot_expert, pair_slots, combine_weights, experts)
+    mixed = jnp.sum(returned * coefficient.T[None, :, :, None], axis=1).astype(jnp.bfloat16)
+    mixed = in_order(h, mixed[:, :, : width // 4], mixed[:, :, width // 4 :], 2)
+    spans = [mixed[j, :, g * group : (g + 1) * group] for g in range(2 * groups) for j in range(2)]
+    return jnp.concatenate(spans, axis=1)
 
 
 def per_device(tokens, norm_gain, expert_weights, slot_expert, pair_slots, combine_weights):
@@ -59,14 +155,23 @@
 
 
 def solution(mesh):
-    placed = (
-        P(("dp", "rep"), None),
-        P(),
-        P(None, ("dp", "rep"), None),
-        P(),
-        P(("dp", "rep"), None),
-        P(("dp", "rep"), None),
-    )
-    return jax.shard_map(
-        per_device, mesh=mesh, in_specs=placed, out_specs=P(("dp", "rep"), None), check_vma=False
-    )
+    slots, engines = mesh.shape["dp"], mesh.shape["rep"]
+
+    def layer(tokens, norm_gain, expert_weights, slot_expert, pair_slots, combine_weights):
+        experts = expert_weights.shape[0]
+        dense = engines == 2 and slots == 2 * experts and slots % 8 == 0 and slots <= 16
+        if dense:
+            devices = mesh.devices.reshape(2, slots // 8, 2, 2, engines)
+            inner, split = Mesh(devices, ("h", "z", "y", "c", "x")), ("h", "z", "y", "c", "x")
+        else:
+            inner, split = mesh, ("dp", "rep")
+        placed = (P(split, None), P(), P(None, split, None), P(), P(split, None), P(split, None))
+        return jax.shard_map(
+            dense_layer if dense else per_device,
+            mesh=inner,
+            in_specs=placed,
+            out_specs=P(split, None),
+            check_vma=False,
+        )(tokens, norm_gain, expert_weights, slot_expert, pair_slots, combine_weights)
+
+    return layer

time: 290 us -> 134 us (0.46)
  blocking collectives: 141 us -> 0 us
  starting transfers between devices: 5.62 us -> 29.4 us
  waiting for transfers between devices: 110 us -> 89.4 us
  between operations: 13.5 us -> 0.36 us
  matrix products: 10.1 us -> 3.09 us
  local copies, waits for them, and re-layouts: 4.07 us -> 8.02 us
    all_to_all x2 -> x0, blocking collectives: 141 us -> none  [the longest x1 111 us: per_device(): lax.all_to_all(outgoing, 'dp', split_axis=0, concat_axis=0, tiled=True)]
    all_gather x1 -> x0, waiting for transfers between devices: 87 us -> none  [per_device(): assembled = lax.all_gather(arrived[:, None], 'rep', axis=1, tiled=True)]
    ppermute x0 -> x11, waiting for transfers between devices: none -> 80.2 us  [the longest x1 26.2 us: dense_layer(): far_down = lax.ppermute(expert_weights[:, :, 2 * hidden_units:], 'h', SWAP)]
    ppermute x0 -> x11, starting transfers between devices: none -> 14.7 us  [the longest x3 11.2 us: dense_layer(): lax.ppermute(rows, axis, SWAP)]
    all_to_all x1 -> x3, waiting for transfers between devices: 22.8 us -> 9.23 us  [the longest x1 9.22 us: dense_layer(): returned = lax.all_to_all(outbound, ('c',) + chip_axes, 0, 0, tiled=True)]
    all_to_all x1 -> x3, starting transfers between devices: 5.62 us -> 14.7 us  [the longest x1 6.34 us: dense_layer(): weights = lax.all_to_all(expert_weights, chip_axes, 0, 0, tiled=True)]
    dot_general x4, matrix products: 10.1 us -> 3.09 us  [the longest x2 1.94 us: result(): lax.dot_general(hidden, down, (((1,), (1,)), ((), ())), preferred_element...]
    slice x0 -> x8, local copies, waits for them, and re-layouts: none -> 6.46 us  [the longest x1 2.09 us: dense_layer(): far_down = lax.ppermute(expert_weights[:, :, 2 * hidden_units:], 'h', SWAP)]
  transfers between devices with their start and end apart: 2 -> 14, of which waited for: 2 -> 10; matrix products, arithmetic and copies ran while one was open for 0% -> 8% of each run, Pallas kernels for 0% -> 0%
where the time goes in v2:
time: 134 us
  waiting for transfers between devices  89.4 us (67%)
  starting transfers between devices  29.4 us (22%)
  local copies, waits for them, and re-layouts  8.02 us (6%)
  other arithmetic  3.37 us (3%)
  matrix products  3.09 us (2%)
    ppermute x1, waiting for transfers between devices, dense_layer(): far_down = lax.ppermute(expert_weights[:, :, 2 * hidden_units:], 'h', SWAP)  26.2 us
    ppermute x1, waiting for transfers between devices, dense_layer(): lax.ppermute(piece(1 - h, 1 - c), ('h', 'c'), CROSS)  22.5 us
    ppermute x1, waiting for transfers between devices, dense_layer(): far = lax.ppermute(products(2).astype(jnp.bfloat16), 'h', SWAP)  20.3 us
    ppermute x3, starting transfers between devices, dense_layer(): lax.ppermute(rows, axis, SWAP)  11.2 us
    ppermute x3, waiting for transfers between devices, dense_layer(): lax.ppermute(rows, axis, SWAP)  10.4 us
    all_to_all x1, waiting for transfers between devices, dense_layer(): returned = lax.all_to_all(outbound, ('c',) + chip_axes, 0, 0, tiled=True)  9.22 us
    all_to_all x1, starting transfers between devices, dense_layer(): weights = lax.all_to_all(expert_weights, chip_axes, 0, 0, tiled=True)  6.34 us
    all_to_all x1, starting transfers between devices, dense_layer(): far_down = lax.all_to_all(far_down, chip_axes, 0, 0, tiled=True)  4.23 us
  transfers between devices with their start and end apart: 14, of which 10 were waited for; matrix products, arithmetic and copies ran while one was open for 8% of the time, Pallas kernels for 0%

profile of v2, /device:TPU:0, one launch (start us, length us, event | category | flops | bytes accessed | tf_op | source)
XLA Modules:
  0.0 133.6 jit_solution(13592349272925102203)
XLA Ops:
  0.0 6.3 %all-to-all-start = ((bf16[8,64,2304]{2,1,0:T(8,128)(2,1)}), bf16[8,64,2304]{2,1,0:T(8,128)(2,1)}, u32[]{:S(2)}, u32[]{:S(2)}) async-start(bf16[8,64,2304]{2,1,0:T(8,128)(2,1)} %param.8), calls=%async_computation | async-start | bytes 4718592 | tf_op jit(solution)/shard_map/all_to_all | solution.py:43
  6.8 2.7 %collective-permute-start.2 = (bf16[16,512]{1,0:T(8,128)(2,1)S(1)}, bf16[16,512]{1,0:T(8,128)(2,1)S(1)}, u32[]{:S(2)}, u32[]{:S(2)}) collective-permute-start(bf16[16,512]{1,0:T(8,128)(2,1)S(1)} %select_select_fusion), channel_id=1, source_target_pairs={{0,18},{2,16},{16,2},{18,0},{1,19},{3,17},{17,3},{19,1},{4,22},{6,... | collective-permute-start | bytes 49160 | tf_op jit(solution)/shard_map/ppermute | solution.py:69
  9.5 0.4 collective-permute-start.1
  10.0 22.5 %collective-permute-done.2 = bf16[16,512]{1,0:T(8,128)(2,1)S(1)} collective-permute-done((bf16[16,512]{1,0:T(8,128)(2,1)S(1)}, bf16[16,512]{1,0:T(8,128)(2,1)S(1)}, u32[]{:S(2)}, u32[]{:S(2)}) %collective-permute-start.2) | collective-permute-done | bytes 16416 | tf_op jit(solution)/shard_map/ppermute | solution.py:69
  32.6 5.0 %collective-permute-start.3 = (bf16[4,16,512]{2,1,0:T(8,128)(2,1)S(1)}, bf16[4,16,512]{2,1,0:T(8,128)(2,1)S(1)}, u32[]{:S(2)}, u32[]{:S(2)}) collective-permute-start(bf16[4,16,512]{2,1,0:T(8,128)(2,1)S(1)} %pad_maximum_fusion.1), channel_id=1, source_target_pairs={{0,1},{1,0},{2,3},{3,2},{4,5},{5,4},{6,7},{7,6},{8,9},{9,8},{10,11... | collective-permute-start | bytes 196616 | tf_op jit(solution)/shard_map/ppermute | solution.py:73
  37.6 2.2 %collective-permute-done.3 = bf16[4,16,512]{2,1,0:T(8,128)(2,1)S(1)} collective-permute-done((bf16[4,16,512]{2,1,0:T(8,128)(2,1)S(1)}, bf16[4,16,512]{2,1,0:T(8,128)(2,1)S(1)}, u32[]{:S(2)}, u32[]{:S(2)}) %collective-permute-start.3) | collective-permute-done | bytes 65568 | tf_op jit(solution)/shard_map/ppermute | solution.py:73
  39.9 1.5 %collective-permute-start.4 = (bf16[4,32,512]{2,1,0:T(8,128)(2,1)S(1)}, bf16[4,32,512]{2,1,0:T(8,128)(2,1)S(1)}, u32[]{:S(2)}, u32[]{:S(2)}) collective-permute-start(bf16[4,32,512]{2,1,0:T(8,128)(2,1)S(1)} %maximum_select_fusion.3), channel_id=1, source_target_pairs={{0,4},{4,0},{1,5},{5,1},{2,6},{6,2},{3,7},{7,3},{8,12},{12,8},{9,1... | collective-permute-start | bytes 393224 | tf_op jit(solution)/shard_map/ppermute | solution.py:73
  41.4 3.5 %collective-permute-done.4 = bf16[4,32,512]{2,1,0:T(8,128)(2,1)S(1)} collective-permute-done((bf16[4,32,512]{2,1,0:T(8,128)(2,1)S(1)}, bf16[4,32,512]{2,1,0:T(8,128)(2,1)S(1)}, u32[]{:S(2)}, u32[]{:S(2)}) %collective-permute-start.4) | collective-permute-done | bytes 131104 | tf_op jit(solution)/shard_map/ppermute | solution.py:73
  45.0 4.7 %collective-permute-start.5 = (bf16[4,64,512]{2,1,0:T(8,128)(2,1)S(1)}, bf16[4,64,512]{2,1,0:T(8,128)(2,1)S(1)}, u32[]{:S(2)}, u32[]{:S(2)}) collective-permute-start(bf16[4,64,512]{2,1,0:T(8,128)(2,1)S(1)} %maximum_select_fusion.2), channel_id=1, source_target_pairs={{0,8},{8,0},{1,9},{9,1},{2,10},{10,2},{3,11},{11,3},{4,12},{12,4},... | collective-permute-start | bytes 786440 | tf_op jit(solution)/shard_map/ppermute | solution.py:73
  49.6 2.1 %slice.192 = bf16[8,64,768]{2,1,0:T(8,128)(2,1)} slice(bf16[8,64,2304]{2,1,0:T(8,128)(2,1)} %param.8), slice={[0:8], [0:64], [1536:2304]} | slice | bytes 1572864 | tf_op jit(solution)/shard_map/slice | solution.py:42
  51.7 4.6 %collective-permute-done.5 = bf16[4,64,512]{2,1,0:T(8,128)(2,1)S(1)} collective-permute-done((bf16[4,64,512]{2,1,0:T(8,128)(2,1)S(1)}, bf16[4,64,512]{2,1,0:T(8,128)(2,1)S(1)}, u32[]{:S(2)}, u32[]{:S(2)}) %collective-permute-start.5) | collective-permute-done | bytes 262176 | tf_op jit(solution)/shard_map/ppermute | solution.py:73
  56.3 0.2 maximum_select_fusion
  56.5 0.7 fusion.10
  57.3 1.6 %slice.228 = bf16[8,64,1536]{2,1,0:T(8,128)(2,1)S(1)} slice(bf16[8,64,2304]{2,1,0:T(8,128)(2,1)} %all-to-all-done), slice={[0:8], [0:64], [0:1536]} | slice | bytes 3145728 | tf_op jit(solution)/shard_map/slice | solution.py:45
  58.9 0.6 fusion.14
  59.5 0.8 slice.331
  60.3 26.2 %collective-permute-done.10 = bf16[8,64,768]{2,1,0:T(8,128)(2,1)} collective-permute-done((bf16[8,64,768]{2,1,0:T(8,128)(2,1)}, bf16[8,64,768]{2,1,0:T(8,128)(2,1)}, u32[]{:S(2)}, u32[]{:S(2)}) %collective-permute-start.10) | collective-permute-done | bytes 786464 | tf_op jit(solution)/shard_map/ppermute | solution.py:42
  86.5 4.2 %all-to-all-start.1 = ((bf16[8,64,768]{2,1,0:T(8,128)(2,1)}), bf16[8,64,768]{2,1,0:T(8,128)(2,1)}, u32[]{:S(2)}, u32[]{:S(2)}) async-start(bf16[8,64,768]{2,1,0:T(8,128)(2,1)} %collective-permute-done.10), calls=%async_computation.1 | async-start | bytes 1572864 | tf_op jit(solution)/shard_map/all_to_all | solution.py:44
  90.7 0.6 fusion.13
  91.4 1.1 fusion.1
  92.6 0.5 collective-permute-done.6
  93.1 20.3 %collective-permute-done.8 = bf16[128,1536]{1,0:T(8,128)(2,1)S(1)} collective-permute-done((bf16[128,1536]{1,0:T(8,128)(2,1)S(1)}, bf16[128,1536]{1,0:T(8,128)(2,1)S(1)}, u32[]{:S(2)}, u32[]{:S(2)}) %collective-permute-start.8) | collective-permute-done | bytes 393248 | tf_op jit(solution)/shard_map/ppermute | solution.py:82
  113.7 1.2 slice.236
  114.9 0.2 collective-permute-done.9
  115.2 1.5 %convolution_convert_fusion = bf16[256,512]{1,0:T(8,128)(2,1)S(1)} fusion(bf16[512,768]{1,0:T(8,128)(2,1)} %bitcast.23, bf16[128,768]{1,0:T(8,128)(2,1)S(1)} %collective-permute-done.9, bf16[128,768]{1,0:T(8,128)(2,1)S(1)} %fusion.3, pred[]{:T(512)S(6)} %eq.66), kind=kOutput, calls=%fused_computation | convolution fusion | flops 203227136 | bytes 1441793 | tf_op jit(solution)/shard_map/dot_general | solution.py:88
  116.7 0.4 convolution_convert_fusion.1
  117.2 0.9 pad_maximum_fusion
  118.0 4.1 %all-to-all-start.2 = ((bf16[16,16,1024]{2,1,0:T(8,128)(2,1)}), bf16[16,16,1024]{2,1,0:T(8,128)(2,1)S(1)}, u32[]{:S(2)}, u32[]{:S(2)}) async-start(bf16[16,16,1024]{2,1,0:T(8,128)(2,1)} %bitcast.24), calls=%async_computation.2 | async-start | bytes 1048576 | tf_op jit(solution)/shard_map/all_to_all | solution.py:94
  122.3 0.4 select_reduce_fusion
  122.8 9.2 %all-to-all-done.2 = bf16[16,16,1024]{2,1,0:T(8,128)(2,1)S(1)} async-done(((bf16[16,16,1024]{2,1,0:T(8,128)(2,1)}), bf16[16,16,1024]{2,1,0:T(8,128)(2,1)S(1)}, u32[]{:S(2)}, u32[]{:S(2)}) %all-to-all-start.2) | async-done | bytes 524320 | tf_op jit(solution)/shard_map/all_to_all | solution.py:94
  132.4 0.6 copy-done.6
  133.0 0.6 constant_dynamic-update-slice_fusion
  (60 shorter events, 1.8 us)
Async XLA Ops:
  0.0 6.3 %copy-start.1 = (bf16[16,2048]{1,0:T(8,128)(2,1)S(1)}, bf16[16,2048]{1,0:T(8,128)(2,1)}, u32[]{:S(2)}) copy-start(bf16[16,2048]{1,0:T(8,128)(2,1)} %param.6) | copy-start | bytes 196612
  0.0 6.5 %copy-start.2 = (f32[2048]{0:T(1024)S(1)}, f32[2048]{0:T(1024)}, u32[]{:S(2)}) copy-start(f32[2048]{0:T(1024)} %param.7) | copy-start | bytes 24580
  0.0 57.3 %all-to-all-start = ((bf16[8,64,2304]{2,1,0:T(8,128)(2,1)}), bf16[8,64,2304]{2,1,0:T(8,128)(2,1)}, u32[]{:S(2)}, u32[]{:S(2)}) async-start(bf16[8,64,2304]{2,1,0:T(8,128)(2,1)} %param.8), calls=%async_computation | async-start | bytes 4718592 | tf_op jit(solution)/shard_map/all_to_all | solution.py:43
  6.7 3.3 %collective-permute-start = (bf16[16,512]{1,0:T(8,128)(2,1)S(1)}, bf16[16,512]{1,0:T(8,128)(2,1)S(1)}, u32[]{:S(2)}, u32[]{:S(2)}) collective-permute-start(bf16[16,512]{1,0:T(8,128)(2,1)S(1)} %select_select_fusion.2), channel_id=1, source_target_pairs={{0,2},{2,0},{1,3},{3,1},{4,6},{6,4},{5,7},{7,5},{8,10},{10,8},{9,1... | collective-permute-start | bytes 49160 | tf_op jit(solution)/shard_map/ppermute | solution.py:67
  6.8 25.7 %collective-permute-start.2 = (bf16[16,512]{1,0:T(8,128)(2,1)S(1)}, bf16[16,512]{1,0:T(8,128)(2,1)S(1)}, u32[]{:S(2)}, u32[]{:S(2)}) collective-permute-start(bf16[16,512]{1,0:T(8,128)(2,1)S(1)} %select_select_fusion), channel_id=1, source_target_pairs={{0,18},{2,16},{16,2},{18,0},{1,19},{3,17},{17,3},{19,1},{4,22},{6,... | collective-permute-start | bytes 49160 | tf_op jit(solution)/shard_map/ppermute | solution.py:69
  9.5 23.1 %collective-permute-start.1 = (bf16[16,512]{1,0:T(8,128)(2,1)S(1)}, bf16[16,512]{1,0:T(8,128)(2,1)S(1)}, u32[]{:S(2)}, u32[]{:S(2)}) collective-permute-start(bf16[16,512]{1,0:T(8,128)(2,1)S(1)} %select_select_fusion.1), channel_id=1, source_target_pairs={{0,16},{16,0},{1,17},{17,1},{2,18},{18,2},{3,19},{19,3},{4,20},{20... | collective-permute-start | bytes 49160 | tf_op jit(solution)/shard_map/ppermute | solution.py:68
  32.6 7.2 %collective-permute-start.3 = (bf16[4,16,512]{2,1,0:T(8,128)(2,1)S(1)}, bf16[4,16,512]{2,1,0:T(8,128)(2,1)S(1)}, u32[]{:S(2)}, u32[]{:S(2)}) collective-permute-start(bf16[4,16,512]{2,1,0:T(8,128)(2,1)S(1)} %pad_maximum_fusion.1), channel_id=1, source_target_pairs={{0,1},{1,0},{2,3},{3,2},{4,5},{5,4},{6,7},{7,6},{8,9},{9,8},{10,11... | collective-permute-start | bytes 196616 | tf_op jit(solution)/shard_map/ppermute | solution.py:73
  39.9 5.0 %collective-permute-start.4 = (bf16[4,32,512]{2,1,0:T(8,128)(2,1)S(1)}, bf16[4,32,512]{2,1,0:T(8,128)(2,1)S(1)}, u32[]{:S(2)}, u32[]{:S(2)}) collective-permute-start(bf16[4,32,512]{2,1,0:T(8,128)(2,1)S(1)} %maximum_select_fusion.3), channel_id=1, source_target_pairs={{0,4},{4,0},{1,5},{5,1},{2,6},{6,2},{3,7},{7,3},{8,12},{12,8},{9,1... | collective-permute-start | bytes 393224 | tf_op jit(solution)/shard_map/ppermute | solution.py:73
  45.0 11.4 %collective-permute-start.5 = (bf16[4,64,512]{2,1,0:T(8,128)(2,1)S(1)}, bf16[4,64,512]{2,1,0:T(8,128)(2,1)S(1)}, u32[]{:S(2)}, u32[]{:S(2)}) collective-permute-start(bf16[4,64,512]{2,1,0:T(8,128)(2,1)S(1)} %maximum_select_fusion.2), channel_id=1, source_target_pairs={{0,8},{8,0},{1,9},{9,1},{2,10},{10,2},{3,11},{11,3},{4,12},{12,4},... | collective-permute-start | bytes 786440 | tf_op jit(solution)/shard_map/ppermute | solution.py:73
  51.7 34.7 %collective-permute-start.10 = (bf16[8,64,768]{2,1,0:T(8,128)(2,1)}, bf16[8,64,768]{2,1,0:T(8,128)(2,1)}, u32[]{:S(2)}, u32[]{:S(2)}) collective-permute-start(bf16[8,64,768]{2,1,0:T(8,128)(2,1)} %slice.192), channel_id=1, source_target_pairs={{0,16},{16,0},{1,17},{17,1},{2,18},{18,2},{3,19},{19,3},{4,20},{20... | collective-permute-start | bytes 2359304 | tf_op jit(solution)/shard_map/ppermute | solution.py:42
  57.3 1.6 %copy-start = (bf16[2,128,512]{2,1,0:T(8,128)(2,1)S(1)}, bf16[2,128,512]{2,1,0:T(8,128)(2,1)}, u32[]{:S(2)}) copy-start(bf16[2,128,512]{2,1,0:T(8,128)(2,1)} %get-tuple-element.5) | copy-start | bytes 786436
  60.3 31.1 %collective-permute-start.7 = (bf16[128,1536]{1,0:T(8,128)(2,1)}, bf16[128,1536]{1,0:T(8,128)(2,1)}, u32[]{:S(2)}, u32[]{:S(2)}) collective-permute-start(bf16[128,1536]{1,0:T(8,128)(2,1)} %slice.331), channel_id=1, source_target_pairs={{0,2},{2,0},{1,3},{3,1},{4,6},{6,4},{5,7},{7,5},{8,10},{10,8},{9,1... | collective-permute-start | bytes 1179656 | tf_op jit(solution)/shard_map/ppermute | solution.py:79
  86.5 28.5 %all-to-all-start.1 = ((bf16[8,64,768]{2,1,0:T(8,128)(2,1)}), bf16[8,64,768]{2,1,0:T(8,128)(2,1)}, u32[]{:S(2)}, u32[]{:S(2)}) async-start(bf16[8,64,768]{2,1,0:T(8,128)(2,1)} %collective-permute-done.10), calls=%async_computation.1 | async-start | bytes 1572864 | tf_op jit(solution)/shard_map/all_to_all | solution.py:44
  91.3 1.8 %collective-permute-start.6 = (bf16[128,1536]{1,0:T(8,128)(2,1)S(1)}, bf16[128,1536]{1,0:T(8,128)(2,1)S(1)}, u32[]{:S(2)}, u32[]{:S(2)}) collective-permute-start(bf16[128,1536]{1,0:T(8,128)(2,1)S(1)} %slice.332), channel_id=1, source_target_pairs={{0,2},{2,0},{1,3},{3,1},{4,6},{6,4},{5,7},{7,5},{8,10},{10,8},{9,1... | collective-permute-start | bytes 1179656 | tf_op jit(solution)/shard_map/ppermute | solution.py:79
  92.5 20.9 %collective-permute-start.8 = (bf16[128,1536]{1,0:T(8,128)(2,1)S(1)}, bf16[128,1536]{1,0:T(8,128)(2,1)S(1)}, u32[]{:S(2)}, u32[]{:S(2)}) collective-permute-start(bf16[128,1536]{1,0:T(8,128)(2,1)S(1)} %fusion.1), channel_id=1, source_target_pairs={{0,16},{16,0},{1,17},{17,1},{2,18},{18,2},{3,19},{19,3},{4,20},{20... | collective-permute-start | bytes 1179656 | tf_op jit(solution)/shard_map/ppermute | solution.py:82
  113.7 1.5 %collective-permute-start.9 = (bf16[128,768]{1,0:T(8,128)(2,1)S(1)}, bf16[128,768]{1,0:T(8,128)(2,1)S(1)}, u32[]{:S(2)}, u32[]{:S(2)}) collective-permute-start(bf16[128,768]{1,0:T(8,128)(2,1)S(1)} %fusion.3), channel_id=1, source_target_pairs={{0,2},{2,0},{1,3},{3,1},{4,6},{6,4},{5,7},{7,5},{8,10},{10,8},{9,1... | collective-permute-start | bytes 589832 | tf_op jit(solution)/shard_map/ppermute | solution.py:85
  117.1 5.1 %copy-start.3 = (s32[16,8]{0,1:T(8,128)S(1)}, s32[16,8]{0,1:T(8,128)}, u32[]{:S(2)}) copy-start(s32[16,8]{0,1:T(8,128)} %param.10) | copy-start | bytes 1540
  117.1 5.1 %copy-start.5 = (s32[16]{0:T(128)S(1)}, s32[16]{0:T(128)}, u32[]{:S(2)}) copy-start(s32[16]{0:T(128)} %param.9) | copy-start | bytes 196
  117.1 5.6 %copy-start.4 = (f32[16,8]{0,1:T(8,128)S(1)}, f32[16,8]{0,1:T(8,128)}, u32[]{:S(2)}) copy-start(f32[16,8]{0,1:T(8,128)} %param.11) | copy-start | bytes 1540
  118.0 14.0 %all-to-all-start.2 = ((bf16[16,16,1024]{2,1,0:T(8,128)(2,1)}), bf16[16,16,1024]{2,1,0:T(8,128)(2,1)S(1)}, u32[]{:S(2)}, u32[]{:S(2)}) async-start(bf16[16,16,1024]{2,1,0:T(8,128)(2,1)} %bitcast.24), calls=%async_computation.2 | async-start | bytes 1048576 | tf_op jit(solution)/shard_map/all_to_all | solution.py:94
  132.4 0.6 copy-start.6

commit v3 on v2

--- a/solution.py
+++ b/solution.py
@@ -28,75 +28,68 @@
     return jnp.sum(jnp.where(chosen[:, :, None] == numbers[None, None, :], weights, 0.0), axis=1)
 
 
+def exchange(value, axes):
+    return lax.all_to_all(value, axes, 0, 0, tiled=True)
+
+
 def dense_layer(tokens, norm_gain, expert_weights, slot_expert, pair_slots, combine_weights):
     experts, own_rows, packed = expert_weights.shape
     token_count, width = tokens.shape
     hidden_units = packed // 3
+    part = hidden_units // 2
     chip_axes = ("z", "y", "x")
     chips = experts
-    engines = lax.axis_size("x")
     h, c = lax.axis_index("h"), lax.axis_index("c")
-    group = engines * own_rows
-    groups = width // (4 * group)
+    chip = lax.axis_index(chip_axes)
+    group = lax.axis_size("x") * own_rows
+    groups = width // (2 * group)
 
-    far_down = lax.ppermute(expert_weights[:, :, 2 * hidden_units :], "h", SWAP)
-    weights = lax.all_to_all(expert_weights, chip_axes, 0, 0, tiled=True)
-    far_down = lax.all_to_all(far_down, chip_axes, 0, 0, tiled=True)
-    gate_up = weights[:, :, : 2 * hidden_units].reshape(chips * own_rows, 2 * hidden_units)
-    near_down = weights[:, :, 2 * hidden_units :].reshape(chips * own_rows, hidden_units)
-    far_down = far_down.reshape(chips * own_rows, hidden_units)
+    gate, up, own_down = (expert_weights[:, :, i * hidden_units :][:, :, :hidden_units] for i in range(3))
+    blocks = [
+        jnp.concatenate([gate[:, :, i * part :][:, :, :part], up[:, :, i * part :][:, :, :part]], axis=2)
+        for i in range(2)
+    ]
+    gate_up = exchange(jnp.concatenate(blocks), ("h",) + chip_axes)
+    gate_up = gate_up.reshape(width // 2, 2 * part)
+    down = exchange(own_down, chip_axes).reshape(width // 4, hidden_units)
 
     normed = normalize(tokens, norm_gain)
-    pieces = [
-        jnp.concatenate(
-            [normed[:, ((i * groups + g) * 2 + j) * group :][:, :group] for g in range(groups)], axis=1
-        )
-        for i in range(2)
+    columns = [
+        jnp.concatenate([normed[:, (2 * g + j) * group :][:, :group] for g in range(groups)], axis=1)
         for j in range(2)
     ]
+    keep = jnp.where(c == 0, columns[0], columns[1])
+    give = jnp.where(c == 0, columns[1], columns[0])
+    from_c = lax.ppermute(give, "c", SWAP)
+    from_h = lax.ppermute(keep, "h", SWAP)
+    from_hc = lax.ppermute(give, ("h", "c"), CROSS)
+    near = jnp.concatenate(
+        [in_order(h, keep[None], from_h[None], 0), in_order(h, from_c[None], from_hc[None], 0)]
+    )
+    rows = jnp.zeros((4, chips * token_count, width // 2), near.dtype)
+    rows = lax.dynamic_update_slice(rows, near, (0, chip * token_count, 0))
+    for step in range(1, chips):
+        pairs = [(i, i ^ step) for i in range(chips)]
+        arrived = lax.ppermute(near, chip_axes, pairs)
+        rows = lax.dynamic_update_slice(rows, arrived, (0, (chip ^ step) * token_count, 0))
+    count = 2 * chips * token_count
+    rows = rows.reshape(2, count, width // 2)
 
-    def piece(i, j):
-        at = 2 * i + j
-        return jnp.where(
-            at < 2, jnp.where(at == 0, pieces[0], pieces[1]), jnp.where(at == 2, pieces[2], pieces[3])
-        )
-
-    rows = jnp.stack(
-        [
-            piece(h, c),
-            lax.ppermute(piece(h, 1 - c), "c", SWAP),
-            lax.ppermute(piece(1 - h, c), "h", SWAP),
-            lax.ppermute(piece(1 - h, 1 - c), ("h", "c"), CROSS),
-        ]
-    )
-    for axis in ("x", "y", "z"):
-        rows = in_order(lax.axis_index(axis), rows, lax.ppermute(rows, axis, SWAP), 1)
-    count = chips * token_count
-
-    def products(first):
-        block = rows[first : first + 2].reshape(2 * count, -1)
-        sums = jnp.dot(block, gate_up, preferred_element_type=jnp.float32)
-        arrived = lax.ppermute(sums[count:].astype(jnp.bfloat16), "c", SWAP)
-        return sums[:count] + arrived.astype(jnp.float32)
-
-    far = lax.ppermute(products(2).astype(jnp.bfloat16), "h", SWAP)
-    pre = products(0) + far.astype(jnp.float32)
-    hidden = (jax.nn.silu(pre[:, :hidden_units]) * pre[:, hidden_units:]).astype(jnp.bfloat16)
+    other = jnp.dot(rows[1], gate_up, preferred_element_type=jnp.float32).astype(jnp.bfloat16)
+    arrived = lax.ppermute(other, "c", SWAP)
+    pre = jnp.dot(rows[0], gate_up, preferred_element_type=jnp.float32) + arrived.astype(jnp.float32)
+    hidden = (jax.nn.silu(pre[:, :part]) * pre[:, part:]).astype(jnp.bfloat16)
+    hidden = in_order(h, hidden, lax.ppermute(hidden, "h", SWAP), 1)
     hidden = in_order(c, hidden, lax.ppermute(hidden, "c", SWAP), 0)
-
-    def result(down):
-        return lax.dot_general(
-            hidden, down, (((1,), (1,)), ((), ())), preferred_element_type=jnp.float32
-        ).astype(jnp.bfloat16)
-
-    outbound = jnp.concatenate([result(near_down), result(far_down)], axis=1)
-    outbound = outbound.reshape(2 * chips, token_count, width // 2)
-    returned = lax.all_to_all(outbound, ("c",) + chip_axes, 0, 0, tiled=True)
-    returned = returned.reshape(2, chips, token_count, width // 2).astype(jnp.float32)
+    result = lax.dot_general(hidden, down, (((1,), (1,)), ((), ())), preferred_element_type=jnp.float32)
+    result = result.astype(jnp.bfloat16).reshape(4 * chips, token_count, width // 4)
+    returned = exchange(result, ("c", "h") + chip_axes)
+    returned = returned.reshape(2, 2, chips, token_count, width // 4).astype(jnp.float32)
     coefficient = slot_coefficients(slot_expert, pair_slots, combine_weights, experts)
-    mixed = jnp.sum(returned * coefficient.T[None, :, :, None], axis=1).astype(jnp.bfloat16)
-    mixed = in_order(h, mixed[:, :, : width // 4], mixed[:, :, width // 4 :], 2)
-    spans = [mixed[j, :, g * group : (g + 1) * group] for g in range(2 * groups) for j in range(2)]
+    mixed = jnp.sum(returned * coefficient.T[None, None, :, :, None], axis=2).astype(jnp.bfloat16)
+    spans = [
+        mixed[j, i, :, g * group : (g + 1) * group] for i in range(2) for g in range(groups // 2) for j in range(2)
+    ]
     return jnp.concatenate(spans, axis=1)
 
 

time: 134 us -> 110 us (0.82)
  waiting for transfers between devices: 89.4 us -> 59.9 us
  starting transfers between devices: 29.4 us -> 34.7 us
  local copies, waits for them, and re-layouts: 8.02 us -> 6.45 us
    ppermute x10 -> x12, waiting for transfers between devices: 80 us -> 41.6 us  [the longest x7 31.4 us: dense_layer(): arrived = lax.ppermute(near, chip_axes, pairs)]
    all_to_all x3, waiting for transfers between devices: 9.23 us -> 18.3 us  [exchange(): return lax.all_to_all(value, axes, 0, 0, tiled=True)]
    all_to_all x3, starting transfers between devices: 14.7 us -> 18.1 us  [exchange(): return lax.all_to_all(value, axes, 0, 0, tiled=True)]
    ppermute x10 -> x12, starting transfers between devices: 14.6 us -> 16.6 us  [the longest x7 9.35 us: dense_layer(): arrived = lax.ppermute(near, chip_axes, pairs)]
    slice x8 -> x3, local copies, waits for them, and re-layouts: 6.46 us -> 4.5 us  [the longest x1 2.06 us: dense_layer(): expert_weights[:, :, i * hidden_units:][:, :, :hidden_units]]
    dot_general x4 -> x3, matrix products: 3.09 us -> 4.39 us  [the longest x1 2.39 us: dense_layer(): jnp.dot(rows[1], gate_up, preferred_element_type=jnp.float32)]
  transfers between devices with their start and end apart: 14 -> 16, of which waited for: 10 -> 9; matrix products, arithmetic and copies ran while one was open for 8% -> 7% of each run, Pallas kernels for 0% -> 0%
where the time goes in v3:
time: 110 us
  waiting for transfers between devices  59.9 us (54%)
  starting transfers between devices  34.7 us (32%)
  local copies, waits for them, and re-layouts  6.45 us (6%)
  matrix products  4.39 us (4%)
  other arithmetic  4.1 us (4%)
    ppermute x7, waiting for transfers between devices, dense_layer(): arrived = lax.ppermute(near, chip_axes, pairs)  31.4 us
    all_to_all x3, waiting for transfers between devices, exchange(): return lax.all_to_all(value, axes, 0, 0, tiled=True)  18.3 us
    all_to_all x3, starting transfers between devices, exchange(): return lax.all_to_all(value, axes, 0, 0, tiled=True)  18.1 us
    ppermute x1, waiting for transfers between devices, dense_layer(): hidden = in_order(h, hidden, lax.ppermute(hidden, 'h', SWAP), 1)  10.2 us
    ppermute x7, starting transfers between devices, dense_layer(): arrived = lax.ppermute(near, chip_axes, pairs)  9.35 us
    ppermute x1, starting transfers between devices, dense_layer(): from_hc = lax.ppermute(give, ('h', 'c'), CROSS)  3.69 us
    ppermute x1, starting transfers between devices, dense_layer(): hidden = in_order(h, hidden, lax.ppermute(hidden, 'h', SWAP), 1)  2.92 us
    dot_general x1, matrix products, dense_layer(): jnp.dot(rows[1], gate_up, preferred_element_type=jnp.float32)  2.39 us
  transfers between devices with their start and end apart: 16, of which 9 were waited for; matrix products, arithmetic and copies ran while one was open for 7% of the time, Pallas kernels for 0%

profile of v3, /device:TPU:0, one launch (start us, length us, event | category | flops | bytes accessed | tf_op | source)
XLA Modules:
  0.0 109.9 jit_solution(51658854946377148)
XLA Ops:
  0.0 1.0 fusion.8
  1.0 0.9 fusion.10
  2.1 0.6 collective-permute-start.1
  2.7 3.7 %collective-permute-start.2 = (bf16[16,1024]{1,0:T(8,128)(2,1)S(1)}, bf16[16,1024]{1,0:T(8,128)(2,1)S(1)}, u32[]{:S(2)}, u32[]{:S(2)}) collective-permute-start(bf16[16,1024]{1,0:T(8,128)(2,1)S(1)} %get-tuple-element.30), channel_id=1, source_target_pairs={{0,18},{2,16},{16,2},{18,0},{1,19},{3,17},{17,3},{19,1},{4,22},{6,... | collective-permute-start | bytes 98312 | tf_op jit(solution)/shard_map/ppermute | solution.py:65
  6.4 1.5 %fusion.12 = (bf16[8,64,384]{2,1,0:T(8,128)(2,1)S(1)}, bf16[8,64,384]{2,1,0:T(8,128)(2,1)S(1)}, bf16[8,64,384]{2,1,0:T(8,128)(2,1)S(1)}, bf16[8,64,384]{2,1,0:T(8,128)(2,1)S(1)}) fusion(bf16[8,64,2304]{2,1,0:T(8,128)(2,1)} %param.8), kind=kLoop, calls=%fused_computation.105 | loop fusion | bytes 3145728 | tf_op jit(solution)/shard_map/slice | solution.py:49
  8.0 1.3 %maximum_maximum_fusion = bf16[16,64,768]{2,1,0:T(8,128)(2,1)} fusion(bf16[8,64,384]{2,1,0:T(8,128)(2,1)S(1)} %get-tuple-element.8, bf16[8,64,384]{2,1,0:T(8,128)(2,1)S(1)} %get-tuple-element.6, bf16[8,64,384]{2,1,0:T(8,128)(2,1)S(1)} %get-tuple-element.7, bf16[8,64,384]{2,1,0:T(8,128)(2,1)S(1)} %get-tuple-element.5), kind=kLoop, calls=%fused_computation | loop fusion | flops 6291456 | bytes 3145728 | tf_op jit(solution)/shard_map/concatenate | solution.py:52
  9.3 7.2 %all-to-all-start = ((bf16[16,64,768]{2,1,0:T(8,128)(2,1)}), bf16[16,64,768]{2,1,0:T(8,128)(2,1)S(1)}, u32[]{:S(2)}, u32[]{:S(2)}) async-start(bf16[16,64,768]{2,1,0:T(8,128)(2,1)} %maximum_maximum_fusion), calls=%async_computation | async-start | bytes 3145728 | tf_op jit(solution)/shard_map/all_to_all | solution.py:32
  16.8 2.0 %collective-permute-start.3 = (bf16[4,16,1024]{2,1,0:T(8,128)(2,1)S(1)}, bf16[4,16,1024]{2,1,0:T(8,128)(2,1)S(1)}, u32[]{:S(2)}, u32[]{:S(2)}) collective-permute-start(bf16[4,16,1024]{2,1,0:T(8,128)(2,1)S(1)} %get-tuple-element.11), channel_id=1, source_target_pairs={{0,1},{1,0},{4,5},{5,4},{8,9},{9,8},{12,13},{13,12},{2,3},{3,2},{6... | collective-permute-start | bytes 393224 | tf_op jit(solution)/shard_map/ppermute | solution.py:73
  18.8 1.5 %collective-permute-start.4 = (bf16[4,16,1024]{2,1,0:T(8,128)(2,1)S(1)}, bf16[4,16,1024]{2,1,0:T(8,128)(2,1)S(1)}, u32[]{:S(2)}, u32[]{:S(2)}) collective-permute-start(bf16[4,16,1024]{2,1,0:T(8,128)(2,1)S(1)} %get-tuple-element.11), channel_id=1, source_target_pairs={{0,4},{1,5},{4,0},{5,1},{8,12},{9,13},{12,8},{13,9},{2,6},{3,7},{6... | collective-permute-start | bytes 393224 | tf_op jit(solution)/shard_map/ppermute | solution.py:73
  20.4 1.9 %collective-permute-start.6 = (bf16[4,16,1024]{2,1,0:T(8,128)(2,1)S(1)}, bf16[4,16,1024]{2,1,0:T(8,128)(2,1)S(1)}, u32[]{:S(2)}, u32[]{:S(2)}) collective-permute-start(bf16[4,16,1024]{2,1,0:T(8,128)(2,1)S(1)} %get-tuple-element.11), channel_id=1, source_target_pairs={{0,8},{1,9},{4,12},{5,13},{8,0},{9,1},{12,4},{13,5},{2,10},{3,11},... | collective-permute-start | bytes 393224 | tf_op jit(solution)/shard_map/ppermute | solution.py:73
  22.3 1.5 %collective-permute-start.7 = (bf16[4,16,1024]{2,1,0:T(8,128)(2,1)S(1)}, bf16[4,16,1024]{2,1,0:T(8,128)(2,1)S(1)}, u32[]{:S(2)}, u32[]{:S(2)}) collective-permute-start(bf16[4,16,1024]{2,1,0:T(8,128)(2,1)S(1)} %get-tuple-element.11), channel_id=1, source_target_pairs={{0,9},{1,8},{4,13},{5,12},{8,1},{9,0},{12,5},{13,4},{2,11},{3,10},... | collective-permute-start | bytes 393224 | tf_op jit(solution)/shard_map/ppermute | solution.py:73
  23.7 3.3 %collective-permute-done.3 = bf16[4,16,1024]{2,1,0:T(8,128)(2,1)S(1)} collective-permute-done((bf16[4,16,1024]{2,1,0:T(8,128)(2,1)S(1)}, bf16[4,16,1024]{2,1,0:T(8,128)(2,1)S(1)}, u32[]{:S(2)}, u32[]{:S(2)}) %collective-permute-start.3) | collective-permute-done | bytes 131104 | tf_op jit(solution)/shard_map/ppermute | solution.py:73
  27.1 2.4 %collective-permute-start.8 = (bf16[4,16,1024]{2,1,0:T(8,128)(2,1)S(1)}, bf16[4,16,1024]{2,1,0:T(8,128)(2,1)S(1)}, u32[]{:S(2)}, u32[]{:S(2)}) collective-permute-start(bf16[4,16,1024]{2,1,0:T(8,128)(2,1)S(1)} %get-tuple-element.11), channel_id=1, source_target_pairs={{0,12},{1,13},{4,8},{5,9},{8,4},{9,5},{12,0},{13,1},{2,14},{3,15},... | collective-permute-start | bytes 393224 | tf_op jit(solution)/shard_map/ppermute | solution.py:73
  29.5 6.3 %collective-permute-done.4 = bf16[4,16,1024]{2,1,0:T(8,128)(2,1)S(1)} collective-permute-done((bf16[4,16,1024]{2,1,0:T(8,128)(2,1)S(1)}, bf16[4,16,1024]{2,1,0:T(8,128)(2,1)S(1)}, u32[]{:S(2)}, u32[]{:S(2)}) %collective-permute-start.4) | collective-permute-done | bytes 131104 | tf_op jit(solution)/shard_map/ppermute | solution.py:73
  35.8 10.0 %collective-permute-done.6 = bf16[4,16,1024]{2,1,0:T(8,128)(2,1)S(1)} collective-permute-done((bf16[4,16,1024]{2,1,0:T(8,128)(2,1)S(1)}, bf16[4,16,1024]{2,1,0:T(8,128)(2,1)S(1)}, u32[]{:S(2)}, u32[]{:S(2)}) %collective-permute-start.6) | collective-permute-done | bytes 131104 | tf_op jit(solution)/shard_map/ppermute | solution.py:73
  45.8 5.6 %collective-permute-done.7 = bf16[4,16,1024]{2,1,0:T(8,128)(2,1)S(1)} collective-permute-done((bf16[4,16,1024]{2,1,0:T(8,128)(2,1)S(1)}, bf16[4,16,1024]{2,1,0:T(8,128)(2,1)S(1)}, u32[]{:S(2)}, u32[]{:S(2)}) %collective-permute-start.7) | collective-permute-done | bytes 131104 | tf_op jit(solution)/shard_map/ppermute | solution.py:73
  51.5 3.8 %collective-permute-done.8 = bf16[4,16,1024]{2,1,0:T(8,128)(2,1)S(1)} collective-permute-done((bf16[4,16,1024]{2,1,0:T(8,128)(2,1)S(1)}, bf16[4,16,1024]{2,1,0:T(8,128)(2,1)S(1)}, u32[]{:S(2)}, u32[]{:S(2)}) %collective-permute-start.8) | collective-permute-done | bytes 131104 | tf_op jit(solution)/shard_map/ppermute | solution.py:73
  55.3 2.3 %collective-permute-done.9 = bf16[4,16,1024]{2,1,0:T(8,128)(2,1)S(1)} collective-permute-done((bf16[4,16,1024]{2,1,0:T(8,128)(2,1)S(1)}, bf16[4,16,1024]{2,1,0:T(8,128)(2,1)S(1)}, u32[]{:S(2)}, u32[]{:S(2)}) %collective-permute-start.9) | collective-permute-done | bytes 131104 | tf_op jit(solution)/shard_map/ppermute | solution.py:73
  57.7 0.9 fusion.13
  58.6 2.4 %convolution_convert_fusion.1 = bf16[256,768]{1,0:T(8,128)(2,1)} fusion(bf16[256,1024]{1,0:T(8,128)(2,1)} %bitcast.117, bf16[1024,768]{1,0:T(8,128)(2,1)S(1)} %bitcast.113), kind=kOutput, calls=%fused_computation.3 | convolution fusion | flops 402849792 | bytes 2490368 | tf_op jit(solution)/shard_map/dot_general | solution.py:78
  61.0 2.1 %slice.185 = bf16[8,64,768]{2,1,0:T(8,128)(2,1)} slice(bf16[8,64,2304]{2,1,0:T(8,128)(2,1)} %param.8), slice={[0:8], [0:64], [1536:2304]} | slice | bytes 1572864 | tf_op jit(solution)/shard_map/slice | solution.py:47
  63.0 3.5 %all-to-all-start.1 = ((bf16[8,64,768]{2,1,0:T(8,128)(2,1)}), bf16[8,64,768]{2,1,0:T(8,128)(2,1)S(1)}, u32[]{:S(2)}, u32[]{:S(2)}) async-start(bf16[8,64,768]{2,1,0:T(8,128)(2,1)} %slice.185), calls=%async_computation.1 | async-start | bytes 1572864 | tf_op jit(solution)/shard_map/all_to_all | solution.py:32
  66.6 0.6 convolution_add_fusion
  67.3 2.9 %collective-permute-start.11 = (bf16[256,384]{1,0:T(8,128)(2,1)S(1)}, bf16[256,384]{1,0:T(8,128)(2,1)S(1)}, u32[]{:S(2)}, u32[]{:S(2)}) collective-permute-start(bf16[256,384]{1,0:T(8,128)(2,1)S(1)} %fusion.7), channel_id=1, source_target_pairs={{0,16},{16,0},{1,17},{17,1},{2,18},{18,2},{3,19},{19,3},{4,20},{20... | collective-permute-start | bytes 589832 | tf_op jit(solution)/shard_map/ppermute | solution.py:82
  70.2 10.2 %collective-permute-done.11 = bf16[256,384]{1,0:T(8,128)(2,1)S(1)} collective-permute-done((bf16[256,384]{1,0:T(8,128)(2,1)S(1)}, bf16[256,384]{1,0:T(8,128)(2,1)S(1)}, u32[]{:S(2)}, u32[]{:S(2)}) %collective-permute-start.11) | collective-permute-done | bytes 196640 | tf_op jit(solution)/shard_map/ppermute | solution.py:82
  80.6 2.1 %all-to-all-done.1 = bf16[8,64,768]{2,1,0:T(8,128)(2,1)S(1)} async-done(((bf16[8,64,768]{2,1,0:T(8,128)(2,1)}), bf16[8,64,768]{2,1,0:T(8,128)(2,1)S(1)}, u32[]{:S(2)}, u32[]{:S(2)}) %all-to-all-start.1) | async-done | bytes 786464 | tf_op jit(solution)/shard_map/all_to_all | solution.py:32
  82.7 1.4 %convolution_convert_fusion = bf16[512,512]{1,0:T(8,128)(2,1)} fusion(bf16[512,768]{1,0:T(8,128)(2,1)S(1)} %bitcast.116, bf16[256,768]{1,0:T(8,128)(2,1)S(1)} %collective-permute-done.12, bf16[256,768]{1,0:T(8,128)(2,1)S(1)} %maximum_select_fusion.2, pred[]{:T(512)S(6)} %eq.16), kind=kOutput, calls=%fused_computation.1 | convolution fusion | flops 406454272 | bytes 2097153 | tf_op jit(solution)/shard_map/dot_general | solution.py:84
  84.1 7.4 %all-to-all-start.2 = ((bf16[32,16,512]{2,1,0:T(8,128)(2,1)}), bf16[32,16,512]{2,1,0:T(8,128)(2,1)S(1)}, u32[]{:S(2)}, u32[]{:S(2)}) async-start(bf16[32,16,512]{2,1,0:T(8,128)(2,1)} %bitcast.23), calls=%async_computation.2 | async-start | bytes 1048576 | tf_op jit(solution)/shard_map/all_to_all | solution.py:32
  91.6 0.4 select_reduce_fusion
  92.1 16.2 %all-to-all-done.2 = bf16[32,16,512]{2,1,0:T(8,128)(2,1)S(1)} async-done(((bf16[32,16,512]{2,1,0:T(8,128)(2,1)}), bf16[32,16,512]{2,1,0:T(8,128)(2,1)S(1)}, u32[]{:S(2)}, u32[]{:S(2)}) %all-to-all-start.2) | async-done | bytes 524320 | tf_op jit(solution)/shard_map/all_to_all | solution.py:32
  108.7 0.6 copy-done.3
  109.3 0.6 constant_dynamic-update-slice_fusion.32
  (77 shorter events, 1.4 us)
Async XLA Ops:
  2.1 14.5 %collective-permute-start.1 = (bf16[16,1024]{1,0:T(8,128)(2,1)S(1)}, bf16[16,1024]{1,0:T(8,128)(2,1)S(1)}, u32[]{:S(2)}, u32[]{:S(2)}) collective-permute-start(bf16[16,1024]{1,0:T(8,128)(2,1)S(1)} %get-tuple-element.30), channel_id=1, source_target_pairs={{0,2},{2,0},{1,3},{3,1},{4,6},{6,4},{5,7},{7,5},{8,10},{10,8},{9,1... | collective-permute-start | bytes 98312 | tf_op jit(solution)/shard_map/ppermute | solution.py:63
  2.7 13.9 %collective-permute-start.2 = (bf16[16,1024]{1,0:T(8,128)(2,1)S(1)}, bf16[16,1024]{1,0:T(8,128)(2,1)S(1)}, u32[]{:S(2)}, u32[]{:S(2)}) collective-permute-start(bf16[16,1024]{1,0:T(8,128)(2,1)S(1)} %get-tuple-element.30), channel_id=1, source_target_pairs={{0,18},{2,16},{16,2},{18,0},{1,19},{3,17},{17,3},{19,1},{4,22},{6,... | collective-permute-start | bytes 98312 | tf_op jit(solution)/shard_map/ppermute | solution.py:65
  6.4 10.2 %collective-permute-start = (bf16[16,1024]{1,0:T(8,128)(2,1)S(1)}, bf16[16,1024]{1,0:T(8,128)(2,1)S(1)}, u32[]{:S(2)}, u32[]{:S(2)}) collective-permute-start(bf16[16,1024]{1,0:T(8,128)(2,1)S(1)} %get-tuple-element.29), channel_id=1, source_target_pairs={{0,16},{16,0},{1,17},{17,1},{2,18},{18,2},{3,19},{19,3},{4,20},{20... | collective-permute-start | bytes 98312 | tf_op jit(solution)/shard_map/ppermute | solution.py:64
  9.3 49.3 %all-to-all-start = ((bf16[16,64,768]{2,1,0:T(8,128)(2,1)}), bf16[16,64,768]{2,1,0:T(8,128)(2,1)S(1)}, u32[]{:S(2)}, u32[]{:S(2)}) async-start(bf16[16,64,768]{2,1,0:T(8,128)(2,1)} %maximum_maximum_fusion), calls=%async_computation | async-start | bytes 3145728 | tf_op jit(solution)/shard_map/all_to_all | solution.py:32
  16.8 10.3 %collective-permute-start.3 = (bf16[4,16,1024]{2,1,0:T(8,128)(2,1)S(1)}, bf16[4,16,1024]{2,1,0:T(8,128)(2,1)S(1)}, u32[]{:S(2)}, u32[]{:S(2)}) collective-permute-start(bf16[4,16,1024]{2,1,0:T(8,128)(2,1)S(1)} %get-tuple-element.11), channel_id=1, source_target_pairs={{0,1},{1,0},{4,5},{5,4},{8,9},{9,8},{12,13},{13,12},{2,3},{3,2},{6... | collective-permute-start | bytes 393224 | tf_op jit(solution)/shard_map/ppermute | solution.py:73
  18.8 17.0 %collective-permute-start.4 = (bf16[4,16,1024]{2,1,0:T(8,128)(2,1)S(1)}, bf16[4,16,1024]{2,1,0:T(8,128)(2,1)S(1)}, u32[]{:S(2)}, u32[]{:S(2)}) collective-permute-start(bf16[4,16,1024]{2,1,0:T(8,128)(2,1)S(1)} %get-tuple-element.11), channel_id=1, source_target_pairs={{0,4},{1,5},{4,0},{5,1},{8,12},{9,13},{12,8},{13,9},{2,6},{3,7},{6... | collective-permute-start | bytes 393224 | tf_op jit(solution)/shard_map/ppermute | solution.py:73
  20.3 15.5 %collective-permute-start.5 = (bf16[4,16,1024]{2,1,0:T(8,128)(2,1)S(1)}, bf16[4,16,1024]{2,1,0:T(8,128)(2,1)S(1)}, u32[]{:S(2)}, u32[]{:S(2)}) collective-permute-start(bf16[4,16,1024]{2,1,0:T(8,128)(2,1)S(1)} %get-tuple-element.11), channel_id=1, source_target_pairs={{0,5},{1,4},{4,1},{5,0},{8,13},{9,12},{12,9},{13,8},{2,7},{3,6},{6... | collective-permute-start | bytes 393224 | tf_op jit(solution)/shard_map/ppermute | solution.py:73
  20.4 25.4 %collective-permute-start.6 = (bf16[4,16,1024]{2,1,0:T(8,128)(2,1)S(1)}, bf16[4,16,1024]{2,1,0:T(8,128)(2,1)S(1)}, u32[]{:S(2)}, u32[]{:S(2)}) collective-permute-start(bf16[4,16,1024]{2,1,0:T(8,128)(2,1)S(1)} %get-tuple-element.11), channel_id=1, source_target_pairs={{0,8},{1,9},{4,12},{5,13},{8,0},{9,1},{12,4},{13,5},{2,10},{3,11},... | collective-permute-start | bytes 393224 | tf_op jit(solution)/shard_map/ppermute | solution.py:73
  22.3 29.2 %collective-permute-start.7 = (bf16[4,16,1024]{2,1,0:T(8,128)(2,1)S(1)}, bf16[4,16,1024]{2,1,0:T(8,128)(2,1)S(1)}, u32[]{:S(2)}, u32[]{:S(2)}) collective-permute-start(bf16[4,16,1024]{2,1,0:T(8,128)(2,1)S(1)} %get-tuple-element.11), channel_id=1, source_target_pairs={{0,9},{1,8},{4,13},{5,12},{8,1},{9,0},{12,5},{13,4},{2,11},{3,10},... | collective-permute-start | bytes 393224 | tf_op jit(solution)/shard_map/ppermute | solution.py:73
  27.1 28.2 %collective-permute-start.8 = (bf16[4,16,1024]{2,1,0:T(8,128)(2,1)S(1)}, bf16[4,16,1024]{2,1,0:T(8,128)(2,1)S(1)}, u32[]{:S(2)}, u32[]{:S(2)}) collective-permute-start(bf16[4,16,1024]{2,1,0:T(8,128)(2,1)S(1)} %get-tuple-element.11), channel_id=1, source_target_pairs={{0,12},{1,13},{4,8},{5,9},{8,4},{9,5},{12,0},{13,1},{2,14},{3,15},... | collective-permute-start | bytes 393224 | tf_op jit(solution)/shard_map/ppermute | solution.py:73
  35.8 21.9 %collective-permute-start.9 = (bf16[4,16,1024]{2,1,0:T(8,128)(2,1)S(1)}, bf16[4,16,1024]{2,1,0:T(8,128)(2,1)S(1)}, u32[]{:S(2)}, u32[]{:S(2)}) collective-permute-start(bf16[4,16,1024]{2,1,0:T(8,128)(2,1)S(1)} %get-tuple-element.11), channel_id=1, source_target_pairs={{0,13},{1,12},{4,9},{5,8},{8,5},{9,4},{12,1},{13,0},{2,15},{3,14},... | collective-permute-start | bytes 393224 | tf_op jit(solution)/shard_map/ppermute | solution.py:73
  61.0 5.6 %collective-permute-start.10 = (bf16[256,768]{1,0:T(8,128)(2,1)}, bf16[256,768]{1,0:T(8,128)(2,1)S(1)}, u32[]{:S(2)}, u32[]{:S(2)}) collective-permute-start(bf16[256,768]{1,0:T(8,128)(2,1)} %convolution_convert_fusion.1), channel_id=1, source_target_pairs={{0,2},{2,0},{1,3},{3,1},{4,6},{6,4},{5,7},{7,5},{8,10},{10,8},{9,1... | collective-permute-start | bytes 1179656 | tf_op jit(solution)/shard_map/ppermute | solution.py:79
  63.0 19.6 %all-to-all-start.1 = ((bf16[8,64,768]{2,1,0:T(8,128)(2,1)}), bf16[8,64,768]{2,1,0:T(8,128)(2,1)S(1)}, u32[]{:S(2)}, u32[]{:S(2)}) async-start(bf16[8,64,768]{2,1,0:T(8,128)(2,1)} %slice.185), calls=%async_computation.1 | async-start | bytes 1572864 | tf_op jit(solution)/shard_map/all_to_all | solution.py:32
  67.3 13.1 %collective-permute-start.11 = (bf16[256,384]{1,0:T(8,128)(2,1)S(1)}, bf16[256,384]{1,0:T(8,128)(2,1)S(1)}, u32[]{:S(2)}, u32[]{:S(2)}) collective-permute-start(bf16[256,384]{1,0:T(8,128)(2,1)S(1)} %fusion.7), channel_id=1, source_target_pairs={{0,16},{16,0},{1,17},{17,1},{2,18},{18,2},{3,19},{19,3},{4,20},{20... | collective-permute-start | bytes 589832 | tf_op jit(solution)/shard_map/ppermute | solution.py:82
  80.5 2.2 %collective-permute-start.12 = (bf16[256,768]{1,0:T(8,128)(2,1)S(1)}, bf16[256,768]{1,0:T(8,128)(2,1)S(1)}, u32[]{:S(2)}, u32[]{:S(2)}) collective-permute-start(bf16[256,768]{1,0:T(8,128)(2,1)S(1)} %maximum_select_fusion.2), channel_id=1, source_target_pairs={{0,2},{2,0},{1,3},{3,1},{4,6},{6,4},{5,7},{7,5},{8,10},{10,8},{9,1... | collective-permute-start | bytes 1179656 | tf_op jit(solution)/shard_map/ppermute | solution.py:83
  82.7 8.8 %copy-start = (s32[16,8]{0,1:T(8,128)S(1)}, s32[16,8]{0,1:T(8,128)}, u32[]{:S(2)}) copy-start(s32[16,8]{0,1:T(8,128)} %param.10) | copy-start | bytes 1540
  82.7 8.9 %copy-start.2 = (s32[16]{0:T(128)S(1)}, s32[16]{0:T(128)}, u32[]{:S(2)}) copy-start(s32[16]{0:T(128)} %param.9) | copy-start | bytes 196
  82.7 9.4 %copy-start.1 = (f32[16,8]{0,1:T(8,128)S(1)}, f32[16,8]{0,1:T(8,128)}, u32[]{:S(2)}) copy-start(f32[16,8]{0,1:T(8,128)} %param.11) | copy-start | bytes 1540
  84.1 24.2 %all-to-all-start.2 = ((bf16[32,16,512]{2,1,0:T(8,128)(2,1)}), bf16[32,16,512]{2,1,0:T(8,128)(2,1)S(1)}, u32[]{:S(2)}, u32[]{:S(2)}) async-start(bf16[32,16,512]{2,1,0:T(8,128)(2,1)} %bitcast.23), calls=%async_computation.2 | async-start | bytes 1048576 | tf_op jit(solution)/shard_map/all_to_all | solution.py:32
  108.7 0.6 copy-start.3

commit v4 on v3

--- a/solution.py
+++ b/solution.py
@@ -1,9 +1,12 @@
 import jax
 import jax.numpy as jnp
 from jax import lax
+from jax.experimental import pallas as pl
+from jax.experimental.pallas import tpu as pltpu
 from jax.sharding import Mesh, PartitionSpec as P
 
 SWAP = [(0, 1), (1, 0)]
+PACK_STEPS = 4
 CROSS = [(0, 3), (1, 2), (2, 1), (3, 0)]
 
 
@@ -30,6 +33,52 @@
 
 def exchange(value, axes):
     return lax.all_to_all(value, axes, 0, 0, tiled=True)
+
+
+def pack_kernel(weights, packed):
+    hidden_units = packed.shape[-1]
+    part = hidden_units // 2
+    for i in range(2):
+        packed[i, :, :, :part] = weights[:, :, i * part : (i + 1) * part]
+        packed[i, :, :, part:] = weights[:, :, hidden_units + i * part : hidden_units + (i + 1) * part]
+
+
+def pack(weights, hidden_units):
+    experts, rows, _ = weights.shape
+    step = experts // PACK_STEPS
+    return pl.pallas_call(
+        pack_kernel,
+        name="pack",
+        grid=(PACK_STEPS,),
+        in_specs=[pl.BlockSpec((step, rows, 2 * hidden_units), lambda k: (k, 0, 0))],
+        out_specs=pl.BlockSpec((2, step, rows, hidden_units), lambda k: (0, k, 0, 0)),
+        out_shape=jax.ShapeDtypeStruct((2, experts, rows, hidden_units), weights.dtype),
+    )(weights)
+
+
+def gather_kernel(place, *refs):
+    *blocks, out, arrived = refs
+    rows = blocks[0].shape[1]
+    copies = []
+    for step, block in enumerate(blocks):
+        target = out.at[pl.ds((place[0] ^ step) * rows, rows)]
+        copies.append(pltpu.make_async_copy(block.at[0], target, arrived.at[step]))
+        copies[-1].start()
+    for copy in copies:
+        copy.wait()
+
+
+def gather_blocks(chip, blocks):
+    _, rows, columns = blocks[0].shape
+    return pl.pallas_call(
+        gather_kernel,
+        name="gather_blocks",
+        in_specs=[pl.BlockSpec(memory_space=pltpu.SMEM)]
+        + [pl.BlockSpec(memory_space=pltpu.HBM)] * len(blocks),
+        out_specs=pl.BlockSpec(memory_space=pltpu.VMEM),
+        out_shape=jax.ShapeDtypeStruct((len(blocks) * rows, columns), blocks[0].dtype),
+        scratch_shapes=[pltpu.SemaphoreType.DMA((len(blocks),))],
+    )(chip.reshape(1).astype(jnp.int32), *blocks)
 
 
 def dense_layer(tokens, norm_gain, expert_weights, slot_expert, pair_slots, combine_weights):
@@ -44,14 +93,14 @@
     group = lax.axis_size("x") * own_rows
     groups = width // (2 * group)
 
-    gate, up, own_down = (expert_weights[:, :, i * hidden_units :][:, :, :hidden_units] for i in range(3))
-    blocks = [
-        jnp.concatenate([gate[:, :, i * part :][:, :, :part], up[:, :, i * part :][:, :, :part]], axis=2)
-        for i in range(2)
-    ]
-    gate_up = exchange(jnp.concatenate(blocks), ("h",) + chip_axes)
+    gate_up = pack(expert_weights, hidden_units)
+    gate_up = exchange(gate_up.reshape(2 * experts, own_rows, 2 * part), ("h",) + chip_axes)
     gate_up = gate_up.reshape(width // 2, 2 * part)
-    down = exchange(own_down, chip_axes).reshape(width // 4, hidden_units)
+    own_down = expert_weights[:, :, 2 * hidden_units :]
+    down = [lax.dynamic_slice_in_dim(own_down, chip ^ step, 1, 0) for step in range(chips)]
+    for step in range(1, chips):
+        down[step] = lax.ppermute(down[step], chip_axes, [(i, i ^ step) for i in range(chips)])
+    down = gather_blocks(chip, down)
 
     normed = normalize(tokens, norm_gain)
     columns = [
@@ -63,33 +112,48 @@
     from_c = lax.ppermute(give, "c", SWAP)
     from_h = lax.ppermute(keep, "h", SWAP)
     from_hc = lax.ppermute(give, ("h", "c"), CROSS)
-    near = jnp.concatenate(
-        [in_order(h, keep[None], from_h[None], 0), in_order(h, from_c[None], from_hc[None], 0)]
-    )
-    rows = jnp.zeros((4, chips * token_count, width // 2), near.dtype)
-    rows = lax.dynamic_update_slice(rows, near, (0, chip * token_count, 0))
-    for step in range(1, chips):
-        pairs = [(i, i ^ step) for i in range(chips)]
-        arrived = lax.ppermute(near, chip_axes, pairs)
-        rows = lax.dynamic_update_slice(rows, arrived, (0, (chip ^ step) * token_count, 0))
-    count = 2 * chips * token_count
-    rows = rows.reshape(2, count, width // 2)
-
-    other = jnp.dot(rows[1], gate_up, preferred_element_type=jnp.float32).astype(jnp.bfloat16)
+    near = jnp.stack([in_order(h, keep, from_h, 0), in_order(h, from_c, from_hc, 0)])
+    z, plane = lax.axis_index("z"), lax.axis_index(("y", "x"))
+    column = in_order(z, near[:, None], lax.ppermute(near, "z", SWAP)[:, None], 1)
+    rows = jnp.zeros((2, 2, chips // 2, 2 * token_count, width // 2), near.dtype)
+    rows = lax.dynamic_update_slice(rows, column[:, :, None], (0, 0, plane, 0, 0))
+    for step in range(1, chips // 2):
+        pairs = [(i, i ^ step) for i in range(chips // 2)]
+        arrived = lax.ppermute(column, ("y", "x"), pairs)
+        rows = lax.dynamic_update_slice(rows, arrived[:, :, None], (0, 0, plane ^ step, 0, 0))
+    count = chips * token_count
+    rows = rows.reshape(2, 1, 2 * count, width // 2)
+
+    other = jnp.dot(rows[1, 0], gate_up, preferred_element_type=jnp.float32).astype(jnp.bfloat16)
     arrived = lax.ppermute(other, "c", SWAP)
-    pre = jnp.dot(rows[0], gate_up, preferred_element_type=jnp.float32) + arrived.astype(jnp.float32)
+    pre = jnp.dot(rows[0, 0], gate_up, preferred_element_type=jnp.float32) + arrived.astype(jnp.float32)
     hidden = (jax.nn.silu(pre[:, :part]) * pre[:, part:]).astype(jnp.bfloat16)
-    hidden = in_order(h, hidden, lax.ppermute(hidden, "h", SWAP), 1)
-    hidden = in_order(c, hidden, lax.ppermute(hidden, "c", SWAP), 0)
+    far = lax.ppermute(hidden, "h", SWAP)
+    coefficient = slot_coefficients(slot_expert, pair_slots, combine_weights, experts).T
+    far_weights = lax.ppermute(coefficient, "h", SWAP)
+    far, far_weights = lax.optimization_barrier((far, far_weights))
+    near_weights = in_order(h, coefficient, far_weights, 1)
+    coefficient = in_order(c, near_weights, lax.ppermute(near_weights, "c", SWAP), 1)
+    hidden = in_order(h, hidden, far, 1).reshape(chips, 2 * token_count, hidden_units)
+    hidden = in_order(c, hidden, lax.ppermute(hidden, "c", SWAP), 1)
+    hidden = hidden.reshape(2 * count * 2, hidden_units)
     result = lax.dot_general(hidden, down, (((1,), (1,)), ((), ())), preferred_element_type=jnp.float32)
-    result = result.astype(jnp.bfloat16).reshape(4 * chips, token_count, width // 4)
-    returned = exchange(result, ("c", "h") + chip_axes)
-    returned = returned.reshape(2, 2, chips, token_count, width // 4).astype(jnp.float32)
-    coefficient = slot_coefficients(slot_expert, pair_slots, combine_weights, experts)
-    mixed = jnp.sum(returned * coefficient.T[None, None, :, :, None], axis=2).astype(jnp.bfloat16)
-    spans = [
-        mixed[j, i, :, g * group : (g + 1) * group] for i in range(2) for g in range(groups // 2) for j in range(2)
-    ]
+    result = result.astype(jnp.bfloat16).reshape(chips, 4 * token_count, width // 4)
+    returned = exchange(result, chip_axes).astype(jnp.float32)
+    mixed = jnp.sum(returned * coefficient[:, :, None], axis=0).astype(jnp.bfloat16)
+    mixed = mixed.reshape(2, 2, token_count, width // 4)
+
+    def owned(j, i):
+        first, second = jnp.where(i == 0, mixed[0, 0], mixed[0, 1]), jnp.where(i == 0, mixed[1, 0], mixed[1, 1])
+        return jnp.where(j == 0, first, second)
+
+    from_h = lax.ppermute(owned(c, 1 - h), "h", SWAP)
+    from_hc = lax.ppermute(owned(1 - c, 1 - h), ("h", "c"), CROSS)
+    from_c = lax.ppermute(owned(1 - c, h), "c", SWAP)
+    mine = in_order(h, owned(c, h), from_h, 1)
+    theirs = in_order(h, from_c, from_hc, 1)
+    even, odd = jnp.where(c == 0, mine, theirs), jnp.where(c == 0, theirs, mine)
+    spans = [side[:, g * group : (g + 1) * group] for g in range(groups) for side in (even, odd)]
     return jnp.concatenate(spans, axis=1)
 
 

time: 110 us -> 128 us (1.16)
  waiting for transfers between devices: 59.9 us -> 80 us
  Pallas kernels: 0 us -> 5.79 us
  local copies, waits for them, and re-layouts: 6.45 us -> 4.02 us
  other arithmetic: 4.1 us -> 1.69 us
  matrix products: 4.39 us -> 2.54 us
  starting transfers between devices: 34.7 us -> 33.2 us
    ppermute x1, waiting for transfers between devices: 0.01 us -> 35.9 us  [dense_layer(): from_h = lax.ppermute(keep, 'h', SWAP)]
    all_to_all x3 -> x2, waiting for transfers between devices: 18.3 us -> 6.58 us  [exchange(): return lax.all_to_all(value, axes, 0, 0, tiled=True)]
    all_to_all x3 -> x2, starting transfers between devices: 18.1 us -> 12 us  [exchange(): return lax.all_to_all(value, axes, 0, 0, tiled=True)]
    pallas_call x0 -> x2, Pallas kernels: none -> 5.79 us  [the longest x1 3.62 us: pack(): pl.pallas_call(pack_kernel, name='pack', grid=(PACK_STEPS,), in_specs=[pl...]
    ppermute x9 -> x18, starting transfers between devices: 12.3 us -> 18.1 us  [the longest x7 7.74 us: dense_layer(): lax.ppermute(down[step], chip_axes, [(i, i ^ step) for i in range(chips)])]
    ppermute x9 -> x18, waiting for transfers between devices: 41.6 us -> 35.9 us  [the longest x3 10.8 us: dense_layer(): arrived = lax.ppermute(column, ('y', 'x'), pairs)]
    slice x3, local copies, waits for them, and re-layouts: 4.5 us -> 0.1 us  [the longest x1 0.09 us: dense_layer(): rows[1, 0]]
    ppermute x1, starting transfers between devices: 3.69 us -> 0.22 us  [dense_layer(): from_hc = lax.ppermute(give, ('h', 'c'), CROSS)]
  transfers between devices with their start and end apart: 16 -> 24, of which waited for: 9 -> 16; matrix products, arithmetic and copies ran while one was open for 7% -> 2% of each run, Pallas kernels for 0% -> 2%
where the time goes in v4:
time: 128 us
  waiting for transfers between devices  80 us (62%)
  starting transfers between devices  33.2 us (26%)
  Pallas kernels  5.79 us (5%)
  local copies, waits for them, and re-layouts  4.02 us (3%)
  matrix products  2.54 us (2%)
  other arithmetic  1.69 us (1%)
    ppermute x1, waiting for transfers between devices, dense_layer(): from_h = lax.ppermute(keep, 'h', SWAP)  35.9 us
    all_to_all x2, starting transfers between devices, exchange(): return lax.all_to_all(value, axes, 0, 0, tiled=True)  12 us
    ppermute x3, waiting for transfers between devices, dense_layer(): arrived = lax.ppermute(column, ('y', 'x'), pairs)  10.8 us
    ppermute x1, waiting for transfers between devices, dense_layer(): far_weights = lax.ppermute(coefficient, 'h', SWAP)  8.73 us
    ppermute x7, waiting for transfers between devices, dense_layer(): lax.ppermute(down[step], chip_axes, [(i, i ^ step) for i in range(chips)])  7.89 us
    ppermute x7, starting transfers between devices, dense_layer(): lax.ppermute(down[step], chip_axes, [(i, i ^ step) for i in range(chips)])  7.74 us
    all_to_all x2, waiting for transfers between devices, exchange(): return lax.all_to_all(value, axes, 0, 0, tiled=True)  6.58 us
    ppermute x1, waiting for transfers between devices, dense_layer(): lax.ppermute(near, 'z', SWAP)[:, None]  5.51 us
  transfers between devices with their start and end apart: 24, of which 16 were waited for; matrix products, arithmetic and copies ran while one was open for 2% of the time, Pallas kernels for 2%

profile of v4, /device:TPU:0, one launch (start us, length us, event | category | flops | bytes accessed | tf_op | source)
XLA Modules:
  0.0 127.8 jit_solution(4588079073773698737)
XLA Ops:
  0.0 3.6 %pack.1 = bf16[2,8,64,768]{3,2,1,0:T(8,128)(2,1)} custom-call(bf16[8,64,2304]{2,1,0:T(8,128)(2,1)} %weights.1), custom_call_target="tpu_custom_call" | custom-call | tf_op jit(solution)/shard_map/pack/pallas_call | solution.py:49
  3.6 8.5 %all-to-all-start = ((bf16[16,64,768]{2,1,0:T(8,128)(2,1)}), bf16[16,64,768]{2,1,0:T(8,128)(2,1)S(1)}, u32[]{:S(2)}, u32[]{:S(2)}) async-start(bf16[16,64,768]{2,1,0:T(8,128)(2,1)} %bitcast.47), calls=%async_computation | async-start | bytes 3145728 | tf_op jit(solution)/shard_map/all_to_all | solution.py:35
  12.5 2.9 %collective-permute-start = (bf16[16,1024]{1,0:T(8,128)(2,1)S(1)}, bf16[16,1024]{1,0:T(8,128)(2,1)S(1)}, u32[]{:S(2)}, u32[]{:S(2)}) collective-permute-start(bf16[16,1024]{1,0:T(8,128)(2,1)S(1)} %get-tuple-element.27), channel_id=1, source_target_pairs={{0,16},{16,0},{1,17},{17,1},{2,18},{18,2},{3,19},{19,3},{4,20},{20... | collective-permute-start | bytes 98312 | tf_op jit(solution)/shard_map/ppermute | solution.py:113
  15.6 35.9 %collective-permute-done = bf16[16,1024]{1,0:T(8,128)(2,1)S(1)} collective-permute-done((bf16[16,1024]{1,0:T(8,128)(2,1)S(1)}, bf16[16,1024]{1,0:T(8,128)(2,1)S(1)}, u32[]{:S(2)}, u32[]{:S(2)}) %collective-permute-start) | collective-permute-done | bytes 32800 | tf_op jit(solution)/shard_map/ppermute | solution.py:113
  51.7 5.5 %collective-permute-done.3 = bf16[2,32,1024]{2,1,0:T(8,128)(2,1)S(1)} collective-permute-done((bf16[2,32,1024]{2,1,0:T(8,128)(2,1)S(1)}, bf16[2,32,1024]{2,1,0:T(8,128)(2,1)S(1)}, u32[]{:S(2)}, u32[]{:S(2)}) %collective-permute-start.3) | collective-permute-done | bytes 131104 | tf_op jit(solution)/shard_map/ppermute | solution.py:117
  57.2 1.5 %collective-permute-start.4 = (bf16[2,2,32,1024]{3,2,1,0:T(8,128)(2,1)S(1)}, bf16[2,2,32,1024]{3,2,1,0:T(8,128)(2,1)S(1)}, u32[]{:S(2)}, u32[]{:S(2)}) collective-permute-start(bf16[2,2,32,1024]{3,2,1,0:T(8,128)(2,1)S(1)} %maximum_select_fusion.3), channel_id=1, source_target_pairs={{0,1},{1,0},{4,5},{5,4},{2,3},{3,2},{6,7},{7,6},{8,9},{9,8},{12,13... | collective-permute-start | bytes 786440 | tf_op jit(solution)/shard_map/ppermute | solution.py:122
  58.7 2.2 %collective-permute-start.5 = (bf16[2,2,32,1024]{3,2,1,0:T(8,128)(2,1)S(1)}, bf16[2,2,32,1024]{3,2,1,0:T(8,128)(2,1)S(1)}, u32[]{:S(2)}, u32[]{:S(2)}) collective-permute-start(bf16[2,2,32,1024]{3,2,1,0:T(8,128)(2,1)S(1)} %maximum_select_fusion.3), channel_id=1, source_target_pairs={{0,4},{1,5},{4,0},{5,1},{2,6},{3,7},{6,2},{7,3},{8,12},{9,13},{12,... | collective-permute-start | bytes 786440 | tf_op jit(solution)/shard_map/ppermute | solution.py:122
  61.5 5.0 %collective-permute-done.4 = bf16[2,2,32,1024]{3,2,1,0:T(8,128)(2,1)S(1)} collective-permute-done((bf16[2,2,32,1024]{3,2,1,0:T(8,128)(2,1)S(1)}, bf16[2,2,32,1024]{3,2,1,0:T(8,128)(2,1)S(1)}, u32[]{:S(2)}, u32[]{:S(2)}) %collective-permute-start.4) | collective-permute-done | bytes 262176 | tf_op jit(solution)/shard_map/ppermute | solution.py:122
  66.5 4.8 %collective-permute-done.5 = bf16[2,2,32,1024]{3,2,1,0:T(8,128)(2,1)S(1)} collective-permute-done((bf16[2,2,32,1024]{3,2,1,0:T(8,128)(2,1)S(1)}, bf16[2,2,32,1024]{3,2,1,0:T(8,128)(2,1)S(1)}, u32[]{:S(2)}, u32[]{:S(2)}) %collective-permute-start.5) | collective-permute-done | bytes 262176 | tf_op jit(solution)/shard_map/ppermute | solution.py:122
  71.3 1.1 collective-permute-done.6
  73.2 1.6 %collective-permute-done.7 = bf16[256,768]{1,0:T(8,128)(2,1)S(1)} collective-permute-done((bf16[256,768]{1,0:T(8,128)(2,1)S(1)}, bf16[256,768]{1,0:T(8,128)(2,1)S(1)}, u32[]{:S(2)}, u32[]{:S(2)}) %collective-permute-start.7) | collective-permute-done | bytes 393248 | tf_op jit(solution)/shard_map/ppermute | solution.py:128
  76.2 3.0 %collective-permute-start.9 = (f32[8,16]{1,0:T(8,128)S(1)}, f32[8,16]{1,0:T(8,128)S(1)}, u32[]{:S(2)}, u32[]{:S(2)}) collective-permute-start(f32[8,16]{1,0:T(8,128)S(1)} %bitcast.61), channel_id=1, source_target_pairs={{0,16},{16,0},{1,17},{17,1},{2,18},{18,2},{3,19},{19,3},{4,20},{20... | collective-permute-start | bytes 1544 | tf_op jit(solution)/shard_map/ppermute | solution.py:133
  79.1 8.7 %collective-permute-done.9 = f32[8,16]{1,0:T(8,128)S(1)} collective-permute-done((f32[8,16]{1,0:T(8,128)S(1)}, f32[8,16]{1,0:T(8,128)S(1)}, u32[]{:S(2)}, u32[]{:S(2)}) %collective-permute-start.9) | collective-permute-done | bytes 544 | tf_op jit(solution)/shard_map/ppermute | solution.py:133
  88.8 1.1 collective-permute-start.11
  89.9 1.3 collective-permute-start.12
  91.2 1.1 collective-permute-start.13
  92.3 1.7 %collective-permute-done.11.refs_1_ = bf16[1,64,768]{2,1,0:T(8,128)(2,1)S(1)} collective-permute-done((bf16[1,64,768]{2,1,0:T(8,128)(2,1)S(1)}, bf16[1,64,768]{2,1,0:T(8,128)(2,1)S(1)}, u32[]{:S(2)}, u32[]{:S(2)}) %collective-permute-start.11) | collective-permute-done | bytes 98336 | tf_op jit(solution)/shard_map/ppermute | solution.py:102
  94.9 0.8 collective-permute-done.12.refs_2_
  95.7 1.6 %collective-permute-start.16 = (bf16[1,64,768]{2,1,0:T(8,128)(2,1)S(1)}, bf16[1,64,768]{2,1,0:T(8,128)(2,1)S(1)}, u32[]{:S(2)}, u32[]{:S(2)}) collective-permute-start(bf16[1,64,768]{2,1,0:T(8,128)(2,1)S(1)} %get-tuple-element.12), channel_id=1, source_target_pairs={{0,12},{1,13},{4,8},{5,9},{8,4},{9,5},{12,0},{13,1},{2,14},{3,15},... | collective-permute-start | bytes 294920 | tf_op jit(solution)/shard_map/ppermute | solution.py:102
  97.3 1.8 %collective-permute-start.17 = (bf16[1,64,768]{2,1,0:T(8,128)(2,1)S(1)}, bf16[1,64,768]{2,1,0:T(8,128)(2,1)S(1)}, u32[]{:S(2)}, u32[]{:S(2)}) collective-permute-start(bf16[1,64,768]{2,1,0:T(8,128)(2,1)S(1)} %get-tuple-element.11), channel_id=1, source_target_pairs={{0,13},{1,12},{4,9},{5,8},{8,5},{9,4},{12,1},{13,0},{2,15},{3,14},... | collective-permute-start | bytes 294920 | tf_op jit(solution)/shard_map/ppermute | solution.py:102
  99.1 1.5 %collective-permute-done.15.refs_5_ = bf16[1,64,768]{2,1,0:T(8,128)(2,1)S(1)} collective-permute-done((bf16[1,64,768]{2,1,0:T(8,128)(2,1)S(1)}, bf16[1,64,768]{2,1,0:T(8,128)(2,1)S(1)}, u32[]{:S(2)}, u32[]{:S(2)}) %collective-permute-start.15) | collective-permute-done | bytes 98336 | tf_op jit(solution)/shard_map/ppermute | solution.py:102
  100.6 2.4 %collective-permute-done.16.refs_6_ = bf16[1,64,768]{2,1,0:T(8,128)(2,1)S(1)} collective-permute-done((bf16[1,64,768]{2,1,0:T(8,128)(2,1)S(1)}, bf16[1,64,768]{2,1,0:T(8,128)(2,1)S(1)}, u32[]{:S(2)}, u32[]{:S(2)}) %collective-permute-start.16) | collective-permute-done | bytes 98336 | tf_op jit(solution)/shard_map/ppermute | solution.py:102
  103.1 1.4 %collective-permute-done.17.refs_7_ = bf16[1,64,768]{2,1,0:T(8,128)(2,1)S(1)} collective-permute-done((bf16[1,64,768]{2,1,0:T(8,128)(2,1)S(1)}, bf16[1,64,768]{2,1,0:T(8,128)(2,1)S(1)}, u32[]{:S(2)}, u32[]{:S(2)}) %collective-permute-start.17) | collective-permute-done | bytes 98336 | tf_op jit(solution)/shard_map/ppermute | solution.py:102
  105.1 2.2 %gather_blocks.1 = bf16[512,768]{1,0:T(8,128)(2,1)} custom-call(s32[1]{0:T(128)} %bitcast.21.place, bf16[1,64,768]{2,1,0:T(8,128)(2,1)} %get-tuple-element.18.refs_0_, bf16[1,64,768]{2,1,0:T(8,128)(2,1)} %copy-done.2, bf16[1,64,768]{2,1,0:T(8,128)(2,1)} %copy-done.3, bf16[1,64,768]{2,1,0:T(8,128)(2,1)} %copy-done.4, bf16[1,64,768]{2,1,0:T(8,128)(2,1)} %copy-done.5, ...), custom_call_target="tpu_custom_call" | custom-call | tf_op jit(solution)/shard_map/gather_blocks/pallas_call | solution.py:73
  107.6 0.8 copy-done
  108.4 1.4 %convolution_convert_fusion = bf16[512,512]{1,0:T(8,128)(2,1)} fusion(bf16[512,768]{1,0:T(8,128)(2,1)S(1)} %bitcast.49, bf16[512,768]{1,0:T(8,128)(2,1)S(1)} %copy-done), kind=kOutput, calls=%fused_computation | convolution fusion | flops 402915328 | bytes 2097152 | tf_op jit(solution)/shard_map/dot_general | solution.py:140
  109.8 3.5 %all-to-all-start.1 = ((bf16[8,64,512]{2,1,0:T(8,128)(2,1)}), bf16[8,64,512]{2,1,0:T(8,128)(2,1)S(1)}, u32[]{:S(2)}, u32[]{:S(2)}) async-start(bf16[8,64,512]{2,1,0:T(8,128)(2,1)} %bitcast.22), calls=%async_computation.1 | async-start | bytes 1048576 | tf_op jit(solution)/shard_map/all_to_all | solution.py:35
  113.4 1.1 collective-permute-done.18
  114.7 6.6 %all-to-all-done.1 = bf16[8,64,512]{2,1,0:T(8,128)(2,1)S(1)} async-done(((bf16[8,64,512]{2,1,0:T(8,128)(2,1)}), bf16[8,64,512]{2,1,0:T(8,128)(2,1)S(1)}, u32[]{:S(2)}, u32[]{:S(2)}) %all-to-all-start.1) | async-done | bytes 524320 | tf_op jit(solution)/shard_map/all_to_all | solution.py:35
  121.4 0.8 collective-permute-start.19
  122.3 2.3 %collective-permute-start.21 = (bf16[16,512]{1,0:T(8,128)(2,1)S(1)}, bf16[16,512]{1,0:T(8,128)(2,1)S(1)}, u32[]{:S(2)}, u32[]{:S(2)}) collective-permute-start(bf16[16,512]{1,0:T(8,128)(2,1)S(1)} %get-tuple-element.26), channel_id=1, source_target_pairs={{0,18},{2,16},{16,2},{18,0},{1,19},{3,17},{17,3},{19,1},{4,22},{6,... | collective-permute-start | bytes 49160 | tf_op jit(solution)/shard_map/ppermute | solution.py:151
  124.6 1.6 %collective-permute-done.19 = bf16[16,512]{1,0:T(8,128)(2,1)S(1)} collective-permute-done((bf16[16,512]{1,0:T(8,128)(2,1)S(1)}, bf16[16,512]{1,0:T(8,128)(2,1)S(1)}, u32[]{:S(2)}, u32[]{:S(2)}) %collective-permute-start.19) | collective-permute-done | bytes 16416 | tf_op jit(solution)/shard_map/ppermute | solution.py:150
  (103 shorter events, 7.9 us)
Async XLA Ops:
  3.6 8.5 %copy-start.1 = (bf16[16,2048]{1,0:T(8,128)(2,1)S(1)}, bf16[16,2048]{1,0:T(8,128)(2,1)}, u32[]{:S(2)}) copy-start(bf16[16,2048]{1,0:T(8,128)(2,1)} %param.6) | copy-start | bytes 196612
  3.6 8.6 %copy-start.9 = (f32[2048]{0:T(1024)S(1)}, f32[2048]{0:T(1024)}, u32[]{:S(2)}) copy-start(f32[2048]{0:T(1024)} %param.7) | copy-start | bytes 24580
  3.6 68.9 %all-to-all-start = ((bf16[16,64,768]{2,1,0:T(8,128)(2,1)}), bf16[16,64,768]{2,1,0:T(8,128)(2,1)S(1)}, u32[]{:S(2)}, u32[]{:S(2)}) async-start(bf16[16,64,768]{2,1,0:T(8,128)(2,1)} %bitcast.47), calls=%async_computation | async-start | bytes 3145728 | tf_op jit(solution)/shard_map/all_to_all | solution.py:35
  12.5 39.0 %collective-permute-start = (bf16[16,1024]{1,0:T(8,128)(2,1)S(1)}, bf16[16,1024]{1,0:T(8,128)(2,1)S(1)}, u32[]{:S(2)}, u32[]{:S(2)}) collective-permute-start(bf16[16,1024]{1,0:T(8,128)(2,1)S(1)} %get-tuple-element.27), channel_id=1, source_target_pairs={{0,16},{16,0},{1,17},{17,1},{2,18},{18,2},{3,19},{19,3},{4,20},{20... | collective-permute-start | bytes 98312 | tf_op jit(solution)/shard_map/ppermute | solution.py:113
  15.4 36.1 %collective-permute-start.1 = (bf16[16,1024]{1,0:T(8,128)(2,1)S(1)}, bf16[16,1024]{1,0:T(8,128)(2,1)S(1)}, u32[]{:S(2)}, u32[]{:S(2)}) collective-permute-start(bf16[16,1024]{1,0:T(8,128)(2,1)S(1)} %get-tuple-element.28), channel_id=1, source_target_pairs={{0,2},{2,0},{1,3},{3,1},{4,6},{6,4},{5,7},{7,5},{8,10},{10,8},{9,1... | collective-permute-start | bytes 98312 | tf_op jit(solution)/shard_map/ppermute | solution.py:112
  15.4 36.1 %collective-permute-start.2 = (bf16[16,1024]{1,0:T(8,128)(2,1)S(1)}, bf16[16,1024]{1,0:T(8,128)(2,1)S(1)}, u32[]{:S(2)}, u32[]{:S(2)}) collective-permute-start(bf16[16,1024]{1,0:T(8,128)(2,1)S(1)} %get-tuple-element.28), channel_id=1, source_target_pairs={{0,18},{2,16},{16,2},{18,0},{1,19},{3,17},{17,3},{19,1},{4,22},{6,... | collective-permute-start | bytes 98312 | tf_op jit(solution)/shard_map/ppermute | solution.py:114
  51.6 5.6 %collective-permute-start.3 = (bf16[2,32,1024]{2,1,0:T(8,128)(2,1)S(1)}, bf16[2,32,1024]{2,1,0:T(8,128)(2,1)S(1)}, u32[]{:S(2)}, u32[]{:S(2)}) collective-permute-start(bf16[2,32,1024]{2,1,0:T(8,128)(2,1)S(1)} %get-tuple-element.21), channel_id=1, source_target_pairs={{0,8},{8,0},{1,9},{9,1},{2,10},{10,2},{3,11},{11,3},{4,12},{12,4},... | collective-permute-start | bytes 393224 | tf_op jit(solution)/shard_map/ppermute | solution.py:117
  57.2 9.2 %collective-permute-start.4 = (bf16[2,2,32,1024]{3,2,1,0:T(8,128)(2,1)S(1)}, bf16[2,2,32,1024]{3,2,1,0:T(8,128)(2,1)S(1)}, u32[]{:S(2)}, u32[]{:S(2)}) collective-permute-start(bf16[2,2,32,1024]{3,2,1,0:T(8,128)(2,1)S(1)} %maximum_select_fusion.3), channel_id=1, source_target_pairs={{0,1},{1,0},{4,5},{5,4},{2,3},{3,2},{6,7},{7,6},{8,9},{9,8},{12,13... | collective-permute-start | bytes 786440 | tf_op jit(solution)/shard_map/ppermute | solution.py:122
  58.7 12.5 %collective-permute-start.5 = (bf16[2,2,32,1024]{3,2,1,0:T(8,128)(2,1)S(1)}, bf16[2,2,32,1024]{3,2,1,0:T(8,128)(2,1)S(1)}, u32[]{:S(2)}, u32[]{:S(2)}) collective-permute-start(bf16[2,2,32,1024]{3,2,1,0:T(8,128)(2,1)S(1)} %maximum_select_fusion.3), channel_id=1, source_target_pairs={{0,4},{1,5},{4,0},{5,1},{2,6},{3,7},{6,2},{7,3},{8,12},{9,13},{12,... | collective-permute-start | bytes 786440 | tf_op jit(solution)/shard_map/ppermute | solution.py:122
  60.9 11.4 %collective-permute-start.6 = (bf16[2,2,32,1024]{3,2,1,0:T(8,128)(2,1)S(1)}, bf16[2,2,32,1024]{3,2,1,0:T(8,128)(2,1)S(1)}, u32[]{:S(2)}, u32[]{:S(2)}) collective-permute-start(bf16[2,2,32,1024]{3,2,1,0:T(8,128)(2,1)S(1)} %maximum_select_fusion.3), channel_id=1, source_target_pairs={{0,5},{1,4},{4,1},{5,0},{2,7},{3,6},{6,3},{7,2},{8,13},{9,12},{12,... | collective-permute-start | bytes 786440 | tf_op jit(solution)/shard_map/ppermute | solution.py:122
  73.1 1.8 %collective-permute-start.7 = (bf16[256,768]{1,0:T(8,128)(2,1)S(1)}, bf16[256,768]{1,0:T(8,128)(2,1)S(1)}, u32[]{:S(2)}, u32[]{:S(2)}) collective-permute-start(bf16[256,768]{1,0:T(8,128)(2,1)S(1)} %convolution_convert_fusion.1), channel_id=1, source_target_pairs={{0,2},{2,0},{1,3},{3,1},{4,6},{6,4},{5,7},{7,5},{8,10},{10,8},{9,1... | collective-permute-start | bytes 1179656 | tf_op jit(solution)/shard_map/ppermute | solution.py:128
  75.4 12.7 %slice-start = ((bf16[8,64,2304]{2,1,0:T(8,128)(2,1)}), bf16[8,64,768]{2,1,0:T(8,128)(2,1)S(1)}, s32[]{:S(2)}) async-start(bf16[8,64,2304]{2,1,0:T(8,128)(2,1)} %weights.1), calls=%async_computation.2 | async-start | bytes 1572864 | tf_op jit(solution)/shard_map/slice | solution.py:99
  75.6 12.3 %collective-permute-start.8 = (bf16[256,384]{1,0:T(8,128)(2,1)S(1)}, bf16[256,384]{1,0:T(8,128)(2,1)S(1)}, u32[]{:S(2)}, u32[]{:S(2)}) collective-permute-start(bf16[256,384]{1,0:T(8,128)(2,1)S(1)} %fusion), channel_id=1, source_target_pairs={{0,16},{16,0},{1,17},{17,1},{2,18},{18,2},{3,19},{19,3},{4,20},{20... | collective-permute-start | bytes 589832 | tf_op jit(solution)/shard_map/ppermute | solution.py:131
  76.2 11.7 %collective-permute-start.9 = (f32[8,16]{1,0:T(8,128)S(1)}, f32[8,16]{1,0:T(8,128)S(1)}, u32[]{:S(2)}, u32[]{:S(2)}) collective-permute-start(f32[8,16]{1,0:T(8,128)S(1)} %bitcast.61), channel_id=1, source_target_pairs={{0,16},{16,0},{1,17},{17,1},{2,18},{18,2},{3,19},{19,3},{4,20},{20... | collective-permute-start | bytes 1544 | tf_op jit(solution)/shard_map/ppermute | solution.py:133
  88.0 19.3 %collective-permute-start.10 = (bf16[8,32,768]{2,1,0:T(8,128)(2,1)S(1)}, bf16[8,32,768]{2,1,0:T(8,128)(2,1)S(1)}, u32[]{:S(2)}, u32[]{:S(2)}) collective-permute-start(bf16[8,32,768]{2,1,0:T(8,128)(2,1)S(1)} %maximum_select_fusion.1), channel_id=1, source_target_pairs={{0,2},{2,0},{1,3},{3,1},{4,6},{6,4},{5,7},{7,5},{8,10},{10,8},{9,1... | collective-permute-start | bytes 1179656 | tf_op jit(solution)/shard_map/ppermute | solution.py:138
  88.8 5.2 %collective-permute-start.11 = (bf16[1,64,768]{2,1,0:T(8,128)(2,1)S(1)}, bf16[1,64,768]{2,1,0:T(8,128)(2,1)S(1)}, u32[]{:S(2)}, u32[]{:S(2)}) collective-permute-start(bf16[1,64,768]{2,1,0:T(8,128)(2,1)S(1)} %get-tuple-element.17), channel_id=1, source_target_pairs={{0,1},{1,0},{4,5},{5,4},{8,9},{9,8},{12,13},{13,12},{2,3},{3,2},{6... | collective-permute-start | bytes 294920 | tf_op jit(solution)/shard_map/ppermute | solution.py:102
  89.9 5.8 %collective-permute-start.12 = (bf16[1,64,768]{2,1,0:T(8,128)(2,1)S(1)}, bf16[1,64,768]{2,1,0:T(8,128)(2,1)S(1)}, u32[]{:S(2)}, u32[]{:S(2)}) collective-permute-start(bf16[1,64,768]{2,1,0:T(8,128)(2,1)S(1)} %get-tuple-element.16), channel_id=1, source_target_pairs={{0,4},{1,5},{4,0},{5,1},{8,12},{9,13},{12,8},{13,9},{2,6},{3,7},{6... | collective-permute-start | bytes 294920 | tf_op jit(solution)/shard_map/ppermute | solution.py:102
  91.2 6.2 %collective-permute-start.13 = (bf16[1,64,768]{2,1,0:T(8,128)(2,1)S(1)}, bf16[1,64,768]{2,1,0:T(8,128)(2,1)S(1)}, u32[]{:S(2)}, u32[]{:S(2)}) collective-permute-start(bf16[1,64,768]{2,1,0:T(8,128)(2,1)S(1)} %get-tuple-element.15), channel_id=1, source_target_pairs={{0,5},{1,4},{4,1},{5,0},{8,13},{9,12},{12,9},{13,8},{2,7},{3,6},{6... | collective-permute-start | bytes 294920 | tf_op jit(solution)/shard_map/ppermute | solution.py:102
  92.3 6.8 %collective-permute-start.14 = (bf16[1,64,768]{2,1,0:T(8,128)(2,1)S(1)}, bf16[1,64,768]{2,1,0:T(8,128)(2,1)S(1)}, u32[]{:S(2)}, u32[]{:S(2)}) collective-permute-start(bf16[1,64,768]{2,1,0:T(8,128)(2,1)S(1)} %get-tuple-element.14), channel_id=1, source_target_pairs={{0,8},{1,9},{4,12},{5,13},{8,0},{9,1},{12,4},{13,5},{2,10},{3,11},... | collective-permute-start | bytes 294920 | tf_op jit(solution)/shard_map/ppermute | solution.py:102
  94.1 10.4 %copy-start.2 = (bf16[1,64,768]{2,1,0:T(8,128)(2,1)}, bf16[1,64,768]{2,1,0:T(8,128)(2,1)S(1)}, u32[]{:S(2)}) copy-start(bf16[1,64,768]{2,1,0:T(8,128)(2,1)S(1)} %collective-permute-done.11.refs_1_) | copy-start | bytes 294916
  94.1 6.6 %collective-permute-start.15 = (bf16[1,64,768]{2,1,0:T(8,128)(2,1)S(1)}, bf16[1,64,768]{2,1,0:T(8,128)(2,1)S(1)}, u32[]{:S(2)}, u32[]{:S(2)}) collective-permute-start(bf16[1,64,768]{2,1,0:T(8,128)(2,1)S(1)} %get-tuple-element.13), channel_id=1, source_target_pairs={{0,9},{1,8},{4,13},{5,12},{8,1},{9,0},{12,5},{13,4},{2,11},{3,10},... | collective-permute-start | bytes 294920 | tf_op jit(solution)/shard_map/ppermute | solution.py:102
  95.7 8.8 %copy-start.3 = (bf16[1,64,768]{2,1,0:T(8,128)(2,1)}, bf16[1,64,768]{2,1,0:T(8,128)(2,1)S(1)}, u32[]{:S(2)}) copy-start(bf16[1,64,768]{2,1,0:T(8,128)(2,1)S(1)} %collective-permute-done.12.refs_2_) | copy-start | bytes 294916
  95.7 7.4 %collective-permute-start.16 = (bf16[1,64,768]{2,1,0:T(8,128)(2,1)S(1)}, bf16[1,64,768]{2,1,0:T(8,128)(2,1)S(1)}, u32[]{:S(2)}, u32[]{:S(2)}) collective-permute-start(bf16[1,64,768]{2,1,0:T(8,128)(2,1)S(1)} %get-tuple-element.12), channel_id=1, source_target_pairs={{0,12},{1,13},{4,8},{5,9},{8,4},{9,5},{12,0},{13,1},{2,14},{3,15},... | collective-permute-start | bytes 294920 | tf_op jit(solution)/shard_map/ppermute | solution.py:102
  97.3 7.2 %copy-start.4 = (bf16[1,64,768]{2,1,0:T(8,128)(2,1)}, bf16[1,64,768]{2,1,0:T(8,128)(2,1)S(1)}, u32[]{:S(2)}) copy-start(bf16[1,64,768]{2,1,0:T(8,128)(2,1)S(1)} %collective-permute-done.13.refs_3_) | copy-start | bytes 294916
  97.3 7.1 %collective-permute-start.17 = (bf16[1,64,768]{2,1,0:T(8,128)(2,1)S(1)}, bf16[1,64,768]{2,1,0:T(8,128)(2,1)S(1)}, u32[]{:S(2)}, u32[]{:S(2)}) collective-permute-start(bf16[1,64,768]{2,1,0:T(8,128)(2,1)S(1)} %get-tuple-element.11), channel_id=1, source_target_pairs={{0,13},{1,12},{4,9},{5,8},{8,5},{9,4},{12,1},{13,0},{2,15},{3,14},... | collective-permute-start | bytes 294920 | tf_op jit(solution)/shard_map/ppermute | solution.py:102
  99.1 5.4 %copy-start.5 = (bf16[1,64,768]{2,1,0:T(8,128)(2,1)}, bf16[1,64,768]{2,1,0:T(8,128)(2,1)S(1)}, u32[]{:S(2)}) copy-start(bf16[1,64,768]{2,1,0:T(8,128)(2,1)S(1)} %collective-permute-done.14.refs_4_) | copy-start | bytes 294916
  100.6 3.9 %copy-start.6 = (bf16[1,64,768]{2,1,0:T(8,128)(2,1)}, bf16[1,64,768]{2,1,0:T(8,128)(2,1)S(1)}, u32[]{:S(2)}) copy-start(bf16[1,64,768]{2,1,0:T(8,128)(2,1)S(1)} %collective-permute-done.15.refs_5_) | copy-start | bytes 294916
  109.8 11.4 %all-to-all-start.1 = ((bf16[8,64,512]{2,1,0:T(8,128)(2,1)}), bf16[8,64,512]{2,1,0:T(8,128)(2,1)S(1)}, u32[]{:S(2)}, u32[]{:S(2)}) async-start(bf16[8,64,512]{2,1,0:T(8,128)(2,1)} %bitcast.22), calls=%async_computation.1 | async-start | bytes 1048576 | tf_op jit(solution)/shard_map/all_to_all | solution.py:35
  113.4 1.2 collective-permute-start.18
  121.4 4.7 %collective-permute-start.19 = (bf16[16,512]{1,0:T(8,128)(2,1)S(1)}, bf16[16,512]{1,0:T(8,128)(2,1)S(1)}, u32[]{:S(2)}, u32[]{:S(2)}) collective-permute-start(bf16[16,512]{1,0:T(8,128)(2,1)S(1)} %get-tuple-element.24), channel_id=1, source_target_pairs={{0,16},{16,0},{1,17},{17,1},{2,18},{18,2},{3,19},{19,3},{4,20},{20... | collective-permute-start | bytes 49160 | tf_op jit(solution)/shard_map/ppermute | solution.py:150
  122.3 3.9 %collective-permute-start.20 = (bf16[16,512]{1,0:T(8,128)(2,1)S(1)}, bf16[16,512]{1,0:T(8,128)(2,1)S(1)}, u32[]{:S(2)}, u32[]{:S(2)}) collective-permute-start(bf16[16,512]{1,0:T(8,128)(2,1)S(1)} %get-tuple-element.25), channel_id=1, source_target_pairs={{0,2},{2,0},{1,3},{3,1},{4,6},{6,4},{5,7},{7,5},{8,10},{10,8},{9,1... | collective-permute-start | bytes 49160 | tf_op jit(solution)/shard_map/ppermute | solution.py:152
  122.3 4.1 %collective-permute-start.21 = (bf16[16,512]{1,0:T(8,128)(2,1)S(1)}, bf16[16,512]{1,0:T(8,128)(2,1)S(1)}, u32[]{:S(2)}, u32[]{:S(2)}) collective-permute-start(bf16[16,512]{1,0:T(8,128)(2,1)S(1)} %get-tuple-element.26), channel_id=1, source_target_pairs={{0,18},{2,16},{16,2},{18,0},{1,19},{3,17},{17,3},{19,1},{4,22},{6,... | collective-permute-start | bytes 49160 | tf_op jit(solution)/shard_map/ppermute | solution.py:151
  (7 other events, 6.6 us)

commit v5 on v3

--- a/solution.py
+++ b/solution.py
@@ -1,16 +1,16 @@
+import functools
+
 import jax
 import jax.numpy as jnp
 from jax import lax
+from jax.experimental import pallas as pl
+from jax.experimental.pallas import tpu as pltpu
 from jax.sharding import Mesh, PartitionSpec as P
 
 SWAP = [(0, 1), (1, 0)]
+PACK_STEPS = 4
+LIMIT = 61 * 2**20
 CROSS = [(0, 3), (1, 2), (2, 1), (3, 0)]
-
-
-def normalize(tokens, norm_gain):
-    values = tokens.astype(jnp.float32)
-    mean_square = jnp.mean(values * values, axis=1, keepdims=True)
-    return (values * lax.rsqrt(mean_square + 1e-06) * norm_gain[None, :]).astype(jnp.bfloat16)
 
 
 def in_order(bit, near, far, axis):
@@ -28,8 +28,144 @@
     return jnp.sum(jnp.where(chosen[:, :, None] == numbers[None, None, :], weights, 0.0), axis=1)
 
 
+def assemble_kernel(group, half, mine, other, out):
+    cores, _, columns = mine.shape
+
+    def write(first, second):
+        for i, side in enumerate((first, second)):
+            for g in range(columns // group):
+                for j in range(cores):
+                    start = ((i * (columns // group) + g) * cores + j) * group
+                    out[:, start : start + group] = side[j, :, g * group : (g + 1) * group]
+
+    @pl.when(half[0] == 0)
+    def _():
+        write(mine, other)
+
+    @pl.when(half[0] != 0)
+    def _():
+        write(other, mine)
+
+
+def assemble(half, mine, other, group):
+    cores, rows, columns = mine.shape
+    vmem = pl.BlockSpec(memory_space=pltpu.VMEM)
+    return pl.pallas_call(
+        functools.partial(assemble_kernel, group),
+        name="assemble",
+        in_specs=[pl.BlockSpec(memory_space=pltpu.SMEM), vmem, vmem],
+        out_specs=vmem,
+        out_shape=jax.ShapeDtypeStruct((rows, 2 * cores * columns), mine.dtype),
+        compiler_params=pltpu.CompilerParams(vmem_limit_bytes=2**20),
+    )(half.reshape(1).astype(jnp.int32), mine, other)
+
+
 def exchange(value, axes):
     return lax.all_to_all(value, axes, 0, 0, tiled=True)
+
+
+def prepare_kernel(groups, core, plane, all_tokens, all_gain, weights, keep, give, packed, *refs):
+    *blocks, tokens, gain, first, ready = refs
+    loads = [
+        pltpu.make_async_copy(all_tokens, tokens, first.at[0]),
+        pltpu.make_async_copy(all_gain, gain, first.at[1]),
+    ]
+    for load in loads:
+        load.start()
+    experts, _, packed_width = weights.shape
+    hidden_units = packed_width // 3
+    part, places = hidden_units // 2, len(blocks)
+    copies = []
+
+    def copy(source, target):
+        copies.append(pltpu.make_async_copy(source, target, ready.at[len(copies)]))
+        copies[-1].start()
+
+    size = experts // PACK_STEPS
+    for k in range(PACK_STEPS):
+        some = pl.ds(k * size, size)
+        for i in range(2):
+            for j in range(2):
+                source = weights.at[some, :, pl.ds(j * hidden_units + i * part, part)]
+                copy(source, packed.at[i, some, :, pl.ds(j * part, part)])
+    for step, block in enumerate(blocks):
+        for level in range(experts // places):
+            expert = level * places + (plane[0] ^ step)
+            copy(weights.at[expert, :, pl.ds(2 * hidden_units, hidden_units)], block.at[level])
+
+    for load in loads:
+        load.wait()
+    values = tokens[...].astype(jnp.float32)
+    mean_square = jnp.mean(values * values, axis=1, keepdims=True)
+    normed = (values * lax.rsqrt(mean_square + 1e-06) * gain[...]).astype(keep.dtype)
+    group = normed.shape[1] // 2 // groups
+
+    def split(first, second):
+        for g in range(groups):
+            at = slice(g * group, (g + 1) * group)
+            first[:, at] = normed[:, 2 * g * group : (2 * g + 1) * group]
+            second[:, at] = normed[:, (2 * g + 1) * group : (2 * g + 2) * group]
+
+    @pl.when(core[0] == 0)
+    def _():
+        split(keep, give)
+
+    @pl.when(core[0] != 0)
+    def _():
+        split(give, keep)
+
+    for started in copies:
+        started.wait()
+
+
+def prepare(core, plane, tokens, gain, weights, groups):
+    experts, rows, packed_width = weights.shape
+    count, width = tokens.shape
+    hidden_units = packed_width // 3
+    places = experts // 2
+    scalar, vmem = pl.BlockSpec(memory_space=pltpu.SMEM), pl.BlockSpec(memory_space=pltpu.VMEM)
+    hbm = pl.BlockSpec(memory_space=pltpu.HBM)
+    columns = jax.ShapeDtypeStruct((count, width // 2), tokens.dtype)
+    block = jax.ShapeDtypeStruct((2, rows, hidden_units), weights.dtype)
+    packed = jax.ShapeDtypeStruct((2, experts, rows, hidden_units), weights.dtype)
+    return pl.pallas_call(
+        functools.partial(prepare_kernel, groups),
+        name="prepare",
+        in_specs=[scalar, scalar, hbm, hbm, hbm],
+        out_specs=[vmem] * (3 + places),
+        out_shape=[columns, columns, packed] + [block] * places,
+        scratch_shapes=[
+            pltpu.VMEM((count, width), tokens.dtype),
+            pltpu.VMEM((1, width), gain.dtype),
+            pltpu.SemaphoreType.DMA((2,)),
+            pltpu.SemaphoreType.DMA((4 * PACK_STEPS + experts,)),
+        ],
+        compiler_params=pltpu.CompilerParams(vmem_limit_bytes=LIMIT),
+    )(core.reshape(1), plane.reshape(1), tokens, gain.reshape(1, width), weights)
+
+
+def gather_kernel(level, plane, kept, arrived, out, ready):
+    copies = []
+    for i, blocks in enumerate((kept, arrived)):
+        for step in range(blocks.shape[0]):
+            target = out.at[level[0] ^ i, plane[0] ^ step]
+            copies.append(pltpu.make_async_copy(blocks.at[step], target, ready.at[i, step]))
+            copies[-1].start()
+    for copy in copies:
+        copy.wait()
+
+
+def gather_blocks(level, plane, kept, arrived):
+    scalar, hbm = pl.BlockSpec(memory_space=pltpu.SMEM), pl.BlockSpec(memory_space=pltpu.HBM)
+    return pl.pallas_call(
+        gather_kernel,
+        name="gather_blocks",
+        in_specs=[scalar, scalar, hbm, hbm],
+        out_specs=pl.BlockSpec(memory_space=pltpu.VMEM),
+        out_shape=jax.ShapeDtypeStruct((2,) + kept.shape, kept.dtype),
+        scratch_shapes=[pltpu.SemaphoreType.DMA((2, kept.shape[0]))],
+        compiler_params=pltpu.CompilerParams(vmem_limit_bytes=2**21),
+    )(level.reshape(1), plane.reshape(1), kept, arrived)
 
 
 def dense_layer(tokens, norm_gain, expert_weights, slot_expert, pair_slots, combine_weights):
@@ -40,57 +176,57 @@
     chip_axes = ("z", "y", "x")
     chips = experts
     h, c = lax.axis_index("h"), lax.axis_index("c")
-    chip = lax.axis_index(chip_axes)
     group = lax.axis_size("x") * own_rows
     groups = width // (2 * group)
 
-    gate, up, own_down = (expert_weights[:, :, i * hidden_units :][:, :, :hidden_units] for i in range(3))
-    blocks = [
-        jnp.concatenate([gate[:, :, i * part :][:, :, :part], up[:, :, i * part :][:, :, :part]], axis=2)
-        for i in range(2)
-    ]
-    gate_up = exchange(jnp.concatenate(blocks), ("h",) + chip_axes)
+    z, plane = lax.axis_index("z"), lax.axis_index(("y", "x"))
+    places = chips // 2
+    keep, give, packed, *blocks = prepare(c, plane, tokens, norm_gain, expert_weights, groups)
+    gate_up = exchange(packed.reshape(2 * experts, own_rows, 2 * part), ("h",) + chip_axes)
     gate_up = gate_up.reshape(width // 2, 2 * part)
-    down = exchange(own_down, chip_axes).reshape(width // 4, hidden_units)
-
-    normed = normalize(tokens, norm_gain)
-    columns = [
-        jnp.concatenate([normed[:, (2 * g + j) * group :][:, :group] for g in range(groups)], axis=1)
-        for j in range(2)
-    ]
-    keep = jnp.where(c == 0, columns[0], columns[1])
-    give = jnp.where(c == 0, columns[1], columns[0])
+
+    for step in range(1, places):
+        pairs = [(i, i ^ step) for i in range(places)]
+        blocks[step] = lax.ppermute(blocks[step], ("y", "x"), pairs)
+    kept = jnp.stack([lax.dynamic_index_in_dim(block, z, 0, keepdims=False) for block in blocks])
+    passed = jnp.stack([lax.dynamic_index_in_dim(block, 1 - z, 0, keepdims=False) for block in blocks])
+    down = gather_blocks(z, plane, kept, lax.ppermute(passed, "z", SWAP))
+    down = down.reshape(width // 4, hidden_units)
+
     from_c = lax.ppermute(give, "c", SWAP)
     from_h = lax.ppermute(keep, "h", SWAP)
     from_hc = lax.ppermute(give, ("h", "c"), CROSS)
-    near = jnp.concatenate(
-        [in_order(h, keep[None], from_h[None], 0), in_order(h, from_c[None], from_hc[None], 0)]
-    )
-    rows = jnp.zeros((4, chips * token_count, width // 2), near.dtype)
-    rows = lax.dynamic_update_slice(rows, near, (0, chip * token_count, 0))
-    for step in range(1, chips):
-        pairs = [(i, i ^ step) for i in range(chips)]
-        arrived = lax.ppermute(near, chip_axes, pairs)
-        rows = lax.dynamic_update_slice(rows, arrived, (0, (chip ^ step) * token_count, 0))
-    count = 2 * chips * token_count
-    rows = rows.reshape(2, count, width // 2)
-
-    other = jnp.dot(rows[1], gate_up, preferred_element_type=jnp.float32).astype(jnp.bfloat16)
+    near = jnp.stack([in_order(h, keep, from_h, 0), in_order(h, from_c, from_hc, 0)])
+    column = in_order(z, near[:, None], lax.ppermute(near, "z", SWAP)[:, None], 1)
+    rows = jnp.zeros((2, 2, chips // 2, 2 * token_count, width // 2), near.dtype)
+    rows = lax.dynamic_update_slice(rows, column[:, :, None], (0, 0, plane, 0, 0))
+    for step in range(1, chips // 2):
+        pairs = [(i, i ^ step) for i in range(chips // 2)]
+        arrived = lax.ppermute(column, ("y", "x"), pairs)
+        rows = lax.dynamic_update_slice(rows, arrived[:, :, None], (0, 0, plane ^ step, 0, 0))
+    count = chips * token_count
+    rows = rows.reshape(2, 1, 2 * count, width // 2)
+
+    other = jnp.dot(rows[1, 0], gate_up, preferred_element_type=jnp.float32).astype(jnp.bfloat16)
     arrived = lax.ppermute(other, "c", SWAP)
-    pre = jnp.dot(rows[0], gate_up, preferred_element_type=jnp.float32) + arrived.astype(jnp.float32)
+    pre = jnp.dot(rows[0, 0], gate_up, preferred_element_type=jnp.float32) + arrived.astype(jnp.float32)
     hidden = (jax.nn.silu(pre[:, :part]) * pre[:, part:]).astype(jnp.bfloat16)
-    hidden = in_order(h, hidden, lax.ppermute(hidden, "h", SWAP), 1)
+    far = lax.ppermute(hidden, "h", SWAP)
+    coefficient = slot_coefficients(slot_expert, pair_slots, combine_weights, experts).T
+    far_weights = lax.ppermute(coefficient, "h", SWAP)
+    far, far_weights = lax.optimization_barrier((far, far_weights))
+    coefficient = in_order(h, coefficient, far_weights, 1)
+    hidden = in_order(h, hidden, far, 1)
     hidden = in_order(c, hidden, lax.ppermute(hidden, "c", SWAP), 0)
+    hidden = lax.optimization_barrier(hidden)
     result = lax.dot_general(hidden, down, (((1,), (1,)), ((), ())), preferred_element_type=jnp.float32)
-    result = result.astype(jnp.bfloat16).reshape(4 * chips, token_count, width // 4)
-    returned = exchange(result, ("c", "h") + chip_axes)
-    returned = returned.reshape(2, 2, chips, token_count, width // 4).astype(jnp.float32)
-    coefficient = slot_coefficients(slot_expert, pair_slots, combine_weights, experts)
-    mixed = jnp.sum(returned * coefficient.T[None, None, :, :, None], axis=2).astype(jnp.bfloat16)
-    spans = [
-        mixed[j, i, :, g * group : (g + 1) * group] for i in range(2) for g in range(groups // 2) for j in range(2)
-    ]
-    return jnp.concatenate(spans, axis=1)
+    result = result.astype(jnp.bfloat16).reshape(2 * chips, 2 * token_count, width // 4)
+    returned = exchange(result, ("c",) + chip_axes).astype(jnp.float32)
+    returned = returned.reshape(2, chips, 2 * token_count, width // 4)
+    mixed = jnp.sum(returned * coefficient[None, :, :, None], axis=1).astype(jnp.bfloat16)
+    low, high = mixed[:, :token_count], mixed[:, token_count:]
+    mine, sent = jnp.where(h == 0, low, high), jnp.where(h == 0, high, low)
+    return assemble(h, mine, lax.ppermute(sent, "h", SWAP), group)
 
 
 def per_device(tokens, norm_gain, expert_weights, slot_expert, pair_slots, combine_weights):

time: 110 us -> 126 us (1.15)
  waiting for transfers between devices: 59.9 us -> 87.1 us
  starting transfers between devices: 34.7 us -> 27.8 us
  local copies, waits for them, and re-layouts: 6.45 us -> 0.51 us
  Pallas kernels: 0 us -> 5.16 us
  other arithmetic: 4.1 us -> 1.44 us
    ppermute x1, waiting for transfers between devices: 0.01 us -> 34.9 us  [dense_layer(): from_hc = lax.ppermute(give, ('h', 'c'), CROSS)]
    all_to_all x3 -> x2, waiting for transfers between devices: 18.3 us -> 9.69 us  [exchange(): return lax.all_to_all(value, axes, 0, 0, tiled=True)]
    all_to_all x3 -> x2, starting transfers between devices: 18.1 us -> 12.1 us  [exchange(): return lax.all_to_all(value, axes, 0, 0, tiled=True)]
    pallas_call x0 -> x3, Pallas kernels: none -> 5.16 us  [the longest x1 3.4 us: prepare(): pl.pallas_call(functools.partial(prepare_kernel, groups), name='prepare',...]
    slice x3 -> x1, local copies, waits for them, and re-layouts: 4.5 us -> 0.09 us  [dense_layer(): rows[1, 0]]
    ppermute x1, starting transfers between devices: 3.69 us -> 1.76 us  [dense_layer(): from_hc = lax.ppermute(give, ('h', 'c'), CROSS)]
    ppermute x1, waiting for transfers between devices: 0.01 us -> 1.68 us  [dense_layer(): from_h = lax.ppermute(keep, 'h', SWAP)]
    concatenate x2 -> x0, other arithmetic: 1.34 us -> none  [the longest x1 1.32 us: dense_layer(): gate_up = exchange(jnp.concatenate(blocks), ('h',) + chip_axes)]
  transfers between devices with their start and end apart: 16 -> 18, of which waited for: 9 -> 10; matrix products, arithmetic and copies ran while one was open for 7% -> 3% of each run, Pallas kernels for 0% -> 1%
where the time goes in v5:
time: 126 us
  waiting for transfers between devices  87.1 us (69%)
  starting transfers between devices  27.8 us (22%)
  Pallas kernels  5.16 us (4%)
  matrix products  3.29 us (3%)
  other arithmetic  1.44 us (1%)
    ppermute x1, waiting for transfers between devices, dense_layer(): from_hc = lax.ppermute(give, ('h', 'c'), CROSS)  34.9 us
    ppermute x3, waiting for transfers between devices, dense_layer(): arrived = lax.ppermute(column, ('y', 'x'), pairs)  13.1 us
    all_to_all x2, starting transfers between devices, exchange(): return lax.all_to_all(value, axes, 0, 0, tiled=True)  12.1 us
    all_to_all x2, waiting for transfers between devices, exchange(): return lax.all_to_all(value, axes, 0, 0, tiled=True)  9.69 us
    ppermute x1, waiting for transfers between devices, dense_layer(): far = lax.ppermute(hidden, 'h', SWAP)  8.15 us
    ppermute x3, waiting for transfers between devices, dense_layer(): blocks[step] = lax.ppermute(blocks[step], ('y', 'x'), pairs)  5.81 us
    ppermute x1, waiting for transfers between devices, dense_layer(): lax.ppermute(near, 'z', SWAP)[:, None]  4.95 us
    ppermute x1, waiting for transfers between devices, dense_layer(): down = gather_blocks(z, plane, kept, lax.ppermute(passed, 'z', SWAP))  4.49 us
  transfers between devices with their start and end apart: 18, of which 10 were waited for; matrix products, arithmetic and copies ran while one was open for 3% of the time, Pallas kernels for 1%

profile of v5, /device:TPU:0, one launch (start us, length us, event | category | flops | bytes accessed | tf_op | source)
XLA Modules:
  0.0 125.6 jit_solution(13307805327126545006)
XLA Ops:
  0.0 3.4 %prepare.1 = (bf16[16,1024]{1,0:T(8,128)(2,1)}, bf16[16,1024]{1,0:T(8,128)(2,1)}, bf16[2,8,64,768]{3,2,1,0:T(8,128)(2,1)}, bf16[2,64,768]{2,1,0:T(8,128)(2,1)}, ...) custom-call(s32[1]{0:T(128)} %bitcast.1.core, s32[1]{0:T(128)} %bitcast.2.plane, ...), custom_call_target="tpu_custom_call" | custom-call | tf_op jit(solution)/shard_map/prepare/pallas_call | solution.py:131
  3.5 8.5 %all-to-all-start = ((bf16[16,64,768]{2,1,0:T(8,128)(2,1)}), bf16[16,64,768]{2,1,0:T(8,128)(2,1)S(1)}, u32[]{:S(2)}, u32[]{:S(2)}) async-start(bf16[16,64,768]{2,1,0:T(8,128)(2,1)} %bitcast.44), calls=%async_computation | async-start | bytes 3145728 | tf_op jit(solution)/shard_map/all_to_all | solution.py:64
  12.0 1.8 %collective-permute-start.2 = (bf16[16,1024]{1,0:T(8,128)(2,1)S(1)}, bf16[16,1024]{1,0:T(8,128)(2,1)S(1)}, u32[]{:S(2)}, u32[]{:S(2)}) collective-permute-start(bf16[16,1024]{1,0:T(8,128)(2,1)S(1)} %copy-done.5), channel_id=1, source_target_pairs={{0,18},{2,16},{16,2},{18,0},{1,19},{3,17},{17,3},{19,1},{4,22},{6,... | collective-permute-start | bytes 98312 | tf_op jit(solution)/shard_map/ppermute | solution.py:198
  13.7 1.2 collective-permute-start.1
  15.1 34.9 %collective-permute-done.2 = bf16[16,1024]{1,0:T(8,128)(2,1)S(1)} collective-permute-done((bf16[16,1024]{1,0:T(8,128)(2,1)S(1)}, bf16[16,1024]{1,0:T(8,128)(2,1)S(1)}, u32[]{:S(2)}, u32[]{:S(2)}) %collective-permute-start.2) | collective-permute-done | bytes 32800 | tf_op jit(solution)/shard_map/ppermute | solution.py:198
  50.0 1.7 %collective-permute-done = bf16[16,1024]{1,0:T(8,128)(2,1)S(1)} collective-permute-done((bf16[16,1024]{1,0:T(8,128)(2,1)S(1)}, bf16[16,1024]{1,0:T(8,128)(2,1)S(1)}, u32[]{:S(2)}, u32[]{:S(2)}) %collective-permute-start) | collective-permute-done | bytes 32800 | tf_op jit(solution)/shard_map/ppermute | solution.py:197
  51.8 4.9 %collective-permute-done.3 = bf16[2,32,1024]{2,1,0:T(8,128)(2,1)S(1)} collective-permute-done((bf16[2,32,1024]{2,1,0:T(8,128)(2,1)S(1)}, bf16[2,32,1024]{2,1,0:T(8,128)(2,1)S(1)}, u32[]{:S(2)}, u32[]{:S(2)}) %collective-permute-start.3) | collective-permute-done | bytes 131104 | tf_op jit(solution)/shard_map/ppermute | solution.py:200
  56.8 1.5 %collective-permute-start.4 = (bf16[2,2,32,1024]{3,2,0,1:T(8,128)(2,1)S(1)}, bf16[2,2,32,1024]{3,2,0,1:T(8,128)(2,1)S(1)}, u32[]{:S(2)}, u32[]{:S(2)}) collective-permute-start(bf16[2,2,32,1024]{3,2,0,1:T(8,128)(2,1)S(1)} %maximum_select_fusion.3), channel_id=1, source_target_pairs={{0,1},{1,0},{4,5},{5,4},{2,3},{3,2},{6,7},{7,6},{8,9},{9,8},{12,13... | collective-permute-start | bytes 786440 | tf_op jit(solution)/shard_map/ppermute | solution.py:205
  58.3 2.5 %collective-permute-start.13 = (bf16[2,64,768]{2,1,0:T(8,128)(2,1)}, bf16[2,64,768]{2,1,0:T(8,128)(2,1)S(1)}, u32[]{:S(2)}, u32[]{:S(2)}) collective-permute-start(bf16[2,64,768]{2,1,0:T(8,128)(2,1)} %get-tuple-element.21), channel_id=1, source_target_pairs={{0,5},{1,4},{4,1},{5,0},{2,7},{3,6},{6,3},{7,2},{8,13},{9,12},{12,... | collective-permute-start | bytes 589832 | tf_op jit(solution)/shard_map/ppermute | solution.py:190
  60.9 0.4 select_reduce_fusion
  61.5 2.5 %collective-permute-start.6 = (bf16[2,2,32,1024]{3,2,0,1:T(8,128)(2,1)S(1)}, bf16[2,2,32,1024]{3,2,0,1:T(8,128)(2,1)S(1)}, u32[]{:S(2)}, u32[]{:S(2)}) collective-permute-start(bf16[2,2,32,1024]{3,2,0,1:T(8,128)(2,1)S(1)} %maximum_select_fusion.3), channel_id=1, source_target_pairs={{0,5},{1,4},{4,1},{5,0},{2,7},{3,6},{6,3},{7,2},{8,13},{9,12},{12,... | collective-permute-start | bytes 786440 | tf_op jit(solution)/shard_map/ppermute | solution.py:205
  64.2 1.9 %collective-permute-done.4 = bf16[2,2,32,1024]{3,2,0,1:T(8,128)(2,1)S(1)} collective-permute-done((bf16[2,2,32,1024]{3,2,0,1:T(8,128)(2,1)S(1)}, bf16[2,2,32,1024]{3,2,0,1:T(8,128)(2,1)S(1)}, u32[]{:S(2)}, u32[]{:S(2)}) %collective-permute-start.4) | collective-permute-done | bytes 262176 | tf_op jit(solution)/shard_map/ppermute | solution.py:205
  66.1 11.2 %collective-permute-done.5 = bf16[2,2,32,1024]{3,2,0,1:T(8,128)(2,1)S(1)} collective-permute-done((bf16[2,2,32,1024]{3,2,0,1:T(8,128)(2,1)S(1)}, bf16[2,2,32,1024]{3,2,0,1:T(8,128)(2,1)S(1)}, u32[]{:S(2)}, u32[]{:S(2)}) %collective-permute-start.5) | collective-permute-done | bytes 262176 | tf_op jit(solution)/shard_map/ppermute | solution.py:205
  77.5 1.3 %convolution_convert_fusion.1 = bf16[256,768]{1,0:T(8,128)(2,1)} fusion(bf16[256,1024]{1,0:T(8,128)(2,1)S(1)} %bitcast.47, bf16[1024,768]{1,0:T(8,128)(2,1)S(1)} %bitcast.41), kind=kOutput, calls=%fused_computation.1 | convolution fusion | flops 402849792 | bytes 2490368 | tf_op jit(solution)/shard_map/dot_general | solution.py:210
  78.9 0.4 collective-permute-start.12
  79.3 1.4 %collective-permute-start.11 = (bf16[2,64,768]{2,1,0:T(8,128)(2,1)}, bf16[2,64,768]{2,1,0:T(8,128)(2,1)S(1)}, u32[]{:S(2)}, u32[]{:S(2)}) collective-permute-start(bf16[2,64,768]{2,1,0:T(8,128)(2,1)} %get-tuple-element.19), channel_id=1, source_target_pairs={{0,1},{1,0},{4,5},{5,4},{2,3},{3,2},{6,7},{7,6},{8,9},{9,8},{12,13... | collective-permute-start | bytes 589832 | tf_op jit(solution)/shard_map/ppermute | solution.py:190
  80.7 5.8 %collective-permute-done.12 = bf16[2,64,768]{2,1,0:T(8,128)(2,1)S(1)} collective-permute-done((bf16[2,64,768]{2,1,0:T(8,128)(2,1)}, bf16[2,64,768]{2,1,0:T(8,128)(2,1)S(1)}, u32[]{:S(2)}, u32[]{:S(2)}) %collective-permute-start.12) | collective-permute-done | bytes 196640 | tf_op jit(solution)/shard_map/ppermute | solution.py:190
  86.5 0.6 convert_add_fusion
  87.1 0.1 fusion.1
  87.2 2.6 %collective-permute-start.8 = (bf16[256,384]{1,0:T(8,128)(2,1)S(1)}, bf16[256,384]{1,0:T(8,128)(2,1)S(1)}, u32[]{:S(2)}, u32[]{:S(2)}) collective-permute-start(bf16[256,384]{1,0:T(8,128)(2,1)S(1)} %fusion.1), channel_id=1, source_target_pairs={{0,16},{16,0},{1,17},{17,1},{2,18},{18,2},{3,19},{19,3},{4,20},{20... | collective-permute-start | bytes 589832 | tf_op jit(solution)/shard_map/ppermute | solution.py:214
  89.9 0.9 collective-permute-start.14
  90.8 8.2 %collective-permute-done.8 = bf16[256,384]{1,0:T(8,128)(2,1)S(1)} collective-permute-done((bf16[256,384]{1,0:T(8,128)(2,1)S(1)}, bf16[256,384]{1,0:T(8,128)(2,1)S(1)}, u32[]{:S(2)}, u32[]{:S(2)}) %collective-permute-start.8) | collective-permute-done | bytes 196640 | tf_op jit(solution)/shard_map/ppermute | solution.py:214
  99.2 4.5 %collective-permute-done.14.arrived = bf16[4,64,768]{2,1,0:T(8,128)(2,1)S(1)} collective-permute-done((bf16[4,64,768]{2,1,0:T(8,128)(2,1)S(1)}, bf16[4,64,768]{2,1,0:T(8,128)(2,1)S(1)}, u32[]{:S(2)}, u32[]{:S(2)}) %collective-permute-start.14) | collective-permute-done | bytes 393248 | tf_op jit(solution)/shard_map/ppermute | solution.py:193
  103.7 1.1 gather_blocks.1
  104.8 0.3 maximum_select_fusion
  105.1 1.4 %convolution_convert_fusion = bf16[512,512]{1,0:T(8,128)(2,1)} fusion(bf16[512,768]{1,0:T(8,128)(2,1)S(1)} %maximum_select_fusion, bf16[512,768]{1,0:T(8,128)(2,1)S(1)} %bitcast.40), kind=kOutput, calls=%fused_computation | convolution fusion | flops 402915328 | bytes 2097152 | tf_op jit(solution)/shard_map/dot_general | solution.py:222
  106.5 3.6 %all-to-all-start.1 = ((bf16[16,32,512]{2,1,0:T(8,128)(2,1)}), bf16[16,32,512]{2,1,0:T(8,128)(2,1)S(1)}, u32[]{:S(2)}, u32[]{:S(2)}) async-start(bf16[16,32,512]{2,1,0:T(8,128)(2,1)} %bitcast.22), calls=%async_computation.1 | async-start | bytes 1048576 | tf_op jit(solution)/shard_map/all_to_all | solution.py:64
  110.2 9.7 %all-to-all-done.1 = bf16[16,32,512]{2,1,0:T(8,128)(2,1)S(1)} async-done(((bf16[16,32,512]{2,1,0:T(8,128)(2,1)}), bf16[16,32,512]{2,1,0:T(8,128)(2,1)S(1)}, u32[]{:S(2)}, u32[]{:S(2)}) %all-to-all-start.1) | async-done | bytes 524320 | tf_op jit(solution)/shard_map/all_to_all | solution.py:64
  119.9 0.2 fusion
  120.1 0.6 collective-permute-start.15
  120.7 4.3 %collective-permute-done.15.other = bf16[2,16,512]{2,1,0:T(8,128)(2,1)S(1)} collective-permute-done((bf16[2,16,512]{2,1,0:T(8,128)(2,1)S(1)}, bf16[2,16,512]{2,1,0:T(8,128)(2,1)S(1)}, u32[]{:S(2)}, u32[]{:S(2)}) %collective-permute-start.15) | collective-permute-done | bytes 32800 | tf_op jit(solution)/shard_map/ppermute | solution.py:229
  125.0 0.6 assemble.1
  (48 shorter events, 1.3 us)
Async XLA Ops:
  3.4 8.5 %copy-start.5 = (bf16[16,1024]{1,0:T(8,128)(2,1)S(1)}, bf16[16,1024]{1,0:T(8,128)(2,1)}, u32[]{:S(2)}) copy-start(bf16[16,1024]{1,0:T(8,128)(2,1)} %get-tuple-element.15) | copy-start | bytes 98308
  3.4 11.5 %copy-start.1 = (bf16[16,1024]{1,0:T(8,128)(2,1)S(1)}, bf16[16,1024]{1,0:T(8,128)(2,1)}, u32[]{:S(2)}) copy-start(bf16[16,1024]{1,0:T(8,128)(2,1)} %get-tuple-element.14) | copy-start | bytes 98308
  3.4 57.4 %copy-start.2 = (s32[16,8]{0,1:T(8,128)S(1)}, s32[16,8]{0,1:T(8,128)}, u32[]{:S(2)}) copy-start(s32[16,8]{0,1:T(8,128)} %param.10) | copy-start | bytes 1540
  3.4 57.5 %copy-start.4 = (s32[16]{0:T(128)S(1)}, s32[16]{0:T(128)}, u32[]{:S(2)}) copy-start(s32[16]{0:T(128)} %param.9) | copy-start | bytes 196
  3.5 74.0 %all-to-all-start = ((bf16[16,64,768]{2,1,0:T(8,128)(2,1)}), bf16[16,64,768]{2,1,0:T(8,128)(2,1)S(1)}, u32[]{:S(2)}, u32[]{:S(2)}) async-start(bf16[16,64,768]{2,1,0:T(8,128)(2,1)} %bitcast.44), calls=%async_computation | async-start | bytes 3145728 | tf_op jit(solution)/shard_map/all_to_all | solution.py:64
  12.0 38.0 %collective-permute-start.2 = (bf16[16,1024]{1,0:T(8,128)(2,1)S(1)}, bf16[16,1024]{1,0:T(8,128)(2,1)S(1)}, u32[]{:S(2)}, u32[]{:S(2)}) collective-permute-start(bf16[16,1024]{1,0:T(8,128)(2,1)S(1)} %copy-done.5), channel_id=1, source_target_pairs={{0,18},{2,16},{16,2},{18,0},{1,19},{3,17},{17,3},{19,1},{4,22},{6,... | collective-permute-start | bytes 98312 | tf_op jit(solution)/shard_map/ppermute | solution.py:198
  13.7 36.3 %collective-permute-start.1 = (bf16[16,1024]{1,0:T(8,128)(2,1)S(1)}, bf16[16,1024]{1,0:T(8,128)(2,1)S(1)}, u32[]{:S(2)}, u32[]{:S(2)}) collective-permute-start(bf16[16,1024]{1,0:T(8,128)(2,1)S(1)} %copy-done.5), channel_id=1, source_target_pairs={{0,2},{2,0},{1,3},{3,1},{4,6},{6,4},{5,7},{7,5},{8,10},{10,8},{9,1... | collective-permute-start | bytes 98312 | tf_op jit(solution)/shard_map/ppermute | solution.py:196
  15.0 36.7 %collective-permute-start = (bf16[16,1024]{1,0:T(8,128)(2,1)S(1)}, bf16[16,1024]{1,0:T(8,128)(2,1)S(1)}, u32[]{:S(2)}, u32[]{:S(2)}) collective-permute-start(bf16[16,1024]{1,0:T(8,128)(2,1)S(1)} %copy-done.1), channel_id=1, source_target_pairs={{0,16},{16,0},{1,17},{17,1},{2,18},{18,2},{3,19},{19,3},{4,20},{20... | collective-permute-start | bytes 98312 | tf_op jit(solution)/shard_map/ppermute | solution.py:197
  51.7 5.0 %collective-permute-start.3 = (bf16[2,32,1024]{2,1,0:T(8,128)(2,1)S(1)}, bf16[2,32,1024]{2,1,0:T(8,128)(2,1)S(1)}, u32[]{:S(2)}, u32[]{:S(2)}) collective-permute-start(bf16[2,32,1024]{2,1,0:T(8,128)(2,1)S(1)} %get-tuple-element.35), channel_id=1, source_target_pairs={{0,8},{8,0},{1,9},{9,1},{2,10},{10,2},{3,11},{11,3},{4,12},{12,4},... | collective-permute-start | bytes 393224 | tf_op jit(solution)/shard_map/ppermute | solution.py:200
  56.8 9.2 %collective-permute-start.4 = (bf16[2,2,32,1024]{3,2,0,1:T(8,128)(2,1)S(1)}, bf16[2,2,32,1024]{3,2,0,1:T(8,128)(2,1)S(1)}, u32[]{:S(2)}, u32[]{:S(2)}) collective-permute-start(bf16[2,2,32,1024]{3,2,0,1:T(8,128)(2,1)S(1)} %maximum_select_fusion.3), channel_id=1, source_target_pairs={{0,1},{1,0},{4,5},{5,4},{2,3},{3,2},{6,7},{7,6},{8,9},{9,8},{12,13... | collective-permute-start | bytes 786440 | tf_op jit(solution)/shard_map/ppermute | solution.py:205
  58.3 22.3 %collective-permute-start.13 = (bf16[2,64,768]{2,1,0:T(8,128)(2,1)}, bf16[2,64,768]{2,1,0:T(8,128)(2,1)S(1)}, u32[]{:S(2)}, u32[]{:S(2)}) collective-permute-start(bf16[2,64,768]{2,1,0:T(8,128)(2,1)} %get-tuple-element.21), channel_id=1, source_target_pairs={{0,5},{1,4},{4,1},{5,0},{2,7},{3,6},{6,3},{7,2},{8,13},{9,12},{12,... | collective-permute-start | bytes 589832 | tf_op jit(solution)/shard_map/ppermute | solution.py:190
  61.4 15.9 %collective-permute-start.5 = (bf16[2,2,32,1024]{3,2,0,1:T(8,128)(2,1)S(1)}, bf16[2,2,32,1024]{3,2,0,1:T(8,128)(2,1)S(1)}, u32[]{:S(2)}, u32[]{:S(2)}) collective-permute-start(bf16[2,2,32,1024]{3,2,0,1:T(8,128)(2,1)S(1)} %maximum_select_fusion.3), channel_id=1, source_target_pairs={{0,4},{1,5},{4,0},{5,1},{2,6},{3,7},{6,2},{7,3},{8,12},{9,13},{12,... | collective-permute-start | bytes 786440 | tf_op jit(solution)/shard_map/ppermute | solution.py:205
  61.5 15.9 %collective-permute-start.6 = (bf16[2,2,32,1024]{3,2,0,1:T(8,128)(2,1)S(1)}, bf16[2,2,32,1024]{3,2,0,1:T(8,128)(2,1)S(1)}, u32[]{:S(2)}, u32[]{:S(2)}) collective-permute-start(bf16[2,2,32,1024]{3,2,0,1:T(8,128)(2,1)S(1)} %maximum_select_fusion.3), channel_id=1, source_target_pairs={{0,5},{1,4},{4,1},{5,0},{2,7},{3,6},{6,3},{7,2},{8,13},{9,12},{12,... | collective-permute-start | bytes 786440 | tf_op jit(solution)/shard_map/ppermute | solution.py:205
  77.5 1.3 %copy-start.3 = (f32[16,8]{0,1:T(8,128)S(1)}, f32[16,8]{0,1:T(8,128)}, u32[]{:S(2)}) copy-start(f32[16,8]{0,1:T(8,128)} %param.11) | copy-start | bytes 1540
  77.5 3.2 %copy-start = (bf16[2,64,768]{2,1,0:T(8,128)(2,1)S(1)}, bf16[2,64,768]{2,1,0:T(8,128)(2,1)}, u32[]{:S(2)}) copy-start(bf16[2,64,768]{2,1,0:T(8,128)(2,1)} %get-tuple-element.18) | copy-start | bytes 589828
  78.8 7.7 %collective-permute-start.7 = (bf16[256,768]{1,0:T(8,128)(2,1)}, bf16[256,768]{1,0:T(8,128)(2,1)S(1)}, u32[]{:S(2)}, u32[]{:S(2)}) collective-permute-start(bf16[256,768]{1,0:T(8,128)(2,1)} %convolution_convert_fusion.1), channel_id=1, source_target_pairs={{0,2},{2,0},{1,3},{3,1},{4,6},{6,4},{5,7},{7,5},{8,10},{10,8},{9,1... | collective-permute-start | bytes 1179656 | tf_op jit(solution)/shard_map/ppermute | solution.py:211
  78.8 12.0 %collective-permute-start.9 = (f32[8,16]{1,0:T(8,128)S(1)}, f32[8,16]{1,0:T(8,128)S(1)}, u32[]{:S(2)}, u32[]{:S(2)}) collective-permute-start(f32[8,16]{1,0:T(8,128)S(1)} %bitcast.52), channel_id=1, source_target_pairs={{0,16},{16,0},{1,17},{17,1},{2,18},{18,2},{3,19},{19,3},{4,20},{20... | collective-permute-start | bytes 1544 | tf_op jit(solution)/shard_map/ppermute | solution.py:216
  78.9 7.6 %collective-permute-start.12 = (bf16[2,64,768]{2,1,0:T(8,128)(2,1)}, bf16[2,64,768]{2,1,0:T(8,128)(2,1)S(1)}, u32[]{:S(2)}, u32[]{:S(2)}) collective-permute-start(bf16[2,64,768]{2,1,0:T(8,128)(2,1)} %get-tuple-element.20), channel_id=1, source_target_pairs={{0,4},{1,5},{4,0},{5,1},{2,6},{3,7},{6,2},{7,3},{8,12},{9,13},{12,... | collective-permute-start | bytes 589832 | tf_op jit(solution)/shard_map/ppermute | solution.py:190
  79.3 10.6 %collective-permute-start.11 = (bf16[2,64,768]{2,1,0:T(8,128)(2,1)}, bf16[2,64,768]{2,1,0:T(8,128)(2,1)S(1)}, u32[]{:S(2)}, u32[]{:S(2)}) collective-permute-start(bf16[2,64,768]{2,1,0:T(8,128)(2,1)} %get-tuple-element.19), channel_id=1, source_target_pairs={{0,1},{1,0},{4,5},{5,4},{2,3},{3,2},{6,7},{7,6},{8,9},{9,8},{12,13... | collective-permute-start | bytes 589832 | tf_op jit(solution)/shard_map/ppermute | solution.py:190
  87.2 11.7 %collective-permute-start.8 = (bf16[256,384]{1,0:T(8,128)(2,1)S(1)}, bf16[256,384]{1,0:T(8,128)(2,1)S(1)}, u32[]{:S(2)}, u32[]{:S(2)}) collective-permute-start(bf16[256,384]{1,0:T(8,128)(2,1)S(1)} %fusion.1), channel_id=1, source_target_pairs={{0,16},{16,0},{1,17},{17,1},{2,18},{18,2},{3,19},{19,3},{4,20},{20... | collective-permute-start | bytes 589832 | tf_op jit(solution)/shard_map/ppermute | solution.py:214
  89.9 13.7 %collective-permute-start.14 = (bf16[4,64,768]{2,1,0:T(8,128)(2,1)S(1)}, bf16[4,64,768]{2,1,0:T(8,128)(2,1)S(1)}, u32[]{:S(2)}, u32[]{:S(2)}) collective-permute-start(bf16[4,64,768]{2,1,0:T(8,128)(2,1)S(1)} %pad_maximum_fusion.1), channel_id=1, source_target_pairs={{0,8},{8,0},{1,9},{9,1},{2,10},{10,2},{3,11},{11,3},{4,12},{12,4},... | collective-permute-start | bytes 1179656 | tf_op jit(solution)/shard_map/ppermute | solution.py:193
  99.1 5.8 %collective-permute-start.10 = (bf16[256,768]{1,0:T(8,128)(2,1)S(1)}, bf16[256,768]{1,0:T(8,128)(2,1)S(1)}, u32[]{:S(2)}, u32[]{:S(2)}) collective-permute-start(bf16[256,768]{1,0:T(8,128)(2,1)S(1)} %maximum_select_fusion.1), channel_id=1, source_target_pairs={{0,2},{2,0},{1,3},{3,1},{4,6},{6,4},{5,7},{7,5},{8,10},{10,8},{9,1... | collective-permute-start | bytes 1179656 | tf_op jit(solution)/shard_map/ppermute | solution.py:220
  106.5 13.3 %all-to-all-start.1 = ((bf16[16,32,512]{2,1,0:T(8,128)(2,1)}), bf16[16,32,512]{2,1,0:T(8,128)(2,1)S(1)}, u32[]{:S(2)}, u32[]{:S(2)}) async-start(bf16[16,32,512]{2,1,0:T(8,128)(2,1)} %bitcast.22), calls=%async_computation.1 | async-start | bytes 1048576 | tf_op jit(solution)/shard_map/all_to_all | solution.py:64
  120.1 4.9 %collective-permute-start.15 = (bf16[2,16,512]{2,1,0:T(8,128)(2,1)S(1)}, bf16[2,16,512]{2,1,0:T(8,128)(2,1)S(1)}, u32[]{:S(2)}, u32[]{:S(2)}) collective-permute-start(bf16[2,16,512]{2,1,0:T(8,128)(2,1)S(1)} %get-tuple-element.36), channel_id=1, source_target_pairs={{0,16},{16,0},{1,17},{17,1},{2,18},{18,2},{3,19},{19,3},{4,20},{20... | collective-permute-start | bytes 98312 | tf_op jit(solution)/shard_map/ppermute | solution.py:229

commit v6 on v5

--- a/solution.py
+++ b/solution.py
@@ -28,50 +28,32 @@
     return jnp.sum(jnp.where(chosen[:, :, None] == numbers[None, None, :], weights, 0.0), axis=1)
 
 
-def assemble_kernel(group, half, mine, other, out):
-    cores, _, columns = mine.shape
-
-    def write(first, second):
-        for i, side in enumerate((first, second)):
-            for g in range(columns // group):
-                for j in range(cores):
-                    start = ((i * (columns // group) + g) * cores + j) * group
-                    out[:, start : start + group] = side[j, :, g * group : (g + 1) * group]
-
-    @pl.when(half[0] == 0)
-    def _():
-        write(mine, other)
-
-    @pl.when(half[0] != 0)
-    def _():
-        write(other, mine)
-
-
-def assemble(half, mine, other, group):
-    cores, rows, columns = mine.shape
+def assemble_kernel(half, mine, other, out):
+    columns = mine.shape[1]
+    own = pl.multiple_of(half[0] * columns, columns)
+    out[:, pl.ds(own, columns)] = mine[...]
+    out[:, pl.ds(columns - own, columns)] = other[...]
+
+
+def assemble(half, mine, other):
+    rows, columns = mine.shape
     vmem = pl.BlockSpec(memory_space=pltpu.VMEM)
     return pl.pallas_call(
-        functools.partial(assemble_kernel, group),
+        assemble_kernel,
         name="assemble",
         in_specs=[pl.BlockSpec(memory_space=pltpu.SMEM), vmem, vmem],
         out_specs=vmem,
-        out_shape=jax.ShapeDtypeStruct((rows, 2 * cores * columns), mine.dtype),
+        out_shape=jax.ShapeDtypeStruct((rows, 2 * columns), mine.dtype),
         compiler_params=pltpu.CompilerParams(vmem_limit_bytes=2**20),
-    )(half.reshape(1).astype(jnp.int32), mine, other)
+    )(half.reshape(1), mine, other)
 
 
 def exchange(value, axes):
     return lax.all_to_all(value, axes, 0, 0, tiled=True)
 
 
-def prepare_kernel(groups, core, plane, all_tokens, all_gain, weights, keep, give, packed, *refs):
-    *blocks, tokens, gain, first, ready = refs
-    loads = [
-        pltpu.make_async_copy(all_tokens, tokens, first.at[0]),
-        pltpu.make_async_copy(all_gain, gain, first.at[1]),
-    ]
-    for load in loads:
-        load.start()
+def pack_kernel(plane, weights, packed, *refs):
+    *blocks, ready = refs
     experts, _, packed_width = weights.shape
     hidden_units = packed_width // 3
     part, places = hidden_units // 2, len(blocks)
@@ -93,6 +75,17 @@
             expert = level * places + (plane[0] ^ step)
             copy(weights.at[expert, :, pl.ds(2 * hidden_units, hidden_units)], block.at[level])
 
+    for started in copies:
+        started.wait()
+
+
+def normalize_kernel(groups, core, all_tokens, all_gain, keep, give, tokens, gain, first):
+    loads = [
+        pltpu.make_async_copy(all_tokens, tokens, first.at[0]),
+        pltpu.make_async_copy(all_gain, gain, first.at[1]),
+    ]
+    for load in loads:
+        load.start()
     for load in loads:
         load.wait()
     values = tokens[...].astype(jnp.float32)
@@ -114,58 +107,68 @@
     def _():
         split(give, keep)
 
-    for started in copies:
-        started.wait()
-
-
-def prepare(core, plane, tokens, gain, weights, groups):
-    experts, rows, packed_width = weights.shape
+
+def normalize(core, tokens, gain, groups):
     count, width = tokens.shape
-    hidden_units = packed_width // 3
-    places = experts // 2
-    scalar, vmem = pl.BlockSpec(memory_space=pltpu.SMEM), pl.BlockSpec(memory_space=pltpu.VMEM)
-    hbm = pl.BlockSpec(memory_space=pltpu.HBM)
-    columns = jax.ShapeDtypeStruct((count, width // 2), tokens.dtype)
-    block = jax.ShapeDtypeStruct((2, rows, hidden_units), weights.dtype)
-    packed = jax.ShapeDtypeStruct((2, experts, rows, hidden_units), weights.dtype)
+    hbm, vmem = pl.BlockSpec(memory_space=pltpu.HBM), pl.BlockSpec(memory_space=pltpu.VMEM)
     return pl.pallas_call(
-        functools.partial(prepare_kernel, groups),
-        name="prepare",
-        in_specs=[scalar, scalar, hbm, hbm, hbm],
-        out_specs=[vmem] * (3 + places),
-        out_shape=[columns, columns, packed] + [block] * places,
+        functools.partial(normalize_kernel, groups),
+        name="normalize",
+        in_specs=[pl.BlockSpec(memory_space=pltpu.SMEM), hbm, hbm],
+        out_specs=[vmem] * 2,
+        out_shape=[jax.ShapeDtypeStruct((count, width // 2), tokens.dtype)] * 2,
         scratch_shapes=[
             pltpu.VMEM((count, width), tokens.dtype),
             pltpu.VMEM((1, width), gain.dtype),
             pltpu.SemaphoreType.DMA((2,)),
-            pltpu.SemaphoreType.DMA((4 * PACK_STEPS + experts,)),
         ],
         compiler_params=pltpu.CompilerParams(vmem_limit_bytes=LIMIT),
-    )(core.reshape(1), plane.reshape(1), tokens, gain.reshape(1, width), weights)
-
-
-def gather_kernel(level, plane, kept, arrived, out, ready):
+    )(core.reshape(1), tokens, gain.reshape(1, width))
+
+
+def pack(plane, weights):
+    experts, rows, packed_width = weights.shape
+    hidden_units = packed_width // 3
+    places = experts // 2
+    vmem = pl.BlockSpec(memory_space=pltpu.VMEM)
+    block = jax.ShapeDtypeStruct((2, rows, hidden_units), weights.dtype)
+    packed = jax.ShapeDtypeStruct((2, experts, rows, hidden_units), weights.dtype)
+    return pl.pallas_call(
+        pack_kernel,
+        name="pack",
+        in_specs=[pl.BlockSpec(memory_space=pltpu.SMEM), pl.BlockSpec(memory_space=pltpu.HBM)],
+        out_specs=[vmem] * (1 + places),
+        out_shape=[packed] + [block] * places,
+        scratch_shapes=[pltpu.SemaphoreType.DMA((4 * PACK_STEPS + experts,))],
+        compiler_params=pltpu.CompilerParams(vmem_limit_bytes=LIMIT),
+    )(plane.reshape(1), weights)
+
+
+def gather_kernel(level, plane, core, *refs):
+    *sources, out, ready = refs
     copies = []
-    for i, blocks in enumerate((kept, arrived)):
+    for at, blocks in enumerate(sources):
         for step in range(blocks.shape[0]):
-            target = out.at[level[0] ^ i, plane[0] ^ step]
-            copies.append(pltpu.make_async_copy(blocks.at[step], target, ready.at[i, step]))
+            place = plane[0] ^ step
+            target = out.at[level[0] ^ (at % 2), place // 2, core[0] ^ (at // 2), place % 2]
+            copies.append(pltpu.make_async_copy(blocks.at[step], target, ready.at[at, step]))
             copies[-1].start()
     for copy in copies:
         copy.wait()
 
 
-def gather_blocks(level, plane, kept, arrived):
+def gather_blocks(level, plane, core, sources):
     scalar, hbm = pl.BlockSpec(memory_space=pltpu.SMEM), pl.BlockSpec(memory_space=pltpu.HBM)
+    places, rows, columns = sources[0].shape
     return pl.pallas_call(
         gather_kernel,
         name="gather_blocks",
-        in_specs=[scalar, scalar, hbm, hbm],
+        in_specs=[scalar] * 3 + [hbm] * len(sources),
         out_specs=pl.BlockSpec(memory_space=pltpu.VMEM),
-        out_shape=jax.ShapeDtypeStruct((2,) + kept.shape, kept.dtype),
-        scratch_shapes=[pltpu.SemaphoreType.DMA((2, kept.shape[0]))],
-        compiler_params=pltpu.CompilerParams(vmem_limit_bytes=2**21),
-    )(level.reshape(1), plane.reshape(1), kept, arrived)
+        out_shape=jax.ShapeDtypeStruct((2, places // 2, 2, 2, rows, columns), sources[0].dtype),
+        scratch_shapes=[pltpu.SemaphoreType.DMA((len(sources), places))],
+        compiler_params=pltpu.CompilerParams(vmem_limit_bytes=3 * 2**20),
+    )(level.reshape(1), plane.reshape(1), core.reshape(1), *sources)
 
 
 def dense_layer(tokens, norm_gain, expert_weights, slot_expert, pair_slots, combine_weights):
@@ -181,7 +184,8 @@
 
     z, plane = lax.axis_index("z"), lax.axis_index(("y", "x"))
     places = chips // 2
-    keep, give, packed, *blocks = prepare(c, plane, tokens, norm_gain, expert_weights, groups)
+    keep, give = normalize(c, tokens, norm_gain, groups)
+    packed, *blocks = pack(plane, expert_weights)
     gate_up = exchange(packed.reshape(2 * experts, own_rows, 2 * part), ("h",) + chip_axes)
     gate_up = gate_up.reshape(width // 2, 2 * part)
 
@@ -190,8 +194,9 @@
         blocks[step] = lax.ppermute(blocks[step], ("y", "x"), pairs)
     kept = jnp.stack([lax.dynamic_index_in_dim(block, z, 0, keepdims=False) for block in blocks])
     passed = jnp.stack([lax.dynamic_index_in_dim(block, 1 - z, 0, keepdims=False) for block in blocks])
-    down = gather_blocks(z, plane, kept, lax.ppermute(passed, "z", SWAP))
-    down = down.reshape(width // 4, hidden_units)
+    arrived = lax.ppermute(passed, "z", SWAP)
+    sources = [kept, arrived, lax.ppermute(kept, "c", SWAP), lax.ppermute(arrived, "c", SWAP)]
+    down = gather_blocks(z, plane, c, sources).reshape(width // 2, hidden_units)
 
     from_c = lax.ppermute(give, "c", SWAP)
     from_h = lax.ppermute(keep, "h", SWAP)
@@ -217,16 +222,14 @@
     far, far_weights = lax.optimization_barrier((far, far_weights))
     coefficient = in_order(h, coefficient, far_weights, 1)
     hidden = in_order(h, hidden, far, 1)
-    hidden = in_order(c, hidden, lax.ppermute(hidden, "c", SWAP), 0)
     hidden = lax.optimization_barrier(hidden)
     result = lax.dot_general(hidden, down, (((1,), (1,)), ((), ())), preferred_element_type=jnp.float32)
-    result = result.astype(jnp.bfloat16).reshape(2 * chips, 2 * token_count, width // 4)
-    returned = exchange(result, ("c",) + chip_axes).astype(jnp.float32)
-    returned = returned.reshape(2, chips, 2 * token_count, width // 4)
-    mixed = jnp.sum(returned * coefficient[None, :, :, None], axis=1).astype(jnp.bfloat16)
-    low, high = mixed[:, :token_count], mixed[:, token_count:]
+    result = result.astype(jnp.bfloat16).reshape(chips, 2 * token_count, width // 2)
+    returned = exchange(result, chip_axes).astype(jnp.float32)
+    mixed = jnp.sum(returned * coefficient[:, :, None], axis=0).astype(jnp.bfloat16)
+    low, high = mixed[:token_count], mixed[token_count:]
     mine, sent = jnp.where(h == 0, low, high), jnp.where(h == 0, high, low)
-    return assemble(h, mine, lax.ppermute(sent, "h", SWAP), group)
+    return assemble(h, mine, lax.ppermute(sent, "h", SWAP))
 
 
 def per_device(tokens, norm_gain, expert_weights, slot_expert, pair_slots, combine_weights):

time: 126 us -> 115 us (0.913)
  waiting for transfers between devices: 87.1 us -> 62.3 us
  starting transfers between devices: 27.8 us -> 33.8 us
  Pallas kernels: 5.16 us -> 7.96 us
  local copies, waits for them, and re-layouts: 0.51 us -> 2.58 us
  other arithmetic: 1.44 us -> 2.91 us
    ppermute x1, waiting for transfers between devices: 8.15 us -> 0.01 us  [dense_layer(): far = lax.ppermute(hidden, 'h', SWAP)]
    ppermute x3, waiting for transfers between devices: 13.1 us -> 6.34 us  [dense_layer(): arrived = lax.ppermute(column, ('y', 'x'), pairs)]
    ppermute x1, waiting for transfers between devices: 0.01 us -> 6.44 us  [dense_layer(): far_weights = lax.ppermute(coefficient, 'h', SWAP)]
    ppermute x3 -> x4, waiting for transfers between devices: 8.78 us -> 3.09 us  [the longest x1 3.09 us: dense_layer(): return assemble(h, mine, lax.ppermute(sent, 'h', SWAP))]
    ppermute x1, waiting for transfers between devices: 4.95 us -> 0.87 us  [dense_layer(): lax.ppermute(near, 'z', SWAP)[:, None]]
    ppermute x3, waiting for transfers between devices: 5.81 us -> 1.79 us  [dense_layer(): blocks[step] = lax.ppermute(blocks[step], ('y', 'x'), pairs)]
    ppermute x3 -> x4, starting transfers between devices: 1.54 us -> 4.46 us  [the longest x1 2.01 us: dense_layer(): arrived = lax.ppermute(passed, 'z', SWAP)]
    pallas_call x3 -> x4, Pallas kernels: 5.16 us -> 7.96 us  [the longest x1 3.35 us: pack(): pl.pallas_call(pack_kernel, name='pack', in_specs=[pl.BlockSpec(memory_sp...]
  transfers between devices with their start and end apart: 18 -> 19, of which waited for: 10 -> 12; matrix products, arithmetic and copies ran while one was open for 3% -> 7% of each run, Pallas kernels for 1% -> 3%
where the time goes in v6:
time: 115 us; the launch traced here: 114 us
  waiting for transfers between devices  62.3 us (54%)
  starting transfers between devices  33.8 us (29%)
  Pallas kernels  7.96 us (7%)
  matrix products  4.37 us (4%)
  other arithmetic  2.91 us (3%)
  local copies, waits for them, and re-layouts  2.58 us (2%)
    ppermute x1, waiting for transfers between devices, dense_layer(): from_hc = lax.ppermute(give, ('h', 'c'), CROSS)  33.3 us
    all_to_all x2, starting transfers between devices, exchange(): return lax.all_to_all(value, axes, 0, 0, tiled=True)  12.4 us
    all_to_all x2, waiting for transfers between devices, exchange(): return lax.all_to_all(value, axes, 0, 0, tiled=True)  8.53 us
    ppermute x3, starting transfers between devices, dense_layer(): arrived = lax.ppermute(column, ('y', 'x'), pairs)  6.59 us
    ppermute x1, waiting for transfers between devices, dense_layer(): far_weights = lax.ppermute(coefficient, 'h', SWAP)  6.44 us
    ppermute x3, waiting for transfers between devices, dense_layer(): arrived = lax.ppermute(column, ('y', 'x'), pairs)  6.34 us
    ppermute x3, starting transfers between devices, dense_layer(): blocks[step] = lax.ppermute(blocks[step], ('y', 'x'), pairs)  4.06 us
    pallas_call x1, Pallas kernels, pack(): pl.pallas_call(pack_kernel, name='pack', in_specs=[pl.BlockSpec(memory_sp...  3.35 us
  transfers between devices with their start and end apart: 19, of which 12 were waited for; matrix products, arithmetic and copies ran while one was open for 7% of the time, Pallas kernels for 3%

profile of v6, /device:TPU:0, one launch (start us, length us, event | category | flops | bytes accessed | tf_op | source)
XLA Modules:
  0.0 114.1 jit_solution(753830823633395279)
XLA Ops:
  0.0 3.4 %pack.1 = (bf16[2,8,64,768]{3,2,1,0:T(8,128)(2,1)}, bf16[2,64,768]{2,1,0:T(8,128)(2,1)}, bf16[2,64,768]{2,1,0:T(8,128)(2,1)}, bf16[2,64,768]{2,1,0:T(8,128)(2,1)}, bf16[2,64,768]{2,1,0:T(8,128)(2,1)}) custom-call(s32[1]{0:T(128)} %bitcast.15.plane, bf16[8,64,2304]{2,1,0:T(8,128)(2,1)} %weights.1), custom_call_target="tpu_custom_call" | custom-call | tf_op jit(solution)/shard_map/pack/pallas_call | solution.py:136
  3.4 8.5 %all-to-all-start = ((bf16[16,64,768]{2,1,0:T(8,128)(2,1)}), bf16[16,64,768]{2,1,0:T(8,128)(2,1)S(1)}, u32[]{:S(2)}, u32[]{:S(2)}) async-start(bf16[16,64,768]{2,1,0:T(8,128)(2,1)} %bitcast.41), calls=%async_computation | async-start | bytes 3145728 | tf_op jit(solution)/shard_map/all_to_all | solution.py:52
  11.9 1.6 %normalize.1 = (bf16[16,1024]{1,0:T(8,128)(2,1)}, bf16[16,1024]{1,0:T(8,128)(2,1)}) custom-call(s32[1]{0:T(128)} %bitcast.1.core, bf16[16,2048]{1,0:T(8,128)(2,1)} %all_tokens.1, f32[1,2048]{1,0:T(1,128)} %bitcast.51), custom_call_target="tpu_custom_call" | custom-call | tf_op jit(solution)/shard_map/normalize/pallas_call | solution.py:114
  13.5 1.8 %collective-permute-start.2 = (bf16[16,1024]{1,0:T(8,128)(2,1)}, bf16[16,1024]{1,0:T(8,128)(2,1)S(1)}, u32[]{:S(2)}, u32[]{:S(2)}) collective-permute-start(bf16[16,1024]{1,0:T(8,128)(2,1)} %get-tuple-element.15), channel_id=1, source_target_pairs={{0,18},{2,16},{16,2},{18,0},{1,19},{3,17},{17,3},{19,1},{4,22},{6,... | collective-permute-start | bytes 98312 | tf_op jit(solution)/shard_map/ppermute | solution.py:203
  15.3 1.2 %collective-permute-start.1 = (bf16[16,1024]{1,0:T(8,128)(2,1)}, bf16[16,1024]{1,0:T(8,128)(2,1)S(1)}, u32[]{:S(2)}, u32[]{:S(2)}) collective-permute-start(bf16[16,1024]{1,0:T(8,128)(2,1)} %get-tuple-element.15), channel_id=1, source_target_pairs={{0,2},{2,0},{1,3},{3,1},{4,6},{6,4},{5,7},{7,5},{8,10},{10,8},{9,1... | collective-permute-start | bytes 98312 | tf_op jit(solution)/shard_map/ppermute | solution.py:201
  16.6 33.3 %collective-permute-done.2 = bf16[16,1024]{1,0:T(8,128)(2,1)S(1)} collective-permute-done((bf16[16,1024]{1,0:T(8,128)(2,1)}, bf16[16,1024]{1,0:T(8,128)(2,1)S(1)}, u32[]{:S(2)}, u32[]{:S(2)}) %collective-permute-start.2) | collective-permute-done | bytes 32800 | tf_op jit(solution)/shard_map/ppermute | solution.py:203
  49.9 1.7 %collective-permute-done = bf16[16,1024]{1,0:T(8,128)(2,1)S(1)} collective-permute-done((bf16[16,1024]{1,0:T(8,128)(2,1)}, bf16[16,1024]{1,0:T(8,128)(2,1)S(1)}, u32[]{:S(2)}, u32[]{:S(2)}) %collective-permute-start) | collective-permute-done | bytes 32800 | tf_op jit(solution)/shard_map/ppermute | solution.py:202
  51.6 0.8 maximum_select_fusion.3
  52.6 3.1 %collective-permute-start.12 = (bf16[2,64,768]{2,1,0:T(8,128)(2,1)}, bf16[2,64,768]{2,1,0:T(8,128)(2,1)S(1)}, u32[]{:S(2)}, u32[]{:S(2)}) collective-permute-start(bf16[2,64,768]{2,1,0:T(8,128)(2,1)} %get-tuple-element.21), channel_id=1, source_target_pairs={{0,5},{1,4},{4,1},{5,0},{2,7},{3,6},{6,3},{7,2},{8,13},{9,12},{12,... | collective-permute-start | bytes 589832 | tf_op jit(solution)/shard_map/ppermute | solution.py:194
  55.7 0.9 collective-permute-start.10
  56.7 0.9 collective-permute-done.3
  57.6 1.5 %collective-permute-start.4 = (bf16[2,2,32,1024]{3,2,0,1:T(8,128)(2,1)S(1)}, bf16[2,2,32,1024]{3,2,0,1:T(8,128)(2,1)S(1)}, u32[]{:S(2)}, u32[]{:S(2)}) collective-permute-start(bf16[2,2,32,1024]{3,2,0,1:T(8,128)(2,1)S(1)} %maximum_select_fusion.2), channel_id=1, source_target_pairs={{0,1},{1,0},{4,5},{5,4},{2,3},{3,2},{6,7},{7,6},{8,9},{9,8},{12,13... | collective-permute-start | bytes 786440 | tf_op jit(solution)/shard_map/ppermute | solution.py:210
  59.1 2.2 %collective-permute-start.5 = (bf16[2,2,32,1024]{3,2,0,1:T(8,128)(2,1)S(1)}, bf16[2,2,32,1024]{3,2,0,1:T(8,128)(2,1)S(1)}, u32[]{:S(2)}, u32[]{:S(2)}) collective-permute-start(bf16[2,2,32,1024]{3,2,0,1:T(8,128)(2,1)S(1)} %maximum_select_fusion.2), channel_id=1, source_target_pairs={{0,4},{1,5},{4,0},{5,1},{2,6},{3,7},{6,2},{7,3},{8,12},{9,13},{12,... | collective-permute-start | bytes 786440 | tf_op jit(solution)/shard_map/ppermute | solution.py:210
  61.7 2.9 %collective-permute-start.6 = (bf16[2,2,32,1024]{3,2,0,1:T(8,128)(2,1)S(1)}, bf16[2,2,32,1024]{3,2,0,1:T(8,128)(2,1)S(1)}, u32[]{:S(2)}, u32[]{:S(2)}) collective-permute-start(bf16[2,2,32,1024]{3,2,0,1:T(8,128)(2,1)S(1)} %maximum_select_fusion.2), channel_id=1, source_target_pairs={{0,5},{1,4},{4,1},{5,0},{2,7},{3,6},{6,3},{7,2},{8,13},{9,12},{12,... | collective-permute-start | bytes 786440 | tf_op jit(solution)/shard_map/ppermute | solution.py:210
  64.8 0.7 constant_dynamic-slice_fusion
  65.5 1.4 %collective-permute-done.10 = bf16[2,64,768]{2,1,0:T(8,128)(2,1)S(1)} collective-permute-done((bf16[2,64,768]{2,1,0:T(8,128)(2,1)S(1)}, bf16[2,64,768]{2,1,0:T(8,128)(2,1)S(1)}, u32[]{:S(2)}, u32[]{:S(2)}) %collective-permute-start.10) | collective-permute-done | bytes 196640 | tf_op jit(solution)/shard_map/ppermute | solution.py:194
  67.5 2.0 %collective-permute-start.13 = (bf16[4,64,768]{2,1,0:T(8,128)(2,1)S(1)}, bf16[4,64,768]{2,1,0:T(8,128)(2,1)S(1)}, u32[]{:S(2)}, u32[]{:S(2)}) collective-permute-start(bf16[4,64,768]{2,1,0:T(8,128)(2,1)S(1)} %pad_maximum_fusion.1), channel_id=1, source_target_pairs={{0,8},{8,0},{1,9},{9,1},{2,10},{10,2},{3,11},{11,3},{4,12},{12,4},... | collective-permute-start | bytes 1179656 | tf_op jit(solution)/shard_map/ppermute | solution.py:197
  69.5 2.9 %collective-permute-done.4 = bf16[2,2,32,1024]{3,2,0,1:T(8,128)(2,1)S(1)} collective-permute-done((bf16[2,2,32,1024]{3,2,0,1:T(8,128)(2,1)S(1)}, bf16[2,2,32,1024]{3,2,0,1:T(8,128)(2,1)S(1)}, u32[]{:S(2)}, u32[]{:S(2)}) %collective-permute-start.4) | collective-permute-done | bytes 262176 | tf_op jit(solution)/shard_map/ppermute | solution.py:210
  72.5 3.4 %collective-permute-done.6 = bf16[2,2,32,1024]{3,2,0,1:T(8,128)(2,1)S(1)} collective-permute-done((bf16[2,2,32,1024]{3,2,0,1:T(8,128)(2,1)S(1)}, bf16[2,2,32,1024]{3,2,0,1:T(8,128)(2,1)S(1)}, u32[]{:S(2)}, u32[]{:S(2)}) %collective-permute-start.6) | collective-permute-done | bytes 262176 | tf_op jit(solution)/shard_map/ppermute | solution.py:210
  76.0 0.9 fusion.3
  76.9 1.3 %convolution_convert_fusion.1 = bf16[256,768]{1,0:T(8,128)(2,1)} fusion(bf16[256,1024]{1,0:T(8,128)(2,1)S(1)} %bitcast.44, bf16[1024,768]{1,0:T(8,128)(2,1)S(1)} %bitcast.38), kind=kOutput, calls=%fused_computation.1 | convolution fusion | flops 402849792 | bytes 2490368 | tf_op jit(solution)/shard_map/dot_general | solution.py:215
  78.3 1.0 pad_maximum_fusion.refs_0_
  80.1 1.6 %convert_add_fusion = f32[256,768]{1,0:T(8,128)S(1)} fusion(bf16[256,768]{1,0:T(8,128)(2,1)S(1)} %collective-permute-done.7, bf16[256,1024]{1,0:T(8,128)(2,1)} %bitcast.40, bf16[1024,768]{1,0:T(8,128)(2,1)S(1)} %bitcast.39), kind=kOutput, calls=%fused_computation.3 | convolution fusion | flops 403046400 | bytes 3276800 | tf_op jit(solution)/shard_map/dot_general | solution.py:217
  81.9 1.3 %collective-permute-start.8 = (bf16[256,384]{1,0:T(8,128)(2,1)S(1)}, bf16[256,384]{1,0:T(8,128)(2,1)S(1)}, u32[]{:S(2)}, u32[]{:S(2)}) collective-permute-start(bf16[256,384]{1,0:T(8,128)(2,1)S(1)} %fusion), channel_id=1, source_target_pairs={{0,16},{16,0},{1,17},{17,1},{2,18},{18,2},{3,19},{19,3},{4,20},{20... | collective-permute-start | bytes 589832 | tf_op jit(solution)/shard_map/ppermute | solution.py:219
  83.7 1.8 %collective-permute-start.9 = (f32[8,16]{1,0:T(8,128)S(1)}, f32[8,16]{1,0:T(8,128)S(1)}, u32[]{:S(2)}, u32[]{:S(2)}) collective-permute-start(f32[8,16]{1,0:T(8,128)S(1)} %bitcast.49), channel_id=1, source_target_pairs={{0,16},{16,0},{1,17},{17,1},{2,18},{18,2},{3,19},{19,3},{4,20},{20... | collective-permute-start | bytes 1544 | tf_op jit(solution)/shard_map/ppermute | solution.py:221
  85.5 2.4 %gather_blocks.1 = bf16[2,2,2,2,64,768]{5,4,3,2,1,0:T(8,128)(2,1)S(1)} custom-call(s32[1]{0:T(128)} %bitcast.20.level, s32[1]{0:T(128)} %bitcast.15.plane, s32[1]{0:T(128)} %bitcast.1.core, bf16[4,64,768]{2,1,0:T(8,128)(2,1)S(1)} %pad_maximum_fusion.refs_0_, bf16[4,64,768]{2,1,0:T(8,128)(2,1)S(1)} %collective-permute-done.13.refs_1_, ...), custom_call_target="tpu_custom_call" | custom-call | tf_op jit(solution)/shard_map/gather_blocks/pallas_call | solution.py:163
  87.9 6.4 %collective-permute-done.9 = f32[8,16]{1,0:T(8,128)S(1)} collective-permute-done((f32[8,16]{1,0:T(8,128)S(1)}, f32[8,16]{1,0:T(8,128)S(1)}, u32[]{:S(2)}, u32[]{:S(2)}) %collective-permute-start.9) | collective-permute-done | bytes 544 | tf_op jit(solution)/shard_map/ppermute | solution.py:221
  94.4 1.4 %convolution_convert_fusion = bf16[256,1024]{1,0:T(8,128)(2,1)} fusion(bf16[256,768]{1,0:T(8,128)(2,1)S(1)} %maximum_select_fusion, bf16[1024,768]{1,0:T(8,128)(2,1)S(1)} %bitcast.37), kind=kOutput, calls=%fused_computation | convolution fusion | flops 402915328 | bytes 2490368 | tf_op jit(solution)/shard_map/dot_general | solution.py:226
  95.8 4.0 %all-to-all-start.1 = ((bf16[8,32,1024]{2,1,0:T(8,128)(2,1)}), bf16[8,32,1024]{2,1,0:T(8,128)(2,1)S(1)}, u32[]{:S(2)}, u32[]{:S(2)}) async-start(bf16[8,32,1024]{2,1,0:T(8,128)(2,1)} %bitcast.22), calls=%async_computation.1 | async-start | bytes 1048576 | tf_op jit(solution)/shard_map/all_to_all | solution.py:52
  99.8 8.5 %all-to-all-done.1 = bf16[8,32,1024]{2,1,0:T(8,128)(2,1)S(1)} async-done(((bf16[8,32,1024]{2,1,0:T(8,128)(2,1)}), bf16[8,32,1024]{2,1,0:T(8,128)(2,1)S(1)}, u32[]{:S(2)}, u32[]{:S(2)}) %all-to-all-start.1) | async-done | bytes 524320 | tf_op jit(solution)/shard_map/all_to_all | solution.py:52
  108.6 1.8 %collective-permute-start.16 = (bf16[16,1024]{1,0:T(8,128)(2,1)S(1)}, bf16[16,1024]{1,0:T(8,128)(2,1)S(1)}, u32[]{:S(2)}, u32[]{:S(2)}) collective-permute-start(bf16[16,1024]{1,0:T(8,128)(2,1)S(1)} %get-tuple-element.36), channel_id=1, source_target_pairs={{0,16},{16,0},{1,17},{17,1},{2,18},{18,2},{3,19},{19,3},{4,20},{20... | collective-permute-start | bytes 98312 | tf_op jit(solution)/shard_map/ppermute | solution.py:232
  110.3 3.1 %collective-permute-done.16.other = bf16[16,1024]{1,0:T(8,128)(2,1)S(1)} collective-permute-done((bf16[16,1024]{1,0:T(8,128)(2,1)S(1)}, bf16[16,1024]{1,0:T(8,128)(2,1)S(1)}, u32[]{:S(2)}, u32[]{:S(2)}) %collective-permute-start.16) | collective-permute-done | bytes 32800 | tf_op jit(solution)/shard_map/ppermute | solution.py:232
  (48 shorter events, 4.2 us)
Async XLA Ops:
  3.4 52.3 %copy-start.4 = (bf16[2,64,768]{2,1,0:T(8,128)(2,1)S(1)}, bf16[2,64,768]{2,1,0:T(8,128)(2,1)}, u32[]{:S(2)}) copy-start(bf16[2,64,768]{2,1,0:T(8,128)(2,1)} %get-tuple-element.19) | copy-start | bytes 589828
  3.4 53.3 %copy-start = (bf16[2,64,768]{2,1,0:T(8,128)(2,1)S(1)}, bf16[2,64,768]{2,1,0:T(8,128)(2,1)}, u32[]{:S(2)}) copy-start(bf16[2,64,768]{2,1,0:T(8,128)(2,1)} %get-tuple-element.18) | copy-start | bytes 589828
  3.4 73.5 %all-to-all-start = ((bf16[16,64,768]{2,1,0:T(8,128)(2,1)}), bf16[16,64,768]{2,1,0:T(8,128)(2,1)S(1)}, u32[]{:S(2)}, u32[]{:S(2)}) async-start(bf16[16,64,768]{2,1,0:T(8,128)(2,1)} %bitcast.41), calls=%async_computation | async-start | bytes 3145728 | tf_op jit(solution)/shard_map/all_to_all | solution.py:52
  13.5 36.4 %collective-permute-start.2 = (bf16[16,1024]{1,0:T(8,128)(2,1)}, bf16[16,1024]{1,0:T(8,128)(2,1)S(1)}, u32[]{:S(2)}, u32[]{:S(2)}) collective-permute-start(bf16[16,1024]{1,0:T(8,128)(2,1)} %get-tuple-element.15), channel_id=1, source_target_pairs={{0,18},{2,16},{16,2},{18,0},{1,19},{3,17},{17,3},{19,1},{4,22},{6,... | collective-permute-start | bytes 98312 | tf_op jit(solution)/shard_map/ppermute | solution.py:203
  15.3 34.7 %collective-permute-start.1 = (bf16[16,1024]{1,0:T(8,128)(2,1)}, bf16[16,1024]{1,0:T(8,128)(2,1)S(1)}, u32[]{:S(2)}, u32[]{:S(2)}) collective-permute-start(bf16[16,1024]{1,0:T(8,128)(2,1)} %get-tuple-element.15), channel_id=1, source_target_pairs={{0,2},{2,0},{1,3},{3,1},{4,6},{6,4},{5,7},{7,5},{8,10},{10,8},{9,1... | collective-permute-start | bytes 98312 | tf_op jit(solution)/shard_map/ppermute | solution.py:201
  16.5 35.1 %collective-permute-start = (bf16[16,1024]{1,0:T(8,128)(2,1)}, bf16[16,1024]{1,0:T(8,128)(2,1)S(1)}, u32[]{:S(2)}, u32[]{:S(2)}) collective-permute-start(bf16[16,1024]{1,0:T(8,128)(2,1)} %get-tuple-element.14), channel_id=1, source_target_pairs={{0,16},{16,0},{1,17},{17,1},{2,18},{18,2},{3,19},{19,3},{4,20},{20... | collective-permute-start | bytes 98312 | tf_op jit(solution)/shard_map/ppermute | solution.py:202
  52.5 5.0 %collective-permute-start.3 = (bf16[2,32,1024]{2,1,0:T(8,128)(2,1)S(1)}, bf16[2,32,1024]{2,1,0:T(8,128)(2,1)S(1)}, u32[]{:S(2)}, u32[]{:S(2)}) collective-permute-start(bf16[2,32,1024]{2,1,0:T(8,128)(2,1)S(1)} %get-tuple-element.35), channel_id=1, source_target_pairs={{0,8},{8,0},{1,9},{9,1},{2,10},{10,2},{3,11},{11,3},{4,12},{12,4},... | collective-permute-start | bytes 393224 | tf_op jit(solution)/shard_map/ppermute | solution.py:205
  52.6 9.1 %collective-permute-start.12 = (bf16[2,64,768]{2,1,0:T(8,128)(2,1)}, bf16[2,64,768]{2,1,0:T(8,128)(2,1)S(1)}, u32[]{:S(2)}, u32[]{:S(2)}) collective-permute-start(bf16[2,64,768]{2,1,0:T(8,128)(2,1)} %get-tuple-element.21), channel_id=1, source_target_pairs={{0,5},{1,4},{4,1},{5,0},{2,7},{3,6},{6,3},{7,2},{8,13},{9,12},{12,... | collective-permute-start | bytes 589832 | tf_op jit(solution)/shard_map/ppermute | solution.py:194
  55.7 9.1 %collective-permute-start.11 = (bf16[2,64,768]{2,1,0:T(8,128)(2,1)}, bf16[2,64,768]{2,1,0:T(8,128)(2,1)S(1)}, u32[]{:S(2)}, u32[]{:S(2)}) collective-permute-start(bf16[2,64,768]{2,1,0:T(8,128)(2,1)} %get-tuple-element.20), channel_id=1, source_target_pairs={{0,4},{1,5},{4,0},{5,1},{2,6},{3,7},{6,2},{7,3},{8,12},{9,13},{12,... | collective-permute-start | bytes 589832 | tf_op jit(solution)/shard_map/ppermute | solution.py:194
  55.7 11.1 %collective-permute-start.10 = (bf16[2,64,768]{2,1,0:T(8,128)(2,1)S(1)}, bf16[2,64,768]{2,1,0:T(8,128)(2,1)S(1)}, u32[]{:S(2)}, u32[]{:S(2)}) collective-permute-start(bf16[2,64,768]{2,1,0:T(8,128)(2,1)S(1)} %copy-done.4), channel_id=1, source_target_pairs={{0,1},{1,0},{4,5},{5,4},{2,3},{3,2},{6,7},{7,6},{8,9},{9,8},{12,13... | collective-permute-start | bytes 589832 | tf_op jit(solution)/shard_map/ppermute | solution.py:194
  57.6 14.9 %collective-permute-start.4 = (bf16[2,2,32,1024]{3,2,0,1:T(8,128)(2,1)S(1)}, bf16[2,2,32,1024]{3,2,0,1:T(8,128)(2,1)S(1)}, u32[]{:S(2)}, u32[]{:S(2)}) collective-permute-start(bf16[2,2,32,1024]{3,2,0,1:T(8,128)(2,1)S(1)} %maximum_select_fusion.2), channel_id=1, source_target_pairs={{0,1},{1,0},{4,5},{5,4},{2,3},{3,2},{6,7},{7,6},{8,9},{9,8},{12,13... | collective-permute-start | bytes 786440 | tf_op jit(solution)/shard_map/ppermute | solution.py:210
  59.1 13.4 %collective-permute-start.5 = (bf16[2,2,32,1024]{3,2,0,1:T(8,128)(2,1)S(1)}, bf16[2,2,32,1024]{3,2,0,1:T(8,128)(2,1)S(1)}, u32[]{:S(2)}, u32[]{:S(2)}) collective-permute-start(bf16[2,2,32,1024]{3,2,0,1:T(8,128)(2,1)S(1)} %maximum_select_fusion.2), channel_id=1, source_target_pairs={{0,4},{1,5},{4,0},{5,1},{2,6},{3,7},{6,2},{7,3},{8,12},{9,13},{12,... | collective-permute-start | bytes 786440 | tf_op jit(solution)/shard_map/ppermute | solution.py:210
  61.7 14.3 %collective-permute-start.6 = (bf16[2,2,32,1024]{3,2,0,1:T(8,128)(2,1)S(1)}, bf16[2,2,32,1024]{3,2,0,1:T(8,128)(2,1)S(1)}, u32[]{:S(2)}, u32[]{:S(2)}) collective-permute-start(bf16[2,2,32,1024]{3,2,0,1:T(8,128)(2,1)S(1)} %maximum_select_fusion.2), channel_id=1, source_target_pairs={{0,5},{1,4},{4,1},{5,0},{2,7},{3,6},{6,3},{7,2},{8,13},{9,12},{12,... | collective-permute-start | bytes 786440 | tf_op jit(solution)/shard_map/ppermute | solution.py:210
  67.5 12.3 %collective-permute-start.13 = (bf16[4,64,768]{2,1,0:T(8,128)(2,1)S(1)}, bf16[4,64,768]{2,1,0:T(8,128)(2,1)S(1)}, u32[]{:S(2)}, u32[]{:S(2)}) collective-permute-start(bf16[4,64,768]{2,1,0:T(8,128)(2,1)S(1)} %pad_maximum_fusion.1), channel_id=1, source_target_pairs={{0,8},{8,0},{1,9},{9,1},{2,10},{10,2},{3,11},{11,3},{4,12},{12,4},... | collective-permute-start | bytes 1179656 | tf_op jit(solution)/shard_map/ppermute | solution.py:197
  76.9 1.3 %copy-start.1 = (s32[16,8]{0,1:T(8,128)S(1)}, s32[16,8]{0,1:T(8,128)}, u32[]{:S(2)}) copy-start(s32[16,8]{0,1:T(8,128)} %param.10) | copy-start | bytes 1540
  78.2 1.9 %collective-permute-start.7 = (bf16[256,768]{1,0:T(8,128)(2,1)}, bf16[256,768]{1,0:T(8,128)(2,1)S(1)}, u32[]{:S(2)}, u32[]{:S(2)}) collective-permute-start(bf16[256,768]{1,0:T(8,128)(2,1)} %convolution_convert_fusion.1), channel_id=1, source_target_pairs={{0,2},{2,0},{1,3},{3,1},{4,6},{6,4},{5,7},{7,5},{8,10},{10,8},{9,1... | collective-permute-start | bytes 1179656 | tf_op jit(solution)/shard_map/ppermute | solution.py:216
  79.3 6.2 %collective-permute-start.14 = (bf16[4,64,768]{2,1,0:T(8,128)(2,1)S(1)}, bf16[4,64,768]{2,1,0:T(8,128)(2,1)S(1)}, u32[]{:S(2)}, u32[]{:S(2)}) collective-permute-start(bf16[4,64,768]{2,1,0:T(8,128)(2,1)S(1)} %pad_maximum_fusion.refs_0_), channel_id=1, source_target_pairs={{0,2},{2,0},{1,3},{3,1},{4,6},{6,4},{5,7},{7,5},{8,10},{10,8},{9,1... | collective-permute-start | bytes 1179656 | tf_op jit(solution)/shard_map/ppermute | solution.py:198
  79.8 5.6 %collective-permute-start.15 = (bf16[4,64,768]{2,1,0:T(8,128)(2,1)S(1)}, bf16[4,64,768]{2,1,0:T(8,128)(2,1)S(1)}, u32[]{:S(2)}, u32[]{:S(2)}) collective-permute-start(bf16[4,64,768]{2,1,0:T(8,128)(2,1)S(1)} %collective-permute-done.13.refs_1_), channel_id=1, source_target_pairs={{0,2},{2,0},{1,3},{3,1},{4,6},{6,4},{5,7},{7,5},{8,10},{10,8},{9,1... | collective-permute-start | bytes 1179656 | tf_op jit(solution)/shard_map/ppermute | solution.py:198
  80.1 3.1 %copy-start.3 = (s32[16]{0:T(128)S(1)}, s32[16]{0:T(128)}, u32[]{:S(2)}) copy-start(s32[16]{0:T(128)} %param.9) | copy-start | bytes 196
  80.1 3.5 %copy-start.2 = (f32[16,8]{0,1:T(8,128)S(1)}, f32[16,8]{0,1:T(8,128)}, u32[]{:S(2)}) copy-start(f32[16,8]{0,1:T(8,128)} %param.11) | copy-start | bytes 1540
  81.9 12.4 %collective-permute-start.8 = (bf16[256,384]{1,0:T(8,128)(2,1)S(1)}, bf16[256,384]{1,0:T(8,128)(2,1)S(1)}, u32[]{:S(2)}, u32[]{:S(2)}) collective-permute-start(bf16[256,384]{1,0:T(8,128)(2,1)S(1)} %fusion), channel_id=1, source_target_pairs={{0,16},{16,0},{1,17},{17,1},{2,18},{18,2},{3,19},{19,3},{4,20},{20... | collective-permute-start | bytes 589832 | tf_op jit(solution)/shard_map/ppermute | solution.py:219
  83.7 10.6 %collective-permute-start.9 = (f32[8,16]{1,0:T(8,128)S(1)}, f32[8,16]{1,0:T(8,128)S(1)}, u32[]{:S(2)}, u32[]{:S(2)}) collective-permute-start(f32[8,16]{1,0:T(8,128)S(1)} %bitcast.49), channel_id=1, source_target_pairs={{0,16},{16,0},{1,17},{17,1},{2,18},{18,2},{3,19},{19,3},{4,20},{20... | collective-permute-start | bytes 1544 | tf_op jit(solution)/shard_map/ppermute | solution.py:221
  95.8 12.6 %all-to-all-start.1 = ((bf16[8,32,1024]{2,1,0:T(8,128)(2,1)}), bf16[8,32,1024]{2,1,0:T(8,128)(2,1)S(1)}, u32[]{:S(2)}, u32[]{:S(2)}) async-start(bf16[8,32,1024]{2,1,0:T(8,128)(2,1)} %bitcast.22), calls=%async_computation.1 | async-start | bytes 1048576 | tf_op jit(solution)/shard_map/all_to_all | solution.py:52
  108.6 4.9 %collective-permute-start.16 = (bf16[16,1024]{1,0:T(8,128)(2,1)S(1)}, bf16[16,1024]{1,0:T(8,128)(2,1)S(1)}, u32[]{:S(2)}, u32[]{:S(2)}) collective-permute-start(bf16[16,1024]{1,0:T(8,128)(2,1)S(1)} %get-tuple-element.36), channel_id=1, source_target_pairs={{0,16},{16,0},{1,17},{17,1},{2,18},{18,2},{3,19},{19,3},{4,20},{20... | collective-permute-start | bytes 98312 | tf_op jit(solution)/shard_map/ppermute | solution.py:232

commit v7 on v6

--- a/solution.py
+++ b/solution.py
@@ -8,7 +8,7 @@
 from jax.sharding import Mesh, PartitionSpec as P
 
 SWAP = [(0, 1), (1, 0)]
-PACK_STEPS = 4
+PACK_STEPS = 2
 LIMIT = 61 * 2**20
 CROSS = [(0, 3), (1, 2), (2, 1), (3, 0)]
 
@@ -53,30 +53,41 @@
 
 
 def pack_kernel(plane, weights, packed, *refs):
-    *blocks, ready = refs
+    places = weights.shape[0] // 2
+    outs, (room, down_room, ready, done) = refs[:places], refs[places:]
     experts, _, packed_width = weights.shape
     hidden_units = packed_width // 3
-    part, places = hidden_units // 2, len(blocks)
-    copies = []
-
-    def copy(source, target):
-        copies.append(pltpu.make_async_copy(source, target, ready.at[len(copies)]))
-        copies[-1].start()
-
-    size = experts // PACK_STEPS
+    part, size = hidden_units // 2, experts // PACK_STEPS
+    loads, stores, at = [], [], 0
+
+    def load(source, target):
+        nonlocal at
+        loads[-1].append(pltpu.make_async_copy(source, target, ready.at[at]))
+        loads[-1][-1].start()
+        at += 1
+
     for k in range(PACK_STEPS):
         some = pl.ds(k * size, size)
         for i in range(2):
+            loads.append([])
             for j in range(2):
                 source = weights.at[some, :, pl.ds(j * hidden_units + i * part, part)]
-                copy(source, packed.at[i, some, :, pl.ds(j * part, part)])
-    for step, block in enumerate(blocks):
-        for level in range(experts // places):
+                load(source, room.at[i, some, :, pl.ds(j * part, part)])
+            stores.append((room.at[i, some], packed.at[i, some]))
+    for step in range(places):
+        loads.append([])
+        for level in range(2):
             expert = level * places + (plane[0] ^ step)
-            copy(weights.at[expert, :, pl.ds(2 * hidden_units, hidden_units)], block.at[level])
-
-    for started in copies:
-        started.wait()
+            load(weights.at[expert, :, pl.ds(2 * hidden_units, hidden_units)], down_room.at[step, level])
+        stores.append((down_room.at[step], outs[step]))
+    writes = []
+    for arriving, (source, target) in zip(loads, stores, strict=True):
+        for copy in arriving:
+            copy.wait()
+        writes.append(pltpu.make_async_copy(source, target, done.at[len(writes)]))
+        writes[-1].start()
+    for copy in writes:
+        copy.wait()
 
 
 def normalize_kernel(groups, core, all_tokens, all_gain, keep, give, tokens, gain, first):
@@ -130,16 +141,21 @@
     experts, rows, packed_width = weights.shape
     hidden_units = packed_width // 3
     places = experts // 2
-    vmem = pl.BlockSpec(memory_space=pltpu.VMEM)
+    hbm = pl.BlockSpec(memory_space=pltpu.HBM)
     block = jax.ShapeDtypeStruct((2, rows, hidden_units), weights.dtype)
     packed = jax.ShapeDtypeStruct((2, experts, rows, hidden_units), weights.dtype)
     return pl.pallas_call(
         pack_kernel,
         name="pack",
-        in_specs=[pl.BlockSpec(memory_space=pltpu.SMEM), pl.BlockSpec(memory_space=pltpu.HBM)],
-        out_specs=[vmem] * (1 + places),
+        in_specs=[pl.BlockSpec(memory_space=pltpu.SMEM), hbm],
+        out_specs=[hbm] * (1 + places),
         out_shape=[packed] + [block] * places,
-        scratch_shapes=[pltpu.SemaphoreType.DMA((4 * PACK_STEPS + experts,))],
+        scratch_shapes=[
+            pltpu.VMEM(packed.shape, weights.dtype),
+            pltpu.VMEM((places,) + block.shape, weights.dtype),
+            pltpu.SemaphoreType.DMA((4 * PACK_STEPS + experts,)),
+            pltpu.SemaphoreType.DMA((2 * PACK_STEPS + places,)),
+        ],
         compiler_params=pltpu.CompilerParams(vmem_limit_bytes=LIMIT),
     )(plane.reshape(1), weights)
 
@@ -194,6 +210,7 @@
         blocks[step] = lax.ppermute(blocks[step], ("y", "x"), pairs)
     kept = jnp.stack([lax.dynamic_index_in_dim(block, z, 0, keepdims=False) for block in blocks])
     passed = jnp.stack([lax.dynamic_index_in_dim(block, 1 - z, 0, keepdims=False) for block in blocks])
+    kept, passed = lax.optimization_barrier((kept, passed))
     arrived = lax.ppermute(passed, "z", SWAP)
     sources = [kept, arrived, lax.ppermute(kept, "c", SWAP), lax.ppermute(arrived, "c", SWAP)]
     down = gather_blocks(z, plane, c, sources).reshape(width // 2, hidden_units)
@@ -214,9 +231,12 @@
 
     other = jnp.dot(rows[1, 0], gate_up, preferred_element_type=jnp.float32).astype(jnp.bfloat16)
     arrived = lax.ppermute(other, "c", SWAP)
-    pre = jnp.dot(rows[0, 0], gate_up, preferred_element_type=jnp.float32) + arrived.astype(jnp.float32)
+    kept_sums = jnp.dot(rows[0, 0], gate_up, preferred_element_type=jnp.float32)
+    kept_sums, arrived = lax.optimization_barrier((kept_sums, arrived))
+    pre = kept_sums + arrived.astype(jnp.float32)
     hidden = (jax.nn.silu(pre[:, :part]) * pre[:, part:]).astype(jnp.bfloat16)
     far = lax.ppermute(hidden, "h", SWAP)
+    hidden, pair_slots = lax.optimization_barrier((hidden, pair_slots))
     coefficient = slot_coefficients(slot_expert, pair_slots, combine_weights, experts).T
     far_weights = lax.ppermute(coefficient, "h", SWAP)
     far, far_weights = lax.optimization_barrier((far, far_weights))

time: 115 us -> 112 us (0.974)
  waiting for transfers between devices: 62.3 us -> 65.9 us
  starting transfers between devices: 33.8 us -> 31.9 us
  matrix products: 4.37 us -> 2.56 us
  local copies, waits for them, and re-layouts: 2.58 us -> 1.29 us
    ppermute x3, waiting for transfers between devices: 1.79 us -> 3.14 us  [dense_layer(): blocks[step] = lax.ppermute(blocks[step], ('y', 'x'), pairs)]
    dynamic_slice x4, local copies, waits for them, and re-layouts: 1.34 us -> 0.05 us  [dense_layer(): lax.dynamic_index_in_dim(block, 1 - z, 0, keepdims=False)]
    ppermute x3, waiting for transfers between devices: 6.34 us -> 7.61 us  [dense_layer(): arrived = lax.ppermute(column, ('y', 'x'), pairs)]
    ppermute x1, starting transfers between devices: 1.24 us -> 0.07 us  [dense_layer(): from_c = lax.ppermute(give, 'c', SWAP)]
    ppermute x1, starting transfers between devices: 1.76 us -> 2.92 us  [dense_layer(): from_hc = lax.ppermute(give, ('h', 'c'), CROSS)]
  transfers between devices with their start and end apart: 19 -> 19, of which waited for: 12 -> 12; matrix products, arithmetic and copies ran while one was open for 7% -> 4% of each run, Pallas kernels for 3% -> 4%
where the time goes in v7:
time: 112 us; the launch traced here: 111 us
  waiting for transfers between devices  65.9 us (59%)
  starting transfers between devices  31.9 us (28%)
  Pallas kernels  7.35 us (7%)
  matrix products  2.56 us (2%)
  other arithmetic  2.03 us (2%)
  local copies, waits for them, and re-layouts  1.29 us (1%)
    ppermute x1, waiting for transfers between devices, dense_layer(): from_hc = lax.ppermute(give, ('h', 'c'), CROSS)  33.3 us
    all_to_all x2, starting transfers between devices, exchange(): return lax.all_to_all(value, axes, 0, 0, tiled=True)  12 us
    all_to_all x2, waiting for transfers between devices, exchange(): return lax.all_to_all(value, axes, 0, 0, tiled=True)  8.7 us
    ppermute x3, waiting for transfers between devices, dense_layer(): arrived = lax.ppermute(column, ('y', 'x'), pairs)  7.61 us
    ppermute x1, waiting for transfers between devices, dense_layer(): far_weights = lax.ppermute(coefficient, 'h', SWAP)  6.27 us
    ppermute x3, starting transfers between devices, dense_layer(): arrived = lax.ppermute(column, ('y', 'x'), pairs)  5.93 us
    ppermute x3, starting transfers between devices, dense_layer(): blocks[step] = lax.ppermute(blocks[step], ('y', 'x'), pairs)  4.06 us
    ppermute x1, waiting for transfers between devices, dense_layer(): return assemble(h, mine, lax.ppermute(sent, 'h', SWAP))  3.75 us
  transfers between devices with their start and end apart: 19, of which 12 were waited for; matrix products, arithmetic and copies ran while one was open for 4% of the time, Pallas kernels for 4%

profile of v7, /device:TPU:0, one launch (start us, length us, event | category | flops | bytes accessed | tf_op | source)
XLA Modules:
  0.0 111.3 jit_solution(13565951665557744717)
XLA Ops:
  0.0 2.7 %pack.1 = (bf16[2,8,64,768]{3,2,1,0:T(8,128)(2,1)}, bf16[2,64,768]{2,1,0:T(8,128)(2,1)}, bf16[2,64,768]{2,1,0:T(8,128)(2,1)}, bf16[2,64,768]{2,1,0:T(8,128)(2,1)}, bf16[2,64,768]{2,1,0:T(8,128)(2,1)}) custom-call(s32[1]{0:T(128)} %bitcast.15.plane, bf16[8,64,2304]{2,1,0:T(8,128)(2,1)} %weights.1), custom_call_target="tpu_custom_call" | custom-call | tf_op jit(solution)/shard_map/pack/pallas_call | solution.py:147
  2.8 8.5 %all-to-all-start = ((bf16[16,64,768]{2,1,0:T(8,128)(2,1)}), bf16[16,64,768]{2,1,0:T(8,128)(2,1)S(1)}, u32[]{:S(2)}, u32[]{:S(2)}) async-start(bf16[16,64,768]{2,1,0:T(8,128)(2,1)} %bitcast.41), calls=%async_computation | async-start | bytes 3145728 | tf_op jit(solution)/shard_map/all_to_all | solution.py:52
  11.3 1.6 %normalize.1 = (bf16[16,1024]{1,0:T(8,128)(2,1)}, bf16[16,1024]{1,0:T(8,128)(2,1)}) custom-call(s32[1]{0:T(128)} %bitcast.1.core, bf16[16,2048]{1,0:T(8,128)(2,1)} %all_tokens.1, f32[1,2048]{1,0:T(1,128)} %bitcast.51), custom_call_target="tpu_custom_call" | custom-call | tf_op jit(solution)/shard_map/normalize/pallas_call | solution.py:125
  13.0 2.9 %collective-permute-start.2 = (bf16[16,1024]{1,0:T(8,128)(2,1)}, bf16[16,1024]{1,0:T(8,128)(2,1)S(1)}, u32[]{:S(2)}, u32[]{:S(2)}) collective-permute-start(bf16[16,1024]{1,0:T(8,128)(2,1)} %get-tuple-element.21), channel_id=1, source_target_pairs={{0,18},{2,16},{16,2},{18,0},{1,19},{3,17},{17,3},{19,1},{4,22},{6,... | collective-permute-start | bytes 98312 | tf_op jit(solution)/shard_map/ppermute | solution.py:220
  16.0 33.3 %collective-permute-done.2 = bf16[16,1024]{1,0:T(8,128)(2,1)S(1)} collective-permute-done((bf16[16,1024]{1,0:T(8,128)(2,1)}, bf16[16,1024]{1,0:T(8,128)(2,1)S(1)}, u32[]{:S(2)}, u32[]{:S(2)}) %collective-permute-start.2) | collective-permute-done | bytes 32800 | tf_op jit(solution)/shard_map/ppermute | solution.py:220
  49.3 1.7 %collective-permute-done = bf16[16,1024]{1,0:T(8,128)(2,1)S(1)} collective-permute-done((bf16[16,1024]{1,0:T(8,128)(2,1)}, bf16[16,1024]{1,0:T(8,128)(2,1)S(1)}, u32[]{:S(2)}, u32[]{:S(2)}) %collective-permute-start) | collective-permute-done | bytes 32800 | tf_op jit(solution)/shard_map/ppermute | solution.py:219
  51.0 0.8 maximum_select_fusion.3
  52.0 1.5 %collective-permute-start.10 = (bf16[2,64,768]{2,1,0:T(8,128)(2,1)}, bf16[2,64,768]{2,1,0:T(8,128)(2,1)S(1)}, u32[]{:S(2)}, u32[]{:S(2)}) collective-permute-start(bf16[2,64,768]{2,1,0:T(8,128)(2,1)} %get-tuple-element.29), channel_id=1, source_target_pairs={{0,1},{1,0},{4,5},{5,4},{2,3},{3,2},{6,7},{7,6},{8,9},{9,8},{12,13... | collective-permute-start | bytes 589832 | tf_op jit(solution)/shard_map/ppermute | solution.py:210
  53.5 2.2 %collective-permute-start.11 = (bf16[2,64,768]{2,1,0:T(8,128)(2,1)}, bf16[2,64,768]{2,1,0:T(8,128)(2,1)S(1)}, u32[]{:S(2)}, u32[]{:S(2)}) collective-permute-start(bf16[2,64,768]{2,1,0:T(8,128)(2,1)} %get-tuple-element.30), channel_id=1, source_target_pairs={{0,4},{1,5},{4,0},{5,1},{2,6},{3,7},{6,2},{7,3},{8,12},{9,13},{12,... | collective-permute-start | bytes 589832 | tf_op jit(solution)/shard_map/ppermute | solution.py:210
  56.0 0.9 collective-permute-done.3
  56.9 1.5 %collective-permute-start.4 = (bf16[2,2,32,1024]{3,2,0,1:T(8,128)(2,1)S(1)}, bf16[2,2,32,1024]{3,2,0,1:T(8,128)(2,1)S(1)}, u32[]{:S(2)}, u32[]{:S(2)}) collective-permute-start(bf16[2,2,32,1024]{3,2,0,1:T(8,128)(2,1)S(1)} %maximum_select_fusion.2), channel_id=1, source_target_pairs={{0,1},{1,0},{4,5},{5,4},{2,3},{3,2},{6,7},{7,6},{8,9},{9,8},{12,13... | collective-permute-start | bytes 786440 | tf_op jit(solution)/shard_map/ppermute | solution.py:227
  58.5 2.2 %collective-permute-start.5 = (bf16[2,2,32,1024]{3,2,0,1:T(8,128)(2,1)S(1)}, bf16[2,2,32,1024]{3,2,0,1:T(8,128)(2,1)S(1)}, u32[]{:S(2)}, u32[]{:S(2)}) collective-permute-start(bf16[2,2,32,1024]{3,2,0,1:T(8,128)(2,1)S(1)} %maximum_select_fusion.2), channel_id=1, source_target_pairs={{0,4},{1,5},{4,0},{5,1},{2,6},{3,7},{6,2},{7,3},{8,12},{9,13},{12,... | collective-permute-start | bytes 786440 | tf_op jit(solution)/shard_map/ppermute | solution.py:227
  60.8 2.2 %collective-permute-start.6 = (bf16[2,2,32,1024]{3,2,0,1:T(8,128)(2,1)S(1)}, bf16[2,2,32,1024]{3,2,0,1:T(8,128)(2,1)S(1)}, u32[]{:S(2)}, u32[]{:S(2)}) collective-permute-start(bf16[2,2,32,1024]{3,2,0,1:T(8,128)(2,1)S(1)} %maximum_select_fusion.2), channel_id=1, source_target_pairs={{0,5},{1,4},{4,1},{5,0},{2,7},{3,6},{6,3},{7,2},{8,13},{9,12},{12,... | collective-permute-start | bytes 786440 | tf_op jit(solution)/shard_map/ppermute | solution.py:227
  63.1 2.0 %collective-permute-done.11 = bf16[2,64,768]{2,1,0:T(8,128)(2,1)S(1)} collective-permute-done((bf16[2,64,768]{2,1,0:T(8,128)(2,1)}, bf16[2,64,768]{2,1,0:T(8,128)(2,1)S(1)}, u32[]{:S(2)}, u32[]{:S(2)}) %collective-permute-start.11) | collective-permute-done | bytes 196640 | tf_op jit(solution)/shard_map/ppermute | solution.py:210
  65.1 1.2 %collective-permute-done.12 = bf16[2,64,768]{2,1,0:T(8,128)(2,1)S(1)} collective-permute-done((bf16[2,64,768]{2,1,0:T(8,128)(2,1)}, bf16[2,64,768]{2,1,0:T(8,128)(2,1)S(1)}, u32[]{:S(2)}, u32[]{:S(2)}) %collective-permute-start.12) | collective-permute-done | bytes 196640 | tf_op jit(solution)/shard_map/ppermute | solution.py:210
  66.4 2.0 %collective-permute-start.13 = (bf16[4,64,768]{2,1,0:T(8,128)(2,1)S(1)}, bf16[4,64,768]{2,1,0:T(8,128)(2,1)S(1)}, u32[]{:S(2)}, u32[]{:S(2)}) collective-permute-start(bf16[4,64,768]{2,1,0:T(8,128)(2,1)S(1)} %get-tuple-element.33), channel_id=1, source_target_pairs={{0,8},{8,0},{1,9},{9,1},{2,10},{10,2},{3,11},{11,3},{4,12},{12,4},... | collective-permute-start | bytes 1179656 | tf_op jit(solution)/shard_map/ppermute | solution.py:214
  68.3 1.5 %collective-permute-done.4 = bf16[2,2,32,1024]{3,2,0,1:T(8,128)(2,1)S(1)} collective-permute-done((bf16[2,2,32,1024]{3,2,0,1:T(8,128)(2,1)S(1)}, bf16[2,2,32,1024]{3,2,0,1:T(8,128)(2,1)S(1)}, u32[]{:S(2)}, u32[]{:S(2)}) %collective-permute-start.4) | collective-permute-done | bytes 262176 | tf_op jit(solution)/shard_map/ppermute | solution.py:227
  69.9 5.0 %collective-permute-done.5 = bf16[2,2,32,1024]{3,2,0,1:T(8,128)(2,1)S(1)} collective-permute-done((bf16[2,2,32,1024]{3,2,0,1:T(8,128)(2,1)S(1)}, bf16[2,2,32,1024]{3,2,0,1:T(8,128)(2,1)S(1)}, u32[]{:S(2)}, u32[]{:S(2)}) %collective-permute-start.5) | collective-permute-done | bytes 262176 | tf_op jit(solution)/shard_map/ppermute | solution.py:227
  74.9 1.1 %collective-permute-done.6 = bf16[2,2,32,1024]{3,2,0,1:T(8,128)(2,1)S(1)} collective-permute-done((bf16[2,2,32,1024]{3,2,0,1:T(8,128)(2,1)S(1)}, bf16[2,2,32,1024]{3,2,0,1:T(8,128)(2,1)S(1)}, u32[]{:S(2)}, u32[]{:S(2)}) %collective-permute-start.6) | collective-permute-done | bytes 262176 | tf_op jit(solution)/shard_map/ppermute | solution.py:227
  76.0 0.9 fusion.3
  76.9 0.6 convolution_convert_fusion.1
  78.2 0.6 fusion.4
  79.5 0.9 collective-permute-start.8
  81.0 2.1 %collective-permute-start.9 = (f32[8,16]{1,0:T(8,128)S(1)}, f32[8,16]{1,0:T(8,128)S(1)}, u32[]{:S(2)}, u32[]{:S(2)}) collective-permute-start(f32[8,16]{1,0:T(8,128)S(1)} %bitcast.49), channel_id=1, source_target_pairs={{0,16},{16,0},{1,17},{17,1},{2,18},{18,2},{3,19},{19,3},{4,20},{20... | collective-permute-start | bytes 1544 | tf_op jit(solution)/shard_map/ppermute | solution.py:241
  83.1 2.4 %gather_blocks.1 = bf16[2,2,2,2,64,768]{5,4,3,2,1,0:T(8,128)(2,1)S(1)} custom-call(s32[1]{0:T(128)} %bitcast.20.level, s32[1]{0:T(128)} %bitcast.15.plane, s32[1]{0:T(128)} %bitcast.1.core, bf16[4,64,768]{2,1,0:T(8,128)(2,1)S(1)} %get-tuple-element.32.refs_0_, bf16[4,64,768]{2,1,0:T(8,128)(2,1)S(1)} %collective-permute-done.13.refs_1_, ...), custom_call_target="tpu_custom_call" | custom-call | tf_op jit(solution)/shard_map/gather_blocks/pallas_call | solution.py:179
  85.5 6.3 %collective-permute-done.9 = f32[8,16]{1,0:T(8,128)S(1)} collective-permute-done((f32[8,16]{1,0:T(8,128)S(1)}, f32[8,16]{1,0:T(8,128)S(1)}, u32[]{:S(2)}, u32[]{:S(2)}) %collective-permute-start.9) | collective-permute-done | bytes 544 | tf_op jit(solution)/shard_map/ppermute | solution.py:241
  91.9 1.4 %convolution_convert_fusion = bf16[256,1024]{1,0:T(8,128)(2,1)} fusion(bf16[256,768]{1,0:T(8,128)(2,1)S(1)} %maximum_select_fusion, bf16[1024,768]{1,0:T(8,128)(2,1)S(1)} %bitcast.37), kind=kOutput, calls=%fused_computation | convolution fusion | flops 402915328 | bytes 2490368 | tf_op jit(solution)/shard_map/dot_general | solution.py:246
  93.3 3.5 %all-to-all-start.1 = ((bf16[8,32,1024]{2,1,0:T(8,128)(2,1)}), bf16[8,32,1024]{2,1,0:T(8,128)(2,1)S(1)}, u32[]{:S(2)}, u32[]{:S(2)}) async-start(bf16[8,32,1024]{2,1,0:T(8,128)(2,1)} %bitcast.22), calls=%async_computation.1 | async-start | bytes 1048576 | tf_op jit(solution)/shard_map/all_to_all | solution.py:52
  96.9 8.7 %all-to-all-done.1 = bf16[8,32,1024]{2,1,0:T(8,128)(2,1)S(1)} async-done(((bf16[8,32,1024]{2,1,0:T(8,128)(2,1)}), bf16[8,32,1024]{2,1,0:T(8,128)(2,1)S(1)}, u32[]{:S(2)}, u32[]{:S(2)}) %all-to-all-start.1) | async-done | bytes 524320 | tf_op jit(solution)/shard_map/all_to_all | solution.py:52
  105.8 1.1 %collective-permute-start.16 = (bf16[16,1024]{1,0:T(8,128)(2,1)S(1)}, bf16[16,1024]{1,0:T(8,128)(2,1)S(1)}, u32[]{:S(2)}, u32[]{:S(2)}) collective-permute-start(bf16[16,1024]{1,0:T(8,128)(2,1)S(1)} %get-tuple-element.48), channel_id=1, source_target_pairs={{0,16},{16,0},{1,17},{17,1},{2,18},{18,2},{3,19},{19,3},{4,20},{20... | collective-permute-start | bytes 98312 | tf_op jit(solution)/shard_map/ppermute | solution.py:252
  106.9 3.7 %collective-permute-done.16.other = bf16[16,1024]{1,0:T(8,128)(2,1)S(1)} collective-permute-done((bf16[16,1024]{1,0:T(8,128)(2,1)S(1)}, bf16[16,1024]{1,0:T(8,128)(2,1)S(1)}, u32[]{:S(2)}, u32[]{:S(2)}) %collective-permute-start.16) | collective-permute-done | bytes 32800 | tf_op jit(solution)/shard_map/ppermute | solution.py:252
  110.7 0.6 assemble.1
  (48 shorter events, 3.4 us)
Async XLA Ops:
  2.7 53.3 %copy-start.1 = (bf16[2,64,768]{2,1,0:T(8,128)(2,1)S(1)}, bf16[2,64,768]{2,1,0:T(8,128)(2,1)}, u32[]{:S(2)}) copy-start(bf16[2,64,768]{2,1,0:T(8,128)(2,1)} %get-tuple-element.28) | copy-start | bytes 589828
  2.8 74.2 %all-to-all-start = ((bf16[16,64,768]{2,1,0:T(8,128)(2,1)}), bf16[16,64,768]{2,1,0:T(8,128)(2,1)S(1)}, u32[]{:S(2)}, u32[]{:S(2)}) async-start(bf16[16,64,768]{2,1,0:T(8,128)(2,1)} %bitcast.41), calls=%async_computation | async-start | bytes 3145728 | tf_op jit(solution)/shard_map/all_to_all | solution.py:52
  12.9 3.1 %collective-permute-start.1 = (bf16[16,1024]{1,0:T(8,128)(2,1)}, bf16[16,1024]{1,0:T(8,128)(2,1)S(1)}, u32[]{:S(2)}, u32[]{:S(2)}) collective-permute-start(bf16[16,1024]{1,0:T(8,128)(2,1)} %get-tuple-element.21), channel_id=1, source_target_pairs={{0,2},{2,0},{1,3},{3,1},{4,6},{6,4},{5,7},{7,5},{8,10},{10,8},{9,1... | collective-permute-start | bytes 98312 | tf_op jit(solution)/shard_map/ppermute | solution.py:218
  13.0 36.3 %collective-permute-start.2 = (bf16[16,1024]{1,0:T(8,128)(2,1)}, bf16[16,1024]{1,0:T(8,128)(2,1)S(1)}, u32[]{:S(2)}, u32[]{:S(2)}) collective-permute-start(bf16[16,1024]{1,0:T(8,128)(2,1)} %get-tuple-element.21), channel_id=1, source_target_pairs={{0,18},{2,16},{16,2},{18,0},{1,19},{3,17},{17,3},{19,1},{4,22},{6,... | collective-permute-start | bytes 98312 | tf_op jit(solution)/shard_map/ppermute | solution.py:220
  15.9 35.1 %collective-permute-start = (bf16[16,1024]{1,0:T(8,128)(2,1)}, bf16[16,1024]{1,0:T(8,128)(2,1)S(1)}, u32[]{:S(2)}, u32[]{:S(2)}) collective-permute-start(bf16[16,1024]{1,0:T(8,128)(2,1)} %get-tuple-element.20), channel_id=1, source_target_pairs={{0,16},{16,0},{1,17},{17,1},{2,18},{18,2},{3,19},{19,3},{4,20},{20... | collective-permute-start | bytes 98312 | tf_op jit(solution)/shard_map/ppermute | solution.py:219
  51.9 5.0 %collective-permute-start.3 = (bf16[2,32,1024]{2,1,0:T(8,128)(2,1)S(1)}, bf16[2,32,1024]{2,1,0:T(8,128)(2,1)S(1)}, u32[]{:S(2)}, u32[]{:S(2)}) collective-permute-start(bf16[2,32,1024]{2,1,0:T(8,128)(2,1)S(1)} %get-tuple-element.47), channel_id=1, source_target_pairs={{0,8},{8,0},{1,9},{9,1},{2,10},{10,2},{3,11},{11,3},{4,12},{12,4},... | collective-permute-start | bytes 393224 | tf_op jit(solution)/shard_map/ppermute | solution.py:222
  52.0 8.9 %collective-permute-start.10 = (bf16[2,64,768]{2,1,0:T(8,128)(2,1)}, bf16[2,64,768]{2,1,0:T(8,128)(2,1)S(1)}, u32[]{:S(2)}, u32[]{:S(2)}) collective-permute-start(bf16[2,64,768]{2,1,0:T(8,128)(2,1)} %get-tuple-element.29), channel_id=1, source_target_pairs={{0,1},{1,0},{4,5},{5,4},{2,3},{3,2},{6,7},{7,6},{8,9},{9,8},{12,13... | collective-permute-start | bytes 589832 | tf_op jit(solution)/shard_map/ppermute | solution.py:210
  53.5 11.6 %collective-permute-start.11 = (bf16[2,64,768]{2,1,0:T(8,128)(2,1)}, bf16[2,64,768]{2,1,0:T(8,128)(2,1)S(1)}, u32[]{:S(2)}, u32[]{:S(2)}) collective-permute-start(bf16[2,64,768]{2,1,0:T(8,128)(2,1)} %get-tuple-element.30), channel_id=1, source_target_pairs={{0,4},{1,5},{4,0},{5,1},{2,6},{3,7},{6,2},{7,3},{8,12},{9,13},{12,... | collective-permute-start | bytes 589832 | tf_op jit(solution)/shard_map/ppermute | solution.py:210
  55.6 10.6 %collective-permute-start.12 = (bf16[2,64,768]{2,1,0:T(8,128)(2,1)}, bf16[2,64,768]{2,1,0:T(8,128)(2,1)S(1)}, u32[]{:S(2)}, u32[]{:S(2)}) collective-permute-start(bf16[2,64,768]{2,1,0:T(8,128)(2,1)} %get-tuple-element.31), channel_id=1, source_target_pairs={{0,5},{1,4},{4,1},{5,0},{2,7},{3,6},{6,3},{7,2},{8,13},{9,12},{12,... | collective-permute-start | bytes 589832 | tf_op jit(solution)/shard_map/ppermute | solution.py:210
  56.9 12.9 %collective-permute-start.4 = (bf16[2,2,32,1024]{3,2,0,1:T(8,128)(2,1)S(1)}, bf16[2,2,32,1024]{3,2,0,1:T(8,128)(2,1)S(1)}, u32[]{:S(2)}, u32[]{:S(2)}) collective-permute-start(bf16[2,2,32,1024]{3,2,0,1:T(8,128)(2,1)S(1)} %maximum_select_fusion.2), channel_id=1, source_target_pairs={{0,1},{1,0},{4,5},{5,4},{2,3},{3,2},{6,7},{7,6},{8,9},{9,8},{12,13... | collective-permute-start | bytes 786440 | tf_op jit(solution)/shard_map/ppermute | solution.py:227
  58.5 16.4 %collective-permute-start.5 = (bf16[2,2,32,1024]{3,2,0,1:T(8,128)(2,1)S(1)}, bf16[2,2,32,1024]{3,2,0,1:T(8,128)(2,1)S(1)}, u32[]{:S(2)}, u32[]{:S(2)}) collective-permute-start(bf16[2,2,32,1024]{3,2,0,1:T(8,128)(2,1)S(1)} %maximum_select_fusion.2), channel_id=1, source_target_pairs={{0,4},{1,5},{4,0},{5,1},{2,6},{3,7},{6,2},{7,3},{8,12},{9,13},{12,... | collective-permute-start | bytes 786440 | tf_op jit(solution)/shard_map/ppermute | solution.py:227
  60.8 15.2 %collective-permute-start.6 = (bf16[2,2,32,1024]{3,2,0,1:T(8,128)(2,1)S(1)}, bf16[2,2,32,1024]{3,2,0,1:T(8,128)(2,1)S(1)}, u32[]{:S(2)}, u32[]{:S(2)}) collective-permute-start(bf16[2,2,32,1024]{3,2,0,1:T(8,128)(2,1)S(1)} %maximum_select_fusion.2), channel_id=1, source_target_pairs={{0,5},{1,4},{4,1},{5,0},{2,7},{3,6},{6,3},{7,2},{8,13},{9,12},{12,... | collective-permute-start | bytes 786440 | tf_op jit(solution)/shard_map/ppermute | solution.py:227
  66.4 11.7 %collective-permute-start.13 = (bf16[4,64,768]{2,1,0:T(8,128)(2,1)S(1)}, bf16[4,64,768]{2,1,0:T(8,128)(2,1)S(1)}, u32[]{:S(2)}, u32[]{:S(2)}) collective-permute-start(bf16[4,64,768]{2,1,0:T(8,128)(2,1)S(1)} %get-tuple-element.33), channel_id=1, source_target_pairs={{0,8},{8,0},{1,9},{9,1},{2,10},{10,2},{3,11},{11,3},{4,12},{12,4},... | collective-permute-start | bytes 1179656 | tf_op jit(solution)/shard_map/ppermute | solution.py:214
  76.9 1.2 %copy-start = (bf16[1,2,4,32,1024]{4,3,2,1,0:T(8,128)(2,1)S(1)}, bf16[1,2,4,32,1024]{4,3,2,1,0:T(8,128)(2,1)}, u32[]{:S(2)}) copy-start(bf16[1,2,4,32,1024]{4,3,2,1,0:T(8,128)(2,1)} %get-tuple-element.36) | copy-start | bytes 1572868
  77.5 1.8 %collective-permute-start.7 = (bf16[256,768]{1,0:T(8,128)(2,1)S(1)}, bf16[256,768]{1,0:T(8,128)(2,1)S(1)}, u32[]{:S(2)}, u32[]{:S(2)}) collective-permute-start(bf16[256,768]{1,0:T(8,128)(2,1)S(1)} %convolution_convert_fusion.1), channel_id=1, source_target_pairs={{0,2},{2,0},{1,3},{3,1},{4,6},{6,4},{5,7},{7,5},{8,10},{10,8},{9,1... | collective-permute-start | bytes 1179656 | tf_op jit(solution)/shard_map/ppermute | solution.py:233
  77.6 5.6 %collective-permute-start.14 = (bf16[4,64,768]{2,1,0:T(8,128)(2,1)S(1)}, bf16[4,64,768]{2,1,0:T(8,128)(2,1)S(1)}, u32[]{:S(2)}, u32[]{:S(2)}) collective-permute-start(bf16[4,64,768]{2,1,0:T(8,128)(2,1)S(1)} %get-tuple-element.32.refs_0_), channel_id=1, source_target_pairs={{0,2},{2,0},{1,3},{3,1},{4,6},{6,4},{5,7},{7,5},{8,10},{10,8},{9,1... | collective-permute-start | bytes 1179656 | tf_op jit(solution)/shard_map/ppermute | solution.py:215
  78.1 5.1 %collective-permute-start.15 = (bf16[4,64,768]{2,1,0:T(8,128)(2,1)S(1)}, bf16[4,64,768]{2,1,0:T(8,128)(2,1)S(1)}, u32[]{:S(2)}, u32[]{:S(2)}) collective-permute-start(bf16[4,64,768]{2,1,0:T(8,128)(2,1)S(1)} %collective-permute-done.13.refs_1_), channel_id=1, source_target_pairs={{0,2},{2,0},{1,3},{3,1},{4,6},{6,4},{5,7},{7,5},{8,10},{10,8},{9,1... | collective-permute-start | bytes 1179656 | tf_op jit(solution)/shard_map/ppermute | solution.py:215
  78.7 1.7 %copy-start.2 = (s32[16,8]{0,1:T(8,128)S(1)}, s32[16,8]{0,1:T(8,128)}, u32[]{:S(2)}) copy-start(s32[16,8]{0,1:T(8,128)} %param.10) | copy-start | bytes 1540
  78.7 1.7 %copy-start.4 = (s32[16]{0:T(128)S(1)}, s32[16]{0:T(128)}, u32[]{:S(2)}) copy-start(s32[16]{0:T(128)} %param.9) | copy-start | bytes 196
  78.8 2.2 %copy-start.3 = (f32[16,8]{0,1:T(8,128)S(1)}, f32[16,8]{0,1:T(8,128)}, u32[]{:S(2)}) copy-start(f32[16,8]{0,1:T(8,128)} %param.11) | copy-start | bytes 1540
  79.5 12.3 %collective-permute-start.8 = (bf16[256,384]{1,0:T(8,128)(2,1)S(1)}, bf16[256,384]{1,0:T(8,128)(2,1)S(1)}, u32[]{:S(2)}, u32[]{:S(2)}) collective-permute-start(bf16[256,384]{1,0:T(8,128)(2,1)S(1)} %fusion), channel_id=1, source_target_pairs={{0,16},{16,0},{1,17},{17,1},{2,18},{18,2},{3,19},{19,3},{4,20},{20... | collective-permute-start | bytes 589832 | tf_op jit(solution)/shard_map/ppermute | solution.py:238
  81.0 10.8 %collective-permute-start.9 = (f32[8,16]{1,0:T(8,128)S(1)}, f32[8,16]{1,0:T(8,128)S(1)}, u32[]{:S(2)}, u32[]{:S(2)}) collective-permute-start(f32[8,16]{1,0:T(8,128)S(1)} %bitcast.49), channel_id=1, source_target_pairs={{0,16},{16,0},{1,17},{17,1},{2,18},{18,2},{3,19},{19,3},{4,20},{20... | collective-permute-start | bytes 1544 | tf_op jit(solution)/shard_map/ppermute | solution.py:241
  93.3 12.3 %all-to-all-start.1 = ((bf16[8,32,1024]{2,1,0:T(8,128)(2,1)}), bf16[8,32,1024]{2,1,0:T(8,128)(2,1)S(1)}, u32[]{:S(2)}, u32[]{:S(2)}) async-start(bf16[8,32,1024]{2,1,0:T(8,128)(2,1)} %bitcast.22), calls=%async_computation.1 | async-start | bytes 1048576 | tf_op jit(solution)/shard_map/all_to_all | solution.py:52
  105.8 4.9 %collective-permute-start.16 = (bf16[16,1024]{1,0:T(8,128)(2,1)S(1)}, bf16[16,1024]{1,0:T(8,128)(2,1)S(1)}, u32[]{:S(2)}, u32[]{:S(2)}) collective-permute-start(bf16[16,1024]{1,0:T(8,128)(2,1)S(1)} %get-tuple-element.48), channel_id=1, source_target_pairs={{0,16},{16,0},{1,17},{17,1},{2,18},{18,2},{3,19},{19,3},{4,20},{20... | collective-permute-start | bytes 98312 | tf_op jit(solution)/shard_map/ppermute | solution.py:252

commit v8 on v7

--- a/solution.py
+++ b/solution.py
@@ -19,11 +19,11 @@
     )
 
 
-def slot_coefficients(slot_expert, pair_slots, combine_weights, experts):
+def slot_coefficients(slot_expert, pair_slots, combine_weights, experts, chip):
     slots = jnp.arange(slot_expert.shape[0], dtype=jnp.int32)
     held = slot_expert[None, None, :]
     chosen = jnp.sum(jnp.where(pair_slots[:, :, None] == slots[None, None, :], held, 0), axis=2)
-    numbers = jnp.arange(experts, dtype=jnp.int32)
+    numbers = jnp.arange(experts, dtype=jnp.int32) ^ chip
     weights = combine_weights[:, :, None]
     return jnp.sum(jnp.where(chosen[:, :, None] == numbers[None, None, :], weights, 0.0), axis=1)
 
@@ -195,6 +195,7 @@
     chip_axes = ("z", "y", "x")
     chips = experts
     h, c = lax.axis_index("h"), lax.axis_index("c")
+    chip = lax.axis_index(chip_axes)
     group = lax.axis_size("x") * own_rows
     groups = width // (2 * group)
 
@@ -219,13 +220,12 @@
     from_h = lax.ppermute(keep, "h", SWAP)
     from_hc = lax.ppermute(give, ("h", "c"), CROSS)
     near = jnp.stack([in_order(h, keep, from_h, 0), in_order(h, from_c, from_hc, 0)])
-    column = in_order(z, near[:, None], lax.ppermute(near, "z", SWAP)[:, None], 1)
-    rows = jnp.zeros((2, 2, chips // 2, 2 * token_count, width // 2), near.dtype)
-    rows = lax.dynamic_update_slice(rows, column[:, :, None], (0, 0, plane, 0, 0))
-    for step in range(1, chips // 2):
-        pairs = [(i, i ^ step) for i in range(chips // 2)]
-        arrived = lax.ppermute(column, ("y", "x"), pairs)
-        rows = lax.dynamic_update_slice(rows, arrived[:, :, None], (0, 0, plane ^ step, 0, 0))
+    column = jnp.stack([near, lax.ppermute(near, "z", SWAP)], axis=1)
+    rows = [column]
+    for step in range(1, places):
+        pairs = [(i, i ^ step) for i in range(places)]
+        rows.append(lax.ppermute(column, ("y", "x"), pairs))
+    rows = jnp.stack(rows, axis=2)
     count = chips * token_count
     rows = rows.reshape(2, 1, 2 * count, width // 2)
 
@@ -237,7 +237,7 @@
     hidden = (jax.nn.silu(pre[:, :part]) * pre[:, part:]).astype(jnp.bfloat16)
     far = lax.ppermute(hidden, "h", SWAP)
     hidden, pair_slots = lax.optimization_barrier((hidden, pair_slots))
-    coefficient = slot_coefficients(slot_expert, pair_slots, combine_weights, experts).T
+    coefficient = slot_coefficients(slot_expert, pair_slots, combine_weights, experts, chip).T
     far_weights = lax.ppermute(coefficient, "h", SWAP)
     far, far_weights = lax.optimization_barrier((far, far_weights))
     coefficient = in_order(h, coefficient, far_weights, 1)
@@ -245,8 +245,12 @@
     hidden = lax.optimization_barrier(hidden)
     result = lax.dot_general(hidden, down, (((1,), (1,)), ((), ())), preferred_element_type=jnp.float32)
     result = result.astype(jnp.bfloat16).reshape(chips, 2 * token_count, width // 2)
-    returned = exchange(result, chip_axes).astype(jnp.float32)
-    mixed = jnp.sum(returned * coefficient[:, :, None], axis=0).astype(jnp.bfloat16)
+    returned = [result[0]]
+    for step in range(1, chips):
+        pairs = [(i, i ^ step) for i in range(chips)]
+        returned.append(lax.ppermute(result[step], chip_axes, pairs))
+    terms = [block.astype(jnp.float32) * coefficient[at][:, None] for at, block in enumerate(returned)]
+    mixed = sum(terms).astype(jnp.bfloat16)
     low, high = mixed[:token_count], mixed[token_count:]
     mine, sent = jnp.where(h == 0, low, high), jnp.where(h == 0, high, low)
     return assemble(h, mine, lax.ppermute(sent, "h", SWAP))

time: 112 us -> 112 us (level)
  waiting for transfers between devices: 65.9 us -> 58.2 us
  starting transfers between devices: 31.9 us -> 38.8 us
    ppermute x1, waiting for transfers between devices: 33.3 us -> 0.01 us  [dense_layer(): from_hc = lax.ppermute(give, ('h', 'c'), CROSS)]
    ppermute x1, waiting for transfers between devices: 1.69 us -> 34.7 us  [dense_layer(): from_h = lax.ppermute(keep, 'h', SWAP)]
    ppermute x4 -> x11, starting transfers between devices: 6 us -> 15.4 us  [the longest x7 9.41 us: dense_layer(): returned.append(lax.ppermute(result[step], chip_axes, pairs))]
    all_to_all x2 -> x1, waiting for transfers between devices: 8.7 us -> 0.01 us  [exchange(): return lax.all_to_all(value, axes, 0, 0, tiled=True)]
    all_to_all x2 -> x1, starting transfers between devices: 12 us -> 8.48 us  [exchange(): return lax.all_to_all(value, axes, 0, 0, tiled=True)]
    ppermute x1, starting transfers between devices: 0.1 us -> 2.89 us  [dense_layer(): from_h = lax.ppermute(keep, 'h', SWAP)]
    ppermute x1, starting transfers between devices: 2.92 us -> 0.22 us  [dense_layer(): from_hc = lax.ppermute(give, ('h', 'c'), CROSS)]
    ppermute x4 -> x11, waiting for transfers between devices: 8.48 us -> 10.9 us  [the longest x3 6.73 us: dense_layer(): rows.append(lax.ppermute(column, ('y', 'x'), pairs))]
  transfers between devices with their start and end apart: 19 -> 25, of which waited for: 12 -> 13; matrix products, arithmetic and copies ran while one was open for 4% -> 5% of each run, Pallas kernels for 4% -> 4%
where the time goes in v8:
time: 112 us
  waiting for transfers between devices  58.2 us (52%)
  starting transfers between devices  38.8 us (35%)
  Pallas kernels  7.34 us (7%)
  other arithmetic  2.96 us (3%)
  matrix products  2.78 us (2%)
  local copies, waits for them, and re-layouts  1.27 us (1%)
    ppermute x1, waiting for transfers between devices, dense_layer(): from_h = lax.ppermute(keep, 'h', SWAP)  34.7 us
    ppermute x7, starting transfers between devices, dense_layer(): returned.append(lax.ppermute(result[step], chip_axes, pairs))  9.41 us
    all_to_all x1, starting transfers between devices, exchange(): return lax.all_to_all(value, axes, 0, 0, tiled=True)  8.48 us
    ppermute x3, waiting for transfers between devices, dense_layer(): rows.append(lax.ppermute(column, ('y', 'x'), pairs))  6.73 us
    ppermute x1, waiting for transfers between devices, dense_layer(): far_weights = lax.ppermute(coefficient, 'h', SWAP)  6.27 us
    ppermute x3, starting transfers between devices, dense_layer(): rows.append(lax.ppermute(column, ('y', 'x'), pairs))  5.9 us
    ppermute x3, starting transfers between devices, dense_layer(): blocks[step] = lax.ppermute(blocks[step], ('y', 'x'), pairs)  4.13 us
    ppermute x7, waiting for transfers between devices, dense_layer(): returned.append(lax.ppermute(result[step], chip_axes, pairs))  3.42 us
  transfers between devices with their start and end apart: 25, of which 13 were waited for; matrix products, arithmetic and copies ran while one was open for 5% of the time, Pallas kernels for 4%

profile of v8, /device:TPU:0, one launch (start us, length us, event | category | flops | bytes accessed | tf_op | source)
XLA Modules:
  0.0 111.7 jit_solution(9963590633920989174)
XLA Ops:
  0.0 2.7 %pack.1 = (bf16[2,8,64,768]{3,2,1,0:T(8,128)(2,1)}, bf16[2,64,768]{2,1,0:T(8,128)(2,1)}, bf16[2,64,768]{2,1,0:T(8,128)(2,1)}, bf16[2,64,768]{2,1,0:T(8,128)(2,1)}, bf16[2,64,768]{2,1,0:T(8,128)(2,1)}) custom-call(s32[1]{0:T(128)} %bitcast.14.plane, bf16[8,64,2304]{2,1,0:T(8,128)(2,1)} %weights.1), custom_call_target="tpu_custom_call" | custom-call | tf_op jit(solution)/shard_map/pack/pallas_call | solution.py:147
  2.8 8.5 %all-to-all-start = ((bf16[16,64,768]{2,1,0:T(8,128)(2,1)}), bf16[16,64,768]{2,1,0:T(8,128)(2,1)S(1)}, u32[]{:S(2)}, u32[]{:S(2)}) async-start(bf16[16,64,768]{2,1,0:T(8,128)(2,1)} %bitcast.49), calls=%async_computation | async-start | bytes 3145728 | tf_op jit(solution)/shard_map/all_to_all | solution.py:52
  11.3 1.6 %normalize.1 = (bf16[16,1024]{1,0:T(8,128)(2,1)}, bf16[16,1024]{1,0:T(8,128)(2,1)}) custom-call(s32[1]{0:T(128)} %bitcast.1.core, bf16[16,2048]{1,0:T(8,128)(2,1)} %all_tokens.1, f32[1,2048]{1,0:T(1,128)} %bitcast.61), custom_call_target="tpu_custom_call" | custom-call | tf_op jit(solution)/shard_map/normalize/pallas_call | solution.py:125
  12.9 2.9 %collective-permute-start = (bf16[16,1024]{1,0:T(8,128)(2,1)}, bf16[16,1024]{1,0:T(8,128)(2,1)S(1)}, u32[]{:S(2)}, u32[]{:S(2)}) collective-permute-start(bf16[16,1024]{1,0:T(8,128)(2,1)} %get-tuple-element.20), channel_id=1, source_target_pairs={{0,16},{16,0},{1,17},{17,1},{2,18},{18,2},{3,19},{19,3},{4,20},{20... | collective-permute-start | bytes 98312 | tf_op jit(solution)/shard_map/ppermute | solution.py:220
  16.0 34.7 %collective-permute-done = bf16[16,1024]{1,0:T(8,128)(2,1)S(1)} collective-permute-done((bf16[16,1024]{1,0:T(8,128)(2,1)}, bf16[16,1024]{1,0:T(8,128)(2,1)S(1)}, u32[]{:S(2)}, u32[]{:S(2)}) %collective-permute-start) | collective-permute-done | bytes 32800 | tf_op jit(solution)/shard_map/ppermute | solution.py:220
  50.7 0.8 maximum_select_fusion.1
  51.7 1.5 %collective-permute-start.10 = (bf16[2,64,768]{2,1,0:T(8,128)(2,1)S(1)}, bf16[2,64,768]{2,1,0:T(8,128)(2,1)S(1)}, u32[]{:S(2)}, u32[]{:S(2)}) collective-permute-start(bf16[2,64,768]{2,1,0:T(8,128)(2,1)S(1)} %copy-done.6), channel_id=1, source_target_pairs={{0,1},{1,0},{4,5},{5,4},{2,3},{3,2},{6,7},{7,6},{8,9},{9,8},{12,13... | collective-permute-start | bytes 589832 | tf_op jit(solution)/shard_map/ppermute | solution.py:211
  53.2 2.2 %collective-permute-start.11 = (bf16[2,64,768]{2,1,0:T(8,128)(2,1)S(1)}, bf16[2,64,768]{2,1,0:T(8,128)(2,1)S(1)}, u32[]{:S(2)}, u32[]{:S(2)}) collective-permute-start(bf16[2,64,768]{2,1,0:T(8,128)(2,1)S(1)} %copy-done.5), channel_id=1, source_target_pairs={{0,4},{1,5},{4,0},{5,1},{2,6},{3,7},{6,2},{7,3},{8,12},{9,13},{12,... | collective-permute-start | bytes 589832 | tf_op jit(solution)/shard_map/ppermute | solution.py:211
  56.7 1.5 %collective-permute-start.4 = (bf16[2,2,32,1024]{3,2,0,1:T(8,128)(2,1)S(1)}, bf16[2,2,32,1024]{3,2,0,1:T(8,128)(2,1)S(1)}, u32[]{:S(2)}, u32[]{:S(2)}) collective-permute-start(bf16[2,2,32,1024]{3,2,0,1:T(8,128)(2,1)S(1)} %get-tuple-element.45), channel_id=1, source_target_pairs={{0,1},{1,0},{4,5},{5,4},{2,3},{3,2},{6,7},{7,6},{8,9},{9,8},{12,13... | collective-permute-start | bytes 786440 | tf_op jit(solution)/shard_map/ppermute | solution.py:227
  58.2 2.2 %collective-permute-start.5 = (bf16[2,2,32,1024]{3,2,0,1:T(8,128)(2,1)S(1)}, bf16[2,2,32,1024]{3,2,0,1:T(8,128)(2,1)S(1)}, u32[]{:S(2)}, u32[]{:S(2)}) collective-permute-start(bf16[2,2,32,1024]{3,2,0,1:T(8,128)(2,1)S(1)} %get-tuple-element.45), channel_id=1, source_target_pairs={{0,4},{1,5},{4,0},{5,1},{2,6},{3,7},{6,2},{7,3},{8,12},{9,13},{12,... | collective-permute-start | bytes 786440 | tf_op jit(solution)/shard_map/ppermute | solution.py:227
  60.3 2.2 %collective-permute-start.6 = (bf16[2,2,32,1024]{3,2,0,1:T(8,128)(2,1)S(1)}, bf16[2,2,32,1024]{3,2,0,1:T(8,128)(2,1)S(1)}, u32[]{:S(2)}, u32[]{:S(2)}) collective-permute-start(bf16[2,2,32,1024]{3,2,0,1:T(8,128)(2,1)S(1)} %get-tuple-element.45), channel_id=1, source_target_pairs={{0,5},{1,4},{4,1},{5,0},{2,7},{3,6},{6,3},{7,2},{8,13},{9,12},{12,... | collective-permute-start | bytes 786440 | tf_op jit(solution)/shard_map/ppermute | solution.py:227
  62.6 1.8 %collective-permute-done.11 = bf16[2,64,768]{2,1,0:T(8,128)(2,1)S(1)} collective-permute-done((bf16[2,64,768]{2,1,0:T(8,128)(2,1)S(1)}, bf16[2,64,768]{2,1,0:T(8,128)(2,1)S(1)}, u32[]{:S(2)}, u32[]{:S(2)}) %collective-permute-start.11) | collective-permute-done | bytes 196640 | tf_op jit(solution)/shard_map/ppermute | solution.py:211
  64.4 1.3 %collective-permute-done.12 = bf16[2,64,768]{2,1,0:T(8,128)(2,1)S(1)} collective-permute-done((bf16[2,64,768]{2,1,0:T(8,128)(2,1)S(1)}, bf16[2,64,768]{2,1,0:T(8,128)(2,1)S(1)}, u32[]{:S(2)}, u32[]{:S(2)}) %collective-permute-start.12) | collective-permute-done | bytes 196640 | tf_op jit(solution)/shard_map/ppermute | solution.py:211
  65.7 0.9 pad_maximum_fusion.1
  66.6 1.9 %collective-permute-start.13 = (bf16[4,64,768]{2,1,0:T(8,128)(2,1)}, bf16[4,64,768]{2,1,0:T(8,128)(2,1)S(1)}, u32[]{:S(2)}, u32[]{:S(2)}) collective-permute-start(bf16[4,64,768]{2,1,0:T(8,128)(2,1)} %get-tuple-element.33), channel_id=1, source_target_pairs={{0,8},{8,0},{1,9},{9,1},{2,10},{10,2},{3,11},{11,3},{4,12},{12,4},... | collective-permute-start | bytes 1179656 | tf_op jit(solution)/shard_map/ppermute | solution.py:215
  69.1 5.1 %collective-permute-done.5 = bf16[2,2,32,1024]{3,2,0,1:T(8,128)(2,1)S(1)} collective-permute-done((bf16[2,2,32,1024]{3,2,0,1:T(8,128)(2,1)S(1)}, bf16[2,2,32,1024]{3,2,0,1:T(8,128)(2,1)S(1)}, u32[]{:S(2)}, u32[]{:S(2)}) %collective-permute-start.5) | collective-permute-done | bytes 262176 | tf_op jit(solution)/shard_map/ppermute | solution.py:227
  74.1 1.1 collective-permute-done.6
  75.5 0.9 copy.14
  76.4 1.6 %convolution_convert_fusion.1 = bf16[256,768]{1,0:T(8,128)(2,1)S(1)} fusion(bf16[256,1024]{1,0:T(8,128)(2,1)} %bitcast.50, bf16[1024,768]{1,0:T(8,128)(2,1)S(1)} %bitcast.46), kind=kOutput, calls=%fused_computation.1 | convolution fusion | flops 402849792 | bytes 2490368 | tf_op jit(solution)/shard_map/dot_general | solution.py:232
  80.0 1.0 collective-permute-start.8
  81.7 2.0 %collective-permute-start.9 = (f32[8,16]{1,0:T(8,128)S(1)}, f32[8,16]{1,0:T(8,128)S(1)}, u32[]{:S(2)}, u32[]{:S(2)}) collective-permute-start(f32[8,16]{1,0:T(8,128)S(1)} %bitcast.59), channel_id=1, source_target_pairs={{0,16},{16,0},{1,17},{17,1},{2,18},{18,2},{3,19},{19,3},{4,20},{20... | collective-permute-start | bytes 1544 | tf_op jit(solution)/shard_map/ppermute | solution.py:241
  83.6 2.4 %gather_blocks.1 = bf16[2,2,2,2,64,768]{5,4,3,2,1,0:T(8,128)(2,1)S(1)} custom-call(s32[1]{0:T(128)} %bitcast.19.level, s32[1]{0:T(128)} %bitcast.14.plane, s32[1]{0:T(128)} %bitcast.1.core, bf16[4,64,768]{2,1,0:T(8,128)(2,1)S(1)} %get-tuple-element.32.refs_0_, bf16[4,64,768]{2,1,0:T(8,128)(2,1)S(1)} %collective-permute-done.13.refs_1_, ...), custom_call_target="tpu_custom_call" | custom-call | tf_op jit(solution)/shard_map/gather_blocks/pallas_call | solution.py:179
  86.0 6.3 %collective-permute-done.9 = f32[8,16]{1,0:T(8,128)S(1)} collective-permute-done((f32[8,16]{1,0:T(8,128)S(1)}, f32[8,16]{1,0:T(8,128)S(1)}, u32[]{:S(2)}, u32[]{:S(2)}) %collective-permute-start.9) | collective-permute-done | bytes 544 | tf_op jit(solution)/shard_map/ppermute | solution.py:241
  93.0 1.1 %collective-permute-start.16 = (bf16[32,1024]{1,0:T(8,128)(2,1)S(1)}, bf16[32,1024]{1,0:T(8,128)(2,1)S(1)}, u32[]{:S(2)}, u32[]{:S(2)}) collective-permute-start(bf16[32,1024]{1,0:T(8,128)(2,1)S(1)} %get-tuple-element.37), channel_id=1, source_target_pairs={{0,1},{1,0},{4,5},{5,4},{8,9},{9,8},{12,13},{13,12},{2,3},{3,2},{6... | collective-permute-start | bytes 196616 | tf_op jit(solution)/shard_map/ppermute | solution.py:251
  94.2 1.2 %collective-permute-start.17 = (bf16[32,1024]{1,0:T(8,128)(2,1)S(1)}, bf16[32,1024]{1,0:T(8,128)(2,1)S(1)}, u32[]{:S(2)}, u32[]{:S(2)}) collective-permute-start(bf16[32,1024]{1,0:T(8,128)(2,1)S(1)} %get-tuple-element.43), channel_id=1, source_target_pairs={{0,4},{1,5},{4,0},{5,1},{8,12},{9,13},{12,8},{13,9},{2,6},{3,7},{6... | collective-permute-start | bytes 196616 | tf_op jit(solution)/shard_map/ppermute | solution.py:251
  95.4 1.2 %collective-permute-start.18 = (bf16[32,1024]{1,0:T(8,128)(2,1)S(1)}, bf16[32,1024]{1,0:T(8,128)(2,1)S(1)}, u32[]{:S(2)}, u32[]{:S(2)}) collective-permute-start(bf16[32,1024]{1,0:T(8,128)(2,1)S(1)} %get-tuple-element.42), channel_id=1, source_target_pairs={{0,5},{1,4},{4,1},{5,0},{8,13},{9,12},{12,9},{13,8},{2,7},{3,6},{6... | collective-permute-start | bytes 196616 | tf_op jit(solution)/shard_map/ppermute | solution.py:251
  96.6 2.5 %collective-permute-start.20 = (bf16[32,1024]{1,0:T(8,128)(2,1)S(1)}, bf16[32,1024]{1,0:T(8,128)(2,1)S(1)}, u32[]{:S(2)}, u32[]{:S(2)}) collective-permute-start(bf16[32,1024]{1,0:T(8,128)(2,1)S(1)} %get-tuple-element.40), channel_id=1, source_target_pairs={{0,9},{1,8},{4,13},{5,12},{8,1},{9,0},{12,5},{13,4},{2,11},{3,10},... | collective-permute-start | bytes 196616 | tf_op jit(solution)/shard_map/ppermute | solution.py:251
  99.9 2.6 %collective-permute-start.22 = (bf16[32,1024]{1,0:T(8,128)(2,1)S(1)}, bf16[32,1024]{1,0:T(8,128)(2,1)S(1)}, u32[]{:S(2)}, u32[]{:S(2)}) collective-permute-start(bf16[32,1024]{1,0:T(8,128)(2,1)S(1)} %get-tuple-element.38), channel_id=1, source_target_pairs={{0,13},{1,12},{4,9},{5,8},{8,5},{9,4},{12,1},{13,0},{2,15},{3,14},... | collective-permute-start | bytes 196616 | tf_op jit(solution)/shard_map/ppermute | solution.py:251
  103.3 1.1 %collective-permute-done.21 = bf16[32,1024]{1,0:T(8,128)(2,1)S(1)} collective-permute-done((bf16[32,1024]{1,0:T(8,128)(2,1)S(1)}, bf16[32,1024]{1,0:T(8,128)(2,1)S(1)}, u32[]{:S(2)}, u32[]{:S(2)}) %collective-permute-start.21) | collective-permute-done | bytes 65568 | tf_op jit(solution)/shard_map/ppermute | solution.py:251
  104.4 1.6 %collective-permute-done.22 = bf16[32,1024]{1,0:T(8,128)(2,1)S(1)} collective-permute-done((bf16[32,1024]{1,0:T(8,128)(2,1)S(1)}, bf16[32,1024]{1,0:T(8,128)(2,1)S(1)}, u32[]{:S(2)}, u32[]{:S(2)}) %collective-permute-start.22) | collective-permute-done | bytes 65568 | tf_op jit(solution)/shard_map/ppermute | solution.py:251
  106.2 2.0 %collective-permute-start.23 = (bf16[16,1024]{1,0:T(8,128)(2,1)S(1)}, bf16[16,1024]{1,0:T(8,128)(2,1)S(1)}, u32[]{:S(2)}, u32[]{:S(2)}) collective-permute-start(bf16[16,1024]{1,0:T(8,128)(2,1)S(1)} %get-tuple-element.56), channel_id=1, source_target_pairs={{0,16},{16,0},{1,17},{17,1},{2,18},{18,2},{3,19},{19,3},{4,20},{20... | collective-permute-start | bytes 98312 | tf_op jit(solution)/shard_map/ppermute | solution.py:256
  108.2 2.9 %collective-permute-done.23.other = bf16[16,1024]{1,0:T(8,128)(2,1)S(1)} collective-permute-done((bf16[16,1024]{1,0:T(8,128)(2,1)S(1)}, bf16[16,1024]{1,0:T(8,128)(2,1)S(1)}, u32[]{:S(2)}, u32[]{:S(2)}) %collective-permute-start.23) | collective-permute-done | bytes 32800 | tf_op jit(solution)/shard_map/ppermute | solution.py:256
  (65 shorter events, 8.0 us)
Async XLA Ops:
  2.7 48.9 %copy-start.6 = (bf16[2,64,768]{2,1,0:T(8,128)(2,1)S(1)}, bf16[2,64,768]{2,1,0:T(8,128)(2,1)}, u32[]{:S(2)}) copy-start(bf16[2,64,768]{2,1,0:T(8,128)(2,1)} %get-tuple-element.29) | copy-start | bytes 589828
  2.8 50.5 %copy-start.5 = (bf16[2,64,768]{2,1,0:T(8,128)(2,1)S(1)}, bf16[2,64,768]{2,1,0:T(8,128)(2,1)}, u32[]{:S(2)}) copy-start(bf16[2,64,768]{2,1,0:T(8,128)(2,1)} %get-tuple-element.30) | copy-start | bytes 589828
  2.8 52.6 %copy-start.4 = (bf16[2,64,768]{2,1,0:T(8,128)(2,1)S(1)}, bf16[2,64,768]{2,1,0:T(8,128)(2,1)}, u32[]{:S(2)}) copy-start(bf16[2,64,768]{2,1,0:T(8,128)(2,1)} %get-tuple-element.31) | copy-start | bytes 589828
  2.8 53.0 %copy-start = (bf16[2,64,768]{2,1,0:T(8,128)(2,1)S(1)}, bf16[2,64,768]{2,1,0:T(8,128)(2,1)}, u32[]{:S(2)}) copy-start(bf16[2,64,768]{2,1,0:T(8,128)(2,1)} %get-tuple-element.28) | copy-start | bytes 589828
  2.8 73.6 %all-to-all-start = ((bf16[16,64,768]{2,1,0:T(8,128)(2,1)}), bf16[16,64,768]{2,1,0:T(8,128)(2,1)S(1)}, u32[]{:S(2)}, u32[]{:S(2)}) async-start(bf16[16,64,768]{2,1,0:T(8,128)(2,1)} %bitcast.49), calls=%async_computation | async-start | bytes 3145728 | tf_op jit(solution)/shard_map/all_to_all | solution.py:52
  12.9 37.8 %collective-permute-start = (bf16[16,1024]{1,0:T(8,128)(2,1)}, bf16[16,1024]{1,0:T(8,128)(2,1)S(1)}, u32[]{:S(2)}, u32[]{:S(2)}) collective-permute-start(bf16[16,1024]{1,0:T(8,128)(2,1)} %get-tuple-element.20), channel_id=1, source_target_pairs={{0,16},{16,0},{1,17},{17,1},{2,18},{18,2},{3,19},{19,3},{4,20},{20... | collective-permute-start | bytes 98312 | tf_op jit(solution)/shard_map/ppermute | solution.py:220
  15.8 35.7 %collective-permute-start.1 = (bf16[16,1024]{1,0:T(8,128)(2,1)}, bf16[16,1024]{1,0:T(8,128)(2,1)S(1)}, u32[]{:S(2)}, u32[]{:S(2)}) collective-permute-start(bf16[16,1024]{1,0:T(8,128)(2,1)} %get-tuple-element.21), channel_id=1, source_target_pairs={{0,2},{2,0},{1,3},{3,1},{4,6},{6,4},{5,7},{7,5},{8,10},{10,8},{9,1... | collective-permute-start | bytes 98312 | tf_op jit(solution)/shard_map/ppermute | solution.py:219
  15.8 35.7 %collective-permute-start.2 = (bf16[16,1024]{1,0:T(8,128)(2,1)}, bf16[16,1024]{1,0:T(8,128)(2,1)S(1)}, u32[]{:S(2)}, u32[]{:S(2)}) collective-permute-start(bf16[16,1024]{1,0:T(8,128)(2,1)} %get-tuple-element.21), channel_id=1, source_target_pairs={{0,18},{2,16},{16,2},{18,0},{1,19},{3,17},{17,3},{19,1},{4,22},{6,... | collective-permute-start | bytes 98312 | tf_op jit(solution)/shard_map/ppermute | solution.py:221
  51.6 5.0 %collective-permute-start.3 = (bf16[2,32,1024]{2,1,0:T(8,128)(2,1)S(1)}, bf16[2,32,1024]{2,1,0:T(8,128)(2,1)S(1)}, u32[]{:S(2)}, u32[]{:S(2)}) collective-permute-start(bf16[2,32,1024]{2,1,0:T(8,128)(2,1)S(1)} %get-tuple-element.55), channel_id=1, source_target_pairs={{0,8},{8,0},{1,9},{9,1},{2,10},{10,2},{3,11},{11,3},{4,12},{12,4},... | collective-permute-start | bytes 393224 | tf_op jit(solution)/shard_map/ppermute | solution.py:223
  51.7 8.7 %collective-permute-start.10 = (bf16[2,64,768]{2,1,0:T(8,128)(2,1)S(1)}, bf16[2,64,768]{2,1,0:T(8,128)(2,1)S(1)}, u32[]{:S(2)}, u32[]{:S(2)}) collective-permute-start(bf16[2,64,768]{2,1,0:T(8,128)(2,1)S(1)} %copy-done.6), channel_id=1, source_target_pairs={{0,1},{1,0},{4,5},{5,4},{2,3},{3,2},{6,7},{7,6},{8,9},{9,8},{12,13... | collective-permute-start | bytes 589832 | tf_op jit(solution)/shard_map/ppermute | solution.py:211
  53.2 11.2 %collective-permute-start.11 = (bf16[2,64,768]{2,1,0:T(8,128)(2,1)S(1)}, bf16[2,64,768]{2,1,0:T(8,128)(2,1)S(1)}, u32[]{:S(2)}, u32[]{:S(2)}) collective-permute-start(bf16[2,64,768]{2,1,0:T(8,128)(2,1)S(1)} %copy-done.5), channel_id=1, source_target_pairs={{0,4},{1,5},{4,0},{5,1},{2,6},{3,7},{6,2},{7,3},{8,12},{9,13},{12,... | collective-permute-start | bytes 589832 | tf_op jit(solution)/shard_map/ppermute | solution.py:211
  55.4 10.3 %collective-permute-start.12 = (bf16[2,64,768]{2,1,0:T(8,128)(2,1)S(1)}, bf16[2,64,768]{2,1,0:T(8,128)(2,1)S(1)}, u32[]{:S(2)}, u32[]{:S(2)}) collective-permute-start(bf16[2,64,768]{2,1,0:T(8,128)(2,1)S(1)} %copy-done.4), channel_id=1, source_target_pairs={{0,5},{1,4},{4,1},{5,0},{2,7},{3,6},{6,3},{7,2},{8,13},{9,12},{12,... | collective-permute-start | bytes 589832 | tf_op jit(solution)/shard_map/ppermute | solution.py:211
  56.7 12.4 %collective-permute-start.4 = (bf16[2,2,32,1024]{3,2,0,1:T(8,128)(2,1)S(1)}, bf16[2,2,32,1024]{3,2,0,1:T(8,128)(2,1)S(1)}, u32[]{:S(2)}, u32[]{:S(2)}) collective-permute-start(bf16[2,2,32,1024]{3,2,0,1:T(8,128)(2,1)S(1)} %get-tuple-element.45), channel_id=1, source_target_pairs={{0,1},{1,0},{4,5},{5,4},{2,3},{3,2},{6,7},{7,6},{8,9},{9,8},{12,13... | collective-permute-start | bytes 786440 | tf_op jit(solution)/shard_map/ppermute | solution.py:227
  58.2 16.0 %collective-permute-start.5 = (bf16[2,2,32,1024]{3,2,0,1:T(8,128)(2,1)S(1)}, bf16[2,2,32,1024]{3,2,0,1:T(8,128)(2,1)S(1)}, u32[]{:S(2)}, u32[]{:S(2)}) collective-permute-start(bf16[2,2,32,1024]{3,2,0,1:T(8,128)(2,1)S(1)} %get-tuple-element.45), channel_id=1, source_target_pairs={{0,4},{1,5},{4,0},{5,1},{2,6},{3,7},{6,2},{7,3},{8,12},{9,13},{12,... | collective-permute-start | bytes 786440 | tf_op jit(solution)/shard_map/ppermute | solution.py:227
  60.3 14.9 %collective-permute-start.6 = (bf16[2,2,32,1024]{3,2,0,1:T(8,128)(2,1)S(1)}, bf16[2,2,32,1024]{3,2,0,1:T(8,128)(2,1)S(1)}, u32[]{:S(2)}, u32[]{:S(2)}) collective-permute-start(bf16[2,2,32,1024]{3,2,0,1:T(8,128)(2,1)S(1)} %get-tuple-element.45), channel_id=1, source_target_pairs={{0,5},{1,4},{4,1},{5,0},{2,7},{3,6},{6,3},{7,2},{8,13},{9,12},{12,... | collective-permute-start | bytes 786440 | tf_op jit(solution)/shard_map/ppermute | solution.py:227
  66.6 12.0 %collective-permute-start.13 = (bf16[4,64,768]{2,1,0:T(8,128)(2,1)}, bf16[4,64,768]{2,1,0:T(8,128)(2,1)S(1)}, u32[]{:S(2)}, u32[]{:S(2)}) collective-permute-start(bf16[4,64,768]{2,1,0:T(8,128)(2,1)} %get-tuple-element.33), channel_id=1, source_target_pairs={{0,8},{8,0},{1,9},{9,1},{2,10},{10,2},{3,11},{11,3},{4,12},{12,4},... | collective-permute-start | bytes 1179656 | tf_op jit(solution)/shard_map/ppermute | solution.py:215
  78.0 1.8 %collective-permute-start.7 = (bf16[256,768]{1,0:T(8,128)(2,1)S(1)}, bf16[256,768]{1,0:T(8,128)(2,1)S(1)}, u32[]{:S(2)}, u32[]{:S(2)}) collective-permute-start(bf16[256,768]{1,0:T(8,128)(2,1)S(1)} %convolution_convert_fusion.1), channel_id=1, source_target_pairs={{0,2},{2,0},{1,3},{3,1},{4,6},{6,4},{5,7},{7,5},{8,10},{10,8},{9,1... | collective-permute-start | bytes 1179656 | tf_op jit(solution)/shard_map/ppermute | solution.py:233
  78.1 5.5 %collective-permute-start.14 = (bf16[4,64,768]{2,1,0:T(8,128)(2,1)S(1)}, bf16[4,64,768]{2,1,0:T(8,128)(2,1)S(1)}, u32[]{:S(2)}, u32[]{:S(2)}) collective-permute-start(bf16[4,64,768]{2,1,0:T(8,128)(2,1)S(1)} %get-tuple-element.32.refs_0_), channel_id=1, source_target_pairs={{0,2},{2,0},{1,3},{3,1},{4,6},{6,4},{5,7},{7,5},{8,10},{10,8},{9,1... | collective-permute-start | bytes 1179656 | tf_op jit(solution)/shard_map/ppermute | solution.py:216
  78.6 5.0 %collective-permute-start.15 = (bf16[4,64,768]{2,1,0:T(8,128)(2,1)S(1)}, bf16[4,64,768]{2,1,0:T(8,128)(2,1)S(1)}, u32[]{:S(2)}, u32[]{:S(2)}) collective-permute-start(bf16[4,64,768]{2,1,0:T(8,128)(2,1)S(1)} %collective-permute-done.13.refs_1_), channel_id=1, source_target_pairs={{0,2},{2,0},{1,3},{3,1},{4,6},{6,4},{5,7},{7,5},{8,10},{10,8},{9,1... | collective-permute-start | bytes 1179656 | tf_op jit(solution)/shard_map/ppermute | solution.py:216
  79.3 1.7 %copy-start.1 = (s32[16,8]{0,1:T(8,128)S(1)}, s32[16,8]{0,1:T(8,128)}, u32[]{:S(2)}) copy-start(s32[16,8]{0,1:T(8,128)} %param.10) | copy-start | bytes 1540
  79.4 1.7 %copy-start.3 = (s32[16]{0:T(128)S(1)}, s32[16]{0:T(128)}, u32[]{:S(2)}) copy-start(s32[16]{0:T(128)} %param.9) | copy-start | bytes 196
  79.4 2.2 %copy-start.2 = (f32[16,8]{0,1:T(8,128)S(1)}, f32[16,8]{0,1:T(8,128)}, u32[]{:S(2)}) copy-start(f32[16,8]{0,1:T(8,128)} %param.11) | copy-start | bytes 1540
  80.0 12.3 %collective-permute-start.8 = (bf16[256,384]{1,0:T(8,128)(2,1)S(1)}, bf16[256,384]{1,0:T(8,128)(2,1)S(1)}, u32[]{:S(2)}, u32[]{:S(2)}) collective-permute-start(bf16[256,384]{1,0:T(8,128)(2,1)S(1)} %fusion), channel_id=1, source_target_pairs={{0,16},{16,0},{1,17},{17,1},{2,18},{18,2},{3,19},{19,3},{4,20},{20... | collective-permute-start | bytes 589832 | tf_op jit(solution)/shard_map/ppermute | solution.py:238
  81.7 10.6 %collective-permute-start.9 = (f32[8,16]{1,0:T(8,128)S(1)}, f32[8,16]{1,0:T(8,128)S(1)}, u32[]{:S(2)}, u32[]{:S(2)}) collective-permute-start(f32[8,16]{1,0:T(8,128)S(1)} %bitcast.59), channel_id=1, source_target_pairs={{0,16},{16,0},{1,17},{17,1},{2,18},{18,2},{3,19},{19,3},{4,20},{20... | collective-permute-start | bytes 1544 | tf_op jit(solution)/shard_map/ppermute | solution.py:241
  93.0 6.2 %collective-permute-start.16 = (bf16[32,1024]{1,0:T(8,128)(2,1)S(1)}, bf16[32,1024]{1,0:T(8,128)(2,1)S(1)}, u32[]{:S(2)}, u32[]{:S(2)}) collective-permute-start(bf16[32,1024]{1,0:T(8,128)(2,1)S(1)} %get-tuple-element.37), channel_id=1, source_target_pairs={{0,1},{1,0},{4,5},{5,4},{8,9},{9,8},{12,13},{13,12},{2,3},{3,2},{6... | collective-permute-start | bytes 196616 | tf_op jit(solution)/shard_map/ppermute | solution.py:251
  94.2 5.7 %collective-permute-start.17 = (bf16[32,1024]{1,0:T(8,128)(2,1)S(1)}, bf16[32,1024]{1,0:T(8,128)(2,1)S(1)}, u32[]{:S(2)}, u32[]{:S(2)}) collective-permute-start(bf16[32,1024]{1,0:T(8,128)(2,1)S(1)} %get-tuple-element.43), channel_id=1, source_target_pairs={{0,4},{1,5},{4,0},{5,1},{8,12},{9,13},{12,8},{13,9},{2,6},{3,7},{6... | collective-permute-start | bytes 196616 | tf_op jit(solution)/shard_map/ppermute | solution.py:251
  95.4 7.1 %collective-permute-start.18 = (bf16[32,1024]{1,0:T(8,128)(2,1)S(1)}, bf16[32,1024]{1,0:T(8,128)(2,1)S(1)}, u32[]{:S(2)}, u32[]{:S(2)}) collective-permute-start(bf16[32,1024]{1,0:T(8,128)(2,1)S(1)} %get-tuple-element.42), channel_id=1, source_target_pairs={{0,5},{1,4},{4,1},{5,0},{8,13},{9,12},{12,9},{13,8},{2,7},{3,6},{6... | collective-permute-start | bytes 196616 | tf_op jit(solution)/shard_map/ppermute | solution.py:251
  96.6 6.0 %collective-permute-start.19 = (bf16[32,1024]{1,0:T(8,128)(2,1)S(1)}, bf16[32,1024]{1,0:T(8,128)(2,1)S(1)}, u32[]{:S(2)}, u32[]{:S(2)}) collective-permute-start(bf16[32,1024]{1,0:T(8,128)(2,1)S(1)} %get-tuple-element.41), channel_id=1, source_target_pairs={{0,8},{1,9},{4,12},{5,13},{8,0},{9,1},{12,4},{13,5},{2,10},{3,11},... | collective-permute-start | bytes 196616 | tf_op jit(solution)/shard_map/ppermute | solution.py:251
  96.6 6.7 %collective-permute-start.20 = (bf16[32,1024]{1,0:T(8,128)(2,1)S(1)}, bf16[32,1024]{1,0:T(8,128)(2,1)S(1)}, u32[]{:S(2)}, u32[]{:S(2)}) collective-permute-start(bf16[32,1024]{1,0:T(8,128)(2,1)S(1)} %get-tuple-element.40), channel_id=1, source_target_pairs={{0,9},{1,8},{4,13},{5,12},{8,1},{9,0},{12,5},{13,4},{2,11},{3,10},... | collective-permute-start | bytes 196616 | tf_op jit(solution)/shard_map/ppermute | solution.py:251
  99.2 5.2 %collective-permute-start.21 = (bf16[32,1024]{1,0:T(8,128)(2,1)S(1)}, bf16[32,1024]{1,0:T(8,128)(2,1)S(1)}, u32[]{:S(2)}, u32[]{:S(2)}) collective-permute-start(bf16[32,1024]{1,0:T(8,128)(2,1)S(1)} %get-tuple-element.39), channel_id=1, source_target_pairs={{0,12},{1,13},{4,8},{5,9},{8,4},{9,5},{12,0},{13,1},{2,14},{3,15},... | collective-permute-start | bytes 196616 | tf_op jit(solution)/shard_map/ppermute | solution.py:251
  99.9 6.1 %collective-permute-start.22 = (bf16[32,1024]{1,0:T(8,128)(2,1)S(1)}, bf16[32,1024]{1,0:T(8,128)(2,1)S(1)}, u32[]{:S(2)}, u32[]{:S(2)}) collective-permute-start(bf16[32,1024]{1,0:T(8,128)(2,1)S(1)} %get-tuple-element.38), channel_id=1, source_target_pairs={{0,13},{1,12},{4,9},{5,8},{8,5},{9,4},{12,1},{13,0},{2,15},{3,14},... | collective-permute-start | bytes 196616 | tf_op jit(solution)/shard_map/ppermute | solution.py:251
  106.2 4.9 %collective-permute-start.23 = (bf16[16,1024]{1,0:T(8,128)(2,1)S(1)}, bf16[16,1024]{1,0:T(8,128)(2,1)S(1)}, u32[]{:S(2)}, u32[]{:S(2)}) collective-permute-start(bf16[16,1024]{1,0:T(8,128)(2,1)S(1)} %get-tuple-element.56), channel_id=1, source_target_pairs={{0,16},{16,0},{1,17},{17,1},{2,18},{18,2},{3,19},{19,3},{4,20},{20... | collective-permute-start | bytes 98312 | tf_op jit(solution)/shard_map/ppermute | solution.py:256

commit v9 on v8

--- a/solution.py
+++ b/solution.py
@@ -26,26 +26,6 @@
     numbers = jnp.arange(experts, dtype=jnp.int32) ^ chip
     weights = combine_weights[:, :, None]
     return jnp.sum(jnp.where(chosen[:, :, None] == numbers[None, None, :], weights, 0.0), axis=1)
-
-
-def assemble_kernel(half, mine, other, out):
-    columns = mine.shape[1]
-    own = pl.multiple_of(half[0] * columns, columns)
-    out[:, pl.ds(own, columns)] = mine[...]
-    out[:, pl.ds(columns - own, columns)] = other[...]
-
-
-def assemble(half, mine, other):
-    rows, columns = mine.shape
-    vmem = pl.BlockSpec(memory_space=pltpu.VMEM)
-    return pl.pallas_call(
-        assemble_kernel,
-        name="assemble",
-        in_specs=[pl.BlockSpec(memory_space=pltpu.SMEM), vmem, vmem],
-        out_specs=vmem,
-        out_shape=jax.ShapeDtypeStruct((rows, 2 * columns), mine.dtype),
-        compiler_params=pltpu.CompilerParams(vmem_limit_bytes=2**20),
-    )(half.reshape(1), mine, other)
 
 
 def exchange(value, axes):
@@ -253,7 +233,7 @@
     mixed = sum(terms).astype(jnp.bfloat16)
     low, high = mixed[:token_count], mixed[token_count:]
     mine, sent = jnp.where(h == 0, low, high), jnp.where(h == 0, high, low)
-    return assemble(h, mine, lax.ppermute(sent, "h", SWAP))
+    return in_order(h, mine, lax.ppermute(sent, "h", SWAP), 1)
 
 
 def per_device(tokens, norm_gain, expert_weights, slot_expert, pair_slots, combine_weights):

time: 112 us -> 113 us (level)
  waiting for transfers between devices: 58.2 us -> 60.7 us
  starting transfers between devices: 38.8 us -> 37.6 us
    ppermute x3, waiting for transfers between devices: 3.1 us -> 9 us  [dense_layer(): blocks[step] = lax.ppermute(blocks[step], ('y', 'x'), pairs)]
    ppermute x3, waiting for transfers between devices: 6.73 us -> 1.5 us  [dense_layer(): rows.append(lax.ppermute(column, ('y', 'x'), pairs))]
    ppermute x3, starting transfers between devices: 5.9 us -> 4.31 us  [dense_layer(): rows.append(lax.ppermute(column, ('y', 'x'), pairs))]
    ppermute x1, starting transfers between devices: 1.04 us -> 2.35 us  [dense_layer(): far = lax.ppermute(hidden, 'h', SWAP)]
    ppermute x1, starting transfers between devices: 1.96 us -> 0.66 us  [dense_layer(): far_weights = lax.ppermute(coefficient, 'h', SWAP)]
  transfers between devices with their start and end apart: 25 -> 25, of which waited for: 13 -> 9; matrix products, arithmetic and copies ran while one was open for 5% -> 5% of each run, Pallas kernels for 4% -> 4%
where the time goes in v9:
time: 113 us
  waiting for transfers between devices  60.7 us (54%)
  starting transfers between devices  37.6 us (33%)
  Pallas kernels  6.71 us (6%)
  other arithmetic  3.61 us (3%)
  matrix products  2.79 us (2%)
  local copies, waits for them, and re-layouts  1.27 us (1%)
    ppermute x1, waiting for transfers between devices, dense_layer(): from_h = lax.ppermute(keep, 'h', SWAP)  34.7 us
    ppermute x7, starting transfers between devices, dense_layer(): returned.append(lax.ppermute(result[step], chip_axes, pairs))  9.42 us
    ppermute x3, waiting for transfers between devices, dense_layer(): blocks[step] = lax.ppermute(blocks[step], ('y', 'x'), pairs)  9 us
    all_to_all x1, starting transfers between devices, exchange(): return lax.all_to_all(value, axes, 0, 0, tiled=True)  8.48 us
    ppermute x1, waiting for transfers between devices, dense_layer(): far_weights = lax.ppermute(coefficient, 'h', SWAP)  6.64 us
    ppermute x3, starting transfers between devices, dense_layer(): rows.append(lax.ppermute(column, ('y', 'x'), pairs))  4.31 us
    ppermute x7, waiting for transfers between devices, dense_layer(): returned.append(lax.ppermute(result[step], chip_axes, pairs))  4.17 us
    ppermute x3, starting transfers between devices, dense_layer(): blocks[step] = lax.ppermute(blocks[step], ('y', 'x'), pairs)  4.13 us
  transfers between devices with their start and end apart: 25, of which 9 were waited for; matrix products, arithmetic and copies ran while one was open for 5% of the time, Pallas kernels for 4%

profile of v9, /device:TPU:0, one launch (start us, length us, event | category | flops | bytes accessed | tf_op | source)
XLA Modules:
  0.0 113.0 jit_solution(3995842918485247509)
XLA Ops:
  0.0 2.7 %pack.1 = (bf16[2,8,64,768]{3,2,1,0:T(8,128)(2,1)}, bf16[2,64,768]{2,1,0:T(8,128)(2,1)}, bf16[2,64,768]{2,1,0:T(8,128)(2,1)}, bf16[2,64,768]{2,1,0:T(8,128)(2,1)}, bf16[2,64,768]{2,1,0:T(8,128)(2,1)}) custom-call(s32[1]{0:T(128)} %bitcast.13.plane, bf16[8,64,2304]{2,1,0:T(8,128)(2,1)} %weights.1), custom_call_target="tpu_custom_call" | custom-call | tf_op jit(solution)/shard_map/pack/pallas_call | solution.py:127
  2.8 8.5 %all-to-all-start = ((bf16[16,64,768]{2,1,0:T(8,128)(2,1)}), bf16[16,64,768]{2,1,0:T(8,128)(2,1)S(1)}, u32[]{:S(2)}, u32[]{:S(2)}) async-start(bf16[16,64,768]{2,1,0:T(8,128)(2,1)} %bitcast.48), calls=%async_computation | async-start | bytes 3145728 | tf_op jit(solution)/shard_map/all_to_all | solution.py:32
  11.3 1.6 %normalize.1 = (bf16[16,1024]{1,0:T(8,128)(2,1)}, bf16[16,1024]{1,0:T(8,128)(2,1)}) custom-call(s32[1]{0:T(128)} %bitcast.core, bf16[16,2048]{1,0:T(8,128)(2,1)} %all_tokens.1, f32[1,2048]{1,0:T(1,128)} %bitcast.60), custom_call_target="tpu_custom_call" | custom-call | tf_op jit(solution)/shard_map/normalize/pallas_call | solution.py:105
  12.9 2.9 %collective-permute-start = (bf16[16,1024]{1,0:T(8,128)(2,1)}, bf16[16,1024]{1,0:T(8,128)(2,1)S(1)}, u32[]{:S(2)}, u32[]{:S(2)}) collective-permute-start(bf16[16,1024]{1,0:T(8,128)(2,1)} %get-tuple-element.20), channel_id=1, source_target_pairs={{0,16},{16,0},{1,17},{17,1},{2,18},{18,2},{3,19},{19,3},{4,20},{20... | collective-permute-start | bytes 98312 | tf_op jit(solution)/shard_map/ppermute | solution.py:200
  16.0 34.7 %collective-permute-done = bf16[16,1024]{1,0:T(8,128)(2,1)S(1)} collective-permute-done((bf16[16,1024]{1,0:T(8,128)(2,1)}, bf16[16,1024]{1,0:T(8,128)(2,1)S(1)}, u32[]{:S(2)}, u32[]{:S(2)}) %collective-permute-start) | collective-permute-done | bytes 32800 | tf_op jit(solution)/shard_map/ppermute | solution.py:200
  50.7 0.8 maximum_select_fusion.1
  51.7 1.5 %collective-permute-start.10 = (bf16[2,64,768]{2,1,0:T(8,128)(2,1)S(1)}, bf16[2,64,768]{2,1,0:T(8,128)(2,1)S(1)}, u32[]{:S(2)}, u32[]{:S(2)}) collective-permute-start(bf16[2,64,768]{2,1,0:T(8,128)(2,1)S(1)} %copy-done.6), channel_id=1, source_target_pairs={{0,1},{1,0},{4,5},{5,4},{2,3},{3,2},{6,7},{7,6},{8,9},{9,8},{12,13... | collective-permute-start | bytes 589832 | tf_op jit(solution)/shard_map/ppermute | solution.py:191
  53.2 2.2 %collective-permute-start.11 = (bf16[2,64,768]{2,1,0:T(8,128)(2,1)S(1)}, bf16[2,64,768]{2,1,0:T(8,128)(2,1)S(1)}, u32[]{:S(2)}, u32[]{:S(2)}) collective-permute-start(bf16[2,64,768]{2,1,0:T(8,128)(2,1)S(1)} %copy-done.5), channel_id=1, source_target_pairs={{0,4},{1,5},{4,0},{5,1},{2,6},{3,7},{6,2},{7,3},{8,12},{9,13},{12,... | collective-permute-start | bytes 589832 | tf_op jit(solution)/shard_map/ppermute | solution.py:191
  55.8 0.8 collective-permute-done.3
  56.7 2.6 %collective-permute-start.5 = (bf16[2,2,32,1024]{3,2,0,1:T(8,128)(2,1)S(1)}, bf16[2,2,32,1024]{3,2,0,1:T(8,128)(2,1)S(1)}, u32[]{:S(2)}, u32[]{:S(2)}) collective-permute-start(bf16[2,2,32,1024]{3,2,0,1:T(8,128)(2,1)S(1)} %get-tuple-element.45), channel_id=1, source_target_pairs={{0,4},{1,5},{4,0},{5,1},{2,6},{3,7},{6,2},{7,3},{8,12},{9,13},{12,... | collective-permute-start | bytes 786440 | tf_op jit(solution)/shard_map/ppermute | solution.py:207
  59.9 1.1 collective-permute-start.4
  61.0 9.0 %collective-permute-done.11 = bf16[2,64,768]{2,1,0:T(8,128)(2,1)S(1)} collective-permute-done((bf16[2,64,768]{2,1,0:T(8,128)(2,1)S(1)}, bf16[2,64,768]{2,1,0:T(8,128)(2,1)S(1)}, u32[]{:S(2)}, u32[]{:S(2)}) %collective-permute-start.11) | collective-permute-done | bytes 196640 | tf_op jit(solution)/shard_map/ppermute | solution.py:191
  70.0 0.9 pad_maximum_fusion.1
  70.9 2.5 %collective-permute-start.13 = (bf16[4,64,768]{2,1,0:T(8,128)(2,1)}, bf16[4,64,768]{2,1,0:T(8,128)(2,1)S(1)}, u32[]{:S(2)}, u32[]{:S(2)}) collective-permute-start(bf16[4,64,768]{2,1,0:T(8,128)(2,1)} %get-tuple-element.33), channel_id=1, source_target_pairs={{0,8},{8,0},{1,9},{9,1},{2,10},{10,2},{3,11},{11,3},{4,12},{12,4},... | collective-permute-start | bytes 1179656 | tf_op jit(solution)/shard_map/ppermute | solution.py:195
  73.4 1.5 %collective-permute-done.5 = bf16[2,2,32,1024]{3,2,0,1:T(8,128)(2,1)S(1)} collective-permute-done((bf16[2,2,32,1024]{3,2,0,1:T(8,128)(2,1)S(1)}, bf16[2,2,32,1024]{3,2,0,1:T(8,128)(2,1)S(1)}, u32[]{:S(2)}, u32[]{:S(2)}) %collective-permute-start.5) | collective-permute-done | bytes 262176 | tf_op jit(solution)/shard_map/ppermute | solution.py:207
  75.1 0.9 copy.14
  76.0 1.6 %convolution_convert_fusion.1 = bf16[256,768]{1,0:T(8,128)(2,1)S(1)} fusion(bf16[256,1024]{1,0:T(8,128)(2,1)} %bitcast.49, bf16[1024,768]{1,0:T(8,128)(2,1)S(1)} %bitcast.45), kind=kOutput, calls=%fused_computation.1 | convolution fusion | flops 402849792 | bytes 2490368 | tf_op jit(solution)/shard_map/dot_general | solution.py:212
  78.2 1.1 collective-permute-done.13.refs_1_
  80.2 2.3 %collective-permute-start.8 = (bf16[256,384]{1,0:T(8,128)(2,1)S(1)}, bf16[256,384]{1,0:T(8,128)(2,1)S(1)}, u32[]{:S(2)}, u32[]{:S(2)}) collective-permute-start(bf16[256,384]{1,0:T(8,128)(2,1)S(1)} %fusion), channel_id=1, source_target_pairs={{0,16},{16,0},{1,17},{17,1},{2,18},{18,2},{3,19},{19,3},{4,20},{20... | collective-permute-start | bytes 589832 | tf_op jit(solution)/shard_map/ppermute | solution.py:218
  83.2 0.7 collective-permute-start.9
  83.8 2.4 %gather_blocks.1 = bf16[2,2,2,2,64,768]{5,4,3,2,1,0:T(8,128)(2,1)S(1)} custom-call(s32[1]{0:T(128)} %bitcast.18.level, s32[1]{0:T(128)} %bitcast.13.plane, s32[1]{0:T(128)} %bitcast.core, bf16[4,64,768]{2,1,0:T(8,128)(2,1)S(1)} %get-tuple-element.32.refs_0_, bf16[4,64,768]{2,1,0:T(8,128)(2,1)S(1)} %collective-permute-done.13.refs_1_, ...), custom_call_target="tpu_custom_call" | custom-call | tf_op jit(solution)/shard_map/gather_blocks/pallas_call | solution.py:159
  86.2 6.6 %collective-permute-done.9 = f32[8,16]{1,0:T(8,128)S(1)} collective-permute-done((f32[8,16]{1,0:T(8,128)S(1)}, f32[8,16]{1,0:T(8,128)S(1)}, u32[]{:S(2)}, u32[]{:S(2)}) %collective-permute-start.9) | collective-permute-done | bytes 544 | tf_op jit(solution)/shard_map/ppermute | solution.py:221
  93.6 0.9 collective-permute-start.16
  94.5 2.3 %collective-permute-start.17 = (bf16[32,1024]{1,0:T(8,128)(2,1)S(1)}, bf16[32,1024]{1,0:T(8,128)(2,1)S(1)}, u32[]{:S(2)}, u32[]{:S(2)}) collective-permute-start(bf16[32,1024]{1,0:T(8,128)(2,1)S(1)} %get-tuple-element.43), channel_id=1, source_target_pairs={{0,4},{1,5},{4,0},{5,1},{8,12},{9,13},{12,8},{13,9},{2,6},{3,7},{6... | collective-permute-start | bytes 196616 | tf_op jit(solution)/shard_map/ppermute | solution.py:231
  97.2 2.5 %collective-permute-start.20 = (bf16[32,1024]{1,0:T(8,128)(2,1)S(1)}, bf16[32,1024]{1,0:T(8,128)(2,1)S(1)}, u32[]{:S(2)}, u32[]{:S(2)}) collective-permute-start(bf16[32,1024]{1,0:T(8,128)(2,1)S(1)} %get-tuple-element.40), channel_id=1, source_target_pairs={{0,9},{1,8},{4,13},{5,12},{8,1},{9,0},{12,5},{13,4},{2,11},{3,10},... | collective-permute-start | bytes 196616 | tf_op jit(solution)/shard_map/ppermute | solution.py:231
  99.8 1.5 %collective-permute-start.21 = (bf16[32,1024]{1,0:T(8,128)(2,1)S(1)}, bf16[32,1024]{1,0:T(8,128)(2,1)S(1)}, u32[]{:S(2)}, u32[]{:S(2)}) collective-permute-start(bf16[32,1024]{1,0:T(8,128)(2,1)S(1)} %get-tuple-element.39), channel_id=1, source_target_pairs={{0,12},{1,13},{4,8},{5,9},{8,4},{9,5},{12,0},{13,1},{2,14},{3,15},... | collective-permute-start | bytes 196616 | tf_op jit(solution)/shard_map/ppermute | solution.py:231
  101.2 1.9 %collective-permute-start.22 = (bf16[32,1024]{1,0:T(8,128)(2,1)S(1)}, bf16[32,1024]{1,0:T(8,128)(2,1)S(1)}, u32[]{:S(2)}, u32[]{:S(2)}) collective-permute-start(bf16[32,1024]{1,0:T(8,128)(2,1)S(1)} %get-tuple-element.38), channel_id=1, source_target_pairs={{0,13},{1,12},{4,9},{5,8},{8,5},{9,4},{12,1},{13,0},{2,15},{3,14},... | collective-permute-start | bytes 196616 | tf_op jit(solution)/shard_map/ppermute | solution.py:231
  103.2 2.4 %collective-permute-done.21 = bf16[32,1024]{1,0:T(8,128)(2,1)S(1)} collective-permute-done((bf16[32,1024]{1,0:T(8,128)(2,1)S(1)}, bf16[32,1024]{1,0:T(8,128)(2,1)S(1)}, u32[]{:S(2)}, u32[]{:S(2)}) %collective-permute-start.21) | collective-permute-done | bytes 65568 | tf_op jit(solution)/shard_map/ppermute | solution.py:231
  105.6 1.7 %collective-permute-done.22 = bf16[32,1024]{1,0:T(8,128)(2,1)S(1)} collective-permute-done((bf16[32,1024]{1,0:T(8,128)(2,1)S(1)}, bf16[32,1024]{1,0:T(8,128)(2,1)S(1)}, u32[]{:S(2)}, u32[]{:S(2)}) %collective-permute-start.22) | collective-permute-done | bytes 65568 | tf_op jit(solution)/shard_map/ppermute | solution.py:231
  107.5 2.0 %collective-permute-start.23 = (bf16[16,1024]{1,0:T(8,128)(2,1)S(1)}, bf16[16,1024]{1,0:T(8,128)(2,1)S(1)}, u32[]{:S(2)}, u32[]{:S(2)}) collective-permute-start(bf16[16,1024]{1,0:T(8,128)(2,1)S(1)} %get-tuple-element.57), channel_id=1, source_target_pairs={{0,16},{16,0},{1,17},{17,1},{2,18},{18,2},{3,19},{19,3},{4,20},{20... | collective-permute-start | bytes 98312 | tf_op jit(solution)/shard_map/ppermute | solution.py:236
  109.5 2.8 %collective-permute-done.23 = bf16[16,1024]{1,0:T(8,128)(2,1)S(1)} collective-permute-done((bf16[16,1024]{1,0:T(8,128)(2,1)S(1)}, bf16[16,1024]{1,0:T(8,128)(2,1)S(1)}, u32[]{:S(2)}, u32[]{:S(2)}) %collective-permute-start.23) | collective-permute-done | bytes 32800 | tf_op jit(solution)/shard_map/ppermute | solution.py:236
  112.4 0.6 maximum_select_fusion.3
  (65 shorter events, 5.2 us)
Async XLA Ops:
  2.7 48.9 %copy-start.6 = (bf16[2,64,768]{2,1,0:T(8,128)(2,1)S(1)}, bf16[2,64,768]{2,1,0:T(8,128)(2,1)}, u32[]{:S(2)}) copy-start(bf16[2,64,768]{2,1,0:T(8,128)(2,1)} %get-tuple-element.29) | copy-start | bytes 589828
  2.8 50.5 %copy-start.5 = (bf16[2,64,768]{2,1,0:T(8,128)(2,1)S(1)}, bf16[2,64,768]{2,1,0:T(8,128)(2,1)}, u32[]{:S(2)}) copy-start(bf16[2,64,768]{2,1,0:T(8,128)(2,1)} %get-tuple-element.30) | copy-start | bytes 589828
  2.8 52.6 %copy-start.4 = (bf16[2,64,768]{2,1,0:T(8,128)(2,1)S(1)}, bf16[2,64,768]{2,1,0:T(8,128)(2,1)}, u32[]{:S(2)}) copy-start(bf16[2,64,768]{2,1,0:T(8,128)(2,1)} %get-tuple-element.31) | copy-start | bytes 589828
  2.8 53.0 %copy-start = (bf16[2,64,768]{2,1,0:T(8,128)(2,1)S(1)}, bf16[2,64,768]{2,1,0:T(8,128)(2,1)}, u32[]{:S(2)}) copy-start(bf16[2,64,768]{2,1,0:T(8,128)(2,1)} %get-tuple-element.28) | copy-start | bytes 589828
  2.8 73.2 %all-to-all-start = ((bf16[16,64,768]{2,1,0:T(8,128)(2,1)}), bf16[16,64,768]{2,1,0:T(8,128)(2,1)S(1)}, u32[]{:S(2)}, u32[]{:S(2)}) async-start(bf16[16,64,768]{2,1,0:T(8,128)(2,1)} %bitcast.48), calls=%async_computation | async-start | bytes 3145728 | tf_op jit(solution)/shard_map/all_to_all | solution.py:32
  12.9 37.8 %collective-permute-start = (bf16[16,1024]{1,0:T(8,128)(2,1)}, bf16[16,1024]{1,0:T(8,128)(2,1)S(1)}, u32[]{:S(2)}, u32[]{:S(2)}) collective-permute-start(bf16[16,1024]{1,0:T(8,128)(2,1)} %get-tuple-element.20), channel_id=1, source_target_pairs={{0,16},{16,0},{1,17},{17,1},{2,18},{18,2},{3,19},{19,3},{4,20},{20... | collective-permute-start | bytes 98312 | tf_op jit(solution)/shard_map/ppermute | solution.py:200
  15.8 35.7 %collective-permute-start.1 = (bf16[16,1024]{1,0:T(8,128)(2,1)}, bf16[16,1024]{1,0:T(8,128)(2,1)S(1)}, u32[]{:S(2)}, u32[]{:S(2)}) collective-permute-start(bf16[16,1024]{1,0:T(8,128)(2,1)} %get-tuple-element.21), channel_id=1, source_target_pairs={{0,2},{2,0},{1,3},{3,1},{4,6},{6,4},{5,7},{7,5},{8,10},{10,8},{9,1... | collective-permute-start | bytes 98312 | tf_op jit(solution)/shard_map/ppermute | solution.py:199
  15.8 35.7 %collective-permute-start.2 = (bf16[16,1024]{1,0:T(8,128)(2,1)}, bf16[16,1024]{1,0:T(8,128)(2,1)S(1)}, u32[]{:S(2)}, u32[]{:S(2)}) collective-permute-start(bf16[16,1024]{1,0:T(8,128)(2,1)} %get-tuple-element.21), channel_id=1, source_target_pairs={{0,18},{2,16},{16,2},{18,0},{1,19},{3,17},{17,3},{19,1},{4,22},{6,... | collective-permute-start | bytes 98312 | tf_op jit(solution)/shard_map/ppermute | solution.py:201
  51.6 5.0 %collective-permute-start.3 = (bf16[2,32,1024]{2,1,0:T(8,128)(2,1)S(1)}, bf16[2,32,1024]{2,1,0:T(8,128)(2,1)S(1)}, u32[]{:S(2)}, u32[]{:S(2)}) collective-permute-start(bf16[2,32,1024]{2,1,0:T(8,128)(2,1)S(1)} %get-tuple-element.55), channel_id=1, source_target_pairs={{0,8},{8,0},{1,9},{9,1},{2,10},{10,2},{3,11},{11,3},{4,12},{12,4},... | collective-permute-start | bytes 393224 | tf_op jit(solution)/shard_map/ppermute | solution.py:203
  51.7 8.2 %collective-permute-start.10 = (bf16[2,64,768]{2,1,0:T(8,128)(2,1)S(1)}, bf16[2,64,768]{2,1,0:T(8,128)(2,1)S(1)}, u32[]{:S(2)}, u32[]{:S(2)}) collective-permute-start(bf16[2,64,768]{2,1,0:T(8,128)(2,1)S(1)} %copy-done.6), channel_id=1, source_target_pairs={{0,1},{1,0},{4,5},{5,4},{2,3},{3,2},{6,7},{7,6},{8,9},{9,8},{12,13... | collective-permute-start | bytes 589832 | tf_op jit(solution)/shard_map/ppermute | solution.py:191
  53.2 16.8 %collective-permute-start.11 = (bf16[2,64,768]{2,1,0:T(8,128)(2,1)S(1)}, bf16[2,64,768]{2,1,0:T(8,128)(2,1)S(1)}, u32[]{:S(2)}, u32[]{:S(2)}) collective-permute-start(bf16[2,64,768]{2,1,0:T(8,128)(2,1)S(1)} %copy-done.5), channel_id=1, source_target_pairs={{0,4},{1,5},{4,0},{5,1},{2,6},{3,7},{6,2},{7,3},{8,12},{9,13},{12,... | collective-permute-start | bytes 589832 | tf_op jit(solution)/shard_map/ppermute | solution.py:191
  55.4 14.6 %collective-permute-start.12 = (bf16[2,64,768]{2,1,0:T(8,128)(2,1)S(1)}, bf16[2,64,768]{2,1,0:T(8,128)(2,1)S(1)}, u32[]{:S(2)}, u32[]{:S(2)}) collective-permute-start(bf16[2,64,768]{2,1,0:T(8,128)(2,1)S(1)} %copy-done.4), channel_id=1, source_target_pairs={{0,5},{1,4},{4,1},{5,0},{2,7},{3,6},{6,3},{7,2},{8,13},{9,12},{12,... | collective-permute-start | bytes 589832 | tf_op jit(solution)/shard_map/ppermute | solution.py:191
  56.7 18.2 %collective-permute-start.5 = (bf16[2,2,32,1024]{3,2,0,1:T(8,128)(2,1)S(1)}, bf16[2,2,32,1024]{3,2,0,1:T(8,128)(2,1)S(1)}, u32[]{:S(2)}, u32[]{:S(2)}) collective-permute-start(bf16[2,2,32,1024]{3,2,0,1:T(8,128)(2,1)S(1)} %get-tuple-element.45), channel_id=1, source_target_pairs={{0,4},{1,5},{4,0},{5,1},{2,6},{3,7},{6,2},{7,3},{8,12},{9,13},{12,... | collective-permute-start | bytes 786440 | tf_op jit(solution)/shard_map/ppermute | solution.py:207
  59.3 15.6 %collective-permute-start.6 = (bf16[2,2,32,1024]{3,2,0,1:T(8,128)(2,1)S(1)}, bf16[2,2,32,1024]{3,2,0,1:T(8,128)(2,1)S(1)}, u32[]{:S(2)}, u32[]{:S(2)}) collective-permute-start(bf16[2,2,32,1024]{3,2,0,1:T(8,128)(2,1)S(1)} %get-tuple-element.45), channel_id=1, source_target_pairs={{0,5},{1,4},{4,1},{5,0},{2,7},{3,6},{6,3},{7,2},{8,13},{9,12},{12,... | collective-permute-start | bytes 786440 | tf_op jit(solution)/shard_map/ppermute | solution.py:207
  59.9 15.0 %collective-permute-start.4 = (bf16[2,2,32,1024]{3,2,0,1:T(8,128)(2,1)S(1)}, bf16[2,2,32,1024]{3,2,0,1:T(8,128)(2,1)S(1)}, u32[]{:S(2)}, u32[]{:S(2)}) collective-permute-start(bf16[2,2,32,1024]{3,2,0,1:T(8,128)(2,1)S(1)} %get-tuple-element.45), channel_id=1, source_target_pairs={{0,1},{1,0},{4,5},{5,4},{2,3},{3,2},{6,7},{7,6},{8,9},{9,8},{12,13... | collective-permute-start | bytes 786440 | tf_op jit(solution)/shard_map/ppermute | solution.py:207
  70.9 8.4 %collective-permute-start.13 = (bf16[4,64,768]{2,1,0:T(8,128)(2,1)}, bf16[4,64,768]{2,1,0:T(8,128)(2,1)S(1)}, u32[]{:S(2)}, u32[]{:S(2)}) collective-permute-start(bf16[4,64,768]{2,1,0:T(8,128)(2,1)} %get-tuple-element.33), channel_id=1, source_target_pairs={{0,8},{8,0},{1,9},{9,1},{2,10},{10,2},{3,11},{11,3},{4,12},{12,4},... | collective-permute-start | bytes 1179656 | tf_op jit(solution)/shard_map/ppermute | solution.py:195
  77.6 2.3 %collective-permute-start.7 = (bf16[256,768]{1,0:T(8,128)(2,1)S(1)}, bf16[256,768]{1,0:T(8,128)(2,1)S(1)}, u32[]{:S(2)}, u32[]{:S(2)}) collective-permute-start(bf16[256,768]{1,0:T(8,128)(2,1)S(1)} %convolution_convert_fusion.1), channel_id=1, source_target_pairs={{0,2},{2,0},{1,3},{3,1},{4,6},{6,4},{5,7},{7,5},{8,10},{10,8},{9,1... | collective-permute-start | bytes 1179656 | tf_op jit(solution)/shard_map/ppermute | solution.py:213
  77.7 6.1 %collective-permute-start.14 = (bf16[4,64,768]{2,1,0:T(8,128)(2,1)S(1)}, bf16[4,64,768]{2,1,0:T(8,128)(2,1)S(1)}, u32[]{:S(2)}, u32[]{:S(2)}) collective-permute-start(bf16[4,64,768]{2,1,0:T(8,128)(2,1)S(1)} %get-tuple-element.32.refs_0_), channel_id=1, source_target_pairs={{0,2},{2,0},{1,3},{3,1},{4,6},{6,4},{5,7},{7,5},{8,10},{10,8},{9,1... | collective-permute-start | bytes 1179656 | tf_op jit(solution)/shard_map/ppermute | solution.py:196
  79.4 4.5 %collective-permute-start.15 = (bf16[4,64,768]{2,1,0:T(8,128)(2,1)S(1)}, bf16[4,64,768]{2,1,0:T(8,128)(2,1)S(1)}, u32[]{:S(2)}, u32[]{:S(2)}) collective-permute-start(bf16[4,64,768]{2,1,0:T(8,128)(2,1)S(1)} %collective-permute-done.13.refs_1_), channel_id=1, source_target_pairs={{0,2},{2,0},{1,3},{3,1},{4,6},{6,4},{5,7},{7,5},{8,10},{10,8},{9,1... | collective-permute-start | bytes 1179656 | tf_op jit(solution)/shard_map/ppermute | solution.py:196
  79.9 2.6 %copy-start.1 = (s32[16,8]{0,1:T(8,128)S(1)}, s32[16,8]{0,1:T(8,128)}, u32[]{:S(2)}) copy-start(s32[16,8]{0,1:T(8,128)} %param.10) | copy-start | bytes 1540
  79.9 2.7 %copy-start.3 = (s32[16]{0:T(128)S(1)}, s32[16]{0:T(128)}, u32[]{:S(2)}) copy-start(s32[16]{0:T(128)} %param.9) | copy-start | bytes 196
  80.0 3.1 %copy-start.2 = (f32[16,8]{0,1:T(8,128)S(1)}, f32[16,8]{0,1:T(8,128)}, u32[]{:S(2)}) copy-start(f32[16,8]{0,1:T(8,128)} %param.11) | copy-start | bytes 1540
  80.2 12.7 %collective-permute-start.8 = (bf16[256,384]{1,0:T(8,128)(2,1)S(1)}, bf16[256,384]{1,0:T(8,128)(2,1)S(1)}, u32[]{:S(2)}, u32[]{:S(2)}) collective-permute-start(bf16[256,384]{1,0:T(8,128)(2,1)S(1)} %fusion), channel_id=1, source_target_pairs={{0,16},{16,0},{1,17},{17,1},{2,18},{18,2},{3,19},{19,3},{4,20},{20... | collective-permute-start | bytes 589832 | tf_op jit(solution)/shard_map/ppermute | solution.py:218
  83.2 9.7 %collective-permute-start.9 = (f32[8,16]{1,0:T(8,128)S(1)}, f32[8,16]{1,0:T(8,128)S(1)}, u32[]{:S(2)}, u32[]{:S(2)}) collective-permute-start(f32[8,16]{1,0:T(8,128)S(1)} %bitcast.58), channel_id=1, source_target_pairs={{0,16},{16,0},{1,17},{17,1},{2,18},{18,2},{3,19},{19,3},{4,20},{20... | collective-permute-start | bytes 1544 | tf_op jit(solution)/shard_map/ppermute | solution.py:221
  93.6 6.2 %collective-permute-start.16 = (bf16[32,1024]{1,0:T(8,128)(2,1)S(1)}, bf16[32,1024]{1,0:T(8,128)(2,1)S(1)}, u32[]{:S(2)}, u32[]{:S(2)}) collective-permute-start(bf16[32,1024]{1,0:T(8,128)(2,1)S(1)} %get-tuple-element.37), channel_id=1, source_target_pairs={{0,1},{1,0},{4,5},{5,4},{8,9},{9,8},{12,13},{13,12},{2,3},{3,2},{6... | collective-permute-start | bytes 196616 | tf_op jit(solution)/shard_map/ppermute | solution.py:231
  94.5 6.8 %collective-permute-start.17 = (bf16[32,1024]{1,0:T(8,128)(2,1)S(1)}, bf16[32,1024]{1,0:T(8,128)(2,1)S(1)}, u32[]{:S(2)}, u32[]{:S(2)}) collective-permute-start(bf16[32,1024]{1,0:T(8,128)(2,1)S(1)} %get-tuple-element.43), channel_id=1, source_target_pairs={{0,4},{1,5},{4,0},{5,1},{8,12},{9,13},{12,8},{13,9},{2,6},{3,7},{6... | collective-permute-start | bytes 196616 | tf_op jit(solution)/shard_map/ppermute | solution.py:231
  96.8 6.4 %collective-permute-start.18 = (bf16[32,1024]{1,0:T(8,128)(2,1)S(1)}, bf16[32,1024]{1,0:T(8,128)(2,1)S(1)}, u32[]{:S(2)}, u32[]{:S(2)}) collective-permute-start(bf16[32,1024]{1,0:T(8,128)(2,1)S(1)} %get-tuple-element.42), channel_id=1, source_target_pairs={{0,5},{1,4},{4,1},{5,0},{8,13},{9,12},{12,9},{13,8},{2,7},{3,6},{6... | collective-permute-start | bytes 196616 | tf_op jit(solution)/shard_map/ppermute | solution.py:231
  97.2 6.0 %collective-permute-start.19 = (bf16[32,1024]{1,0:T(8,128)(2,1)S(1)}, bf16[32,1024]{1,0:T(8,128)(2,1)S(1)}, u32[]{:S(2)}, u32[]{:S(2)}) collective-permute-start(bf16[32,1024]{1,0:T(8,128)(2,1)S(1)} %get-tuple-element.41), channel_id=1, source_target_pairs={{0,8},{1,9},{4,12},{5,13},{8,0},{9,1},{12,4},{13,5},{2,10},{3,11},... | collective-permute-start | bytes 196616 | tf_op jit(solution)/shard_map/ppermute | solution.py:231
  97.2 6.0 %collective-permute-start.20 = (bf16[32,1024]{1,0:T(8,128)(2,1)S(1)}, bf16[32,1024]{1,0:T(8,128)(2,1)S(1)}, u32[]{:S(2)}, u32[]{:S(2)}) collective-permute-start(bf16[32,1024]{1,0:T(8,128)(2,1)S(1)} %get-tuple-element.40), channel_id=1, source_target_pairs={{0,9},{1,8},{4,13},{5,12},{8,1},{9,0},{12,5},{13,4},{2,11},{3,10},... | collective-permute-start | bytes 196616 | tf_op jit(solution)/shard_map/ppermute | solution.py:231
  99.8 5.8 %collective-permute-start.21 = (bf16[32,1024]{1,0:T(8,128)(2,1)S(1)}, bf16[32,1024]{1,0:T(8,128)(2,1)S(1)}, u32[]{:S(2)}, u32[]{:S(2)}) collective-permute-start(bf16[32,1024]{1,0:T(8,128)(2,1)S(1)} %get-tuple-element.39), channel_id=1, source_target_pairs={{0,12},{1,13},{4,8},{5,9},{8,4},{9,5},{12,0},{13,1},{2,14},{3,15},... | collective-permute-start | bytes 196616 | tf_op jit(solution)/shard_map/ppermute | solution.py:231
  101.2 6.1 %collective-permute-start.22 = (bf16[32,1024]{1,0:T(8,128)(2,1)S(1)}, bf16[32,1024]{1,0:T(8,128)(2,1)S(1)}, u32[]{:S(2)}, u32[]{:S(2)}) collective-permute-start(bf16[32,1024]{1,0:T(8,128)(2,1)S(1)} %get-tuple-element.38), channel_id=1, source_target_pairs={{0,13},{1,12},{4,9},{5,8},{8,5},{9,4},{12,1},{13,0},{2,15},{3,14},... | collective-permute-start | bytes 196616 | tf_op jit(solution)/shard_map/ppermute | solution.py:231
  107.5 4.9 %collective-permute-start.23 = (bf16[16,1024]{1,0:T(8,128)(2,1)S(1)}, bf16[16,1024]{1,0:T(8,128)(2,1)S(1)}, u32[]{:S(2)}, u32[]{:S(2)}) collective-permute-start(bf16[16,1024]{1,0:T(8,128)(2,1)S(1)} %get-tuple-element.57), channel_id=1, source_target_pairs={{0,16},{16,0},{1,17},{17,1},{2,18},{18,2},{3,19},{19,3},{4,20},{20... | collective-permute-start | bytes 98312 | tf_op jit(solution)/shard_map/ppermute | solution.py:236
